TPU v7x, 32 devices: a whole 2x2x4 slice. The times are simulated.
32 devices in a mesh: groups: 2 (over x), seq: 16 (over z, y, core).
Axes of the slice: x: 2, y: 2, z: 4, core: 2. Of those that a mesh axis runs over, the one named last changes fastest.
Arguments:
- seqs_in: bfloat16 [4, 4096, 1536], P('groups', 'seq'), parts along dimension 0, may hold values from -6 to 6
- pooled_grad: bfloat16 [4, 1024, 1536], P('groups', 'seq'), parts along dimension 0, may hold values from -6 to 6
- scale_in: float32 [1536], replicated, may hold values from 0.5 to 2
- shift_in: float32 [1536], replicated, may hold values from -3 to 3
- tap_weight_stack: bfloat16 [3, 1536, 768], replicated, may hold values from -0.09375 to 0.09375
- scale_mid: float32 [768], replicated, may hold values from 0.5 to 2
- shift_mid: float32 [768], replicated, may hold values from -3 to 3
- out_weight: bfloat16 [768, 1536], replicated, may hold values from -0.21875 to 0.21875
- out_bias: float32 [1536], replicated, may hold values from -3 to 3
Outputs:
- pooled: bfloat16 [4, 1024, 1536], P('groups', 'seq'), parts along dimension 0
- seq_grad: bfloat16 [4, 4096, 1536], P('groups', 'seq'), parts along dimension 0
There are 2 independent parts, one for each index of `groups`. A program takes and returns all parts, laid end to end along the dimension named above; an argument that names none is the same for every part. Nothing has to cross between parts.
All inputs are finite; a program needn't handle non-finite values.
Results may differ from a plain program's by a relative error of at most 0.0051.
Values may be sent and summed in bfloat16 or wider, within the bound.
No kernel may reach another device: no remote copies, remote signals or barrier semaphores. Data moves between devices by JAX's collectives and lax.ppermute only.
A program may use at most 64 MiB of HBM per device.

v0:
```python
import jax
import jax.numpy as jnp
from jax import lax
from jax.sharding import PartitionSpec as P

DILATION_STEP = 512


gelu_coef = 0.7978845608028654


def shifted(value, axis, steps):
    count = lax.axis_size(axis)
    first, last = (max(0, -steps), min(count, count - steps))
    return lax.ppermute(value, axis, [(source, source + steps) for source in range(first, last)])


def gelu_value(v):
    inner = jnp.tanh(gelu_coef * (v + 0.044715 * v * v * v))
    return 0.5 * v * (1.0 + inner)


def gelu_slope(v):
    inner = jnp.tanh(gelu_coef * (v + 0.044715 * v * v * v))
    return 0.5 * (1.0 + inner) + 0.5 * v * (1.0 - inner * inner) * gelu_coef * (
        1.0 + 0.134145 * v * v
    )


def product_over_rows(value, weight):
    flat = value.reshape(-1, value.shape[-1])
    prod = jnp.dot(flat, weight, preferred_element_type=jnp.float32)
    return prod.reshape(value.shape[:-1] + (weight.shape[1],))


def product_backward(value, weight):
    flat = value.reshape(-1, value.shape[-1])
    prod = lax.dot_general(
        flat, weight, (((1,), (1,)), ((), ())), preferred_element_type=jnp.float32
    )
    return prod.reshape(value.shape[:-1] + (weight.shape[0],))


def spread_grad(binned):
    return (jnp.repeat(binned, 4, axis=-2).astype(jnp.float32) * 0.25).astype(jnp.bfloat16)


def pool_bins(values):
    wide = lax.optimization_barrier(values).astype(jnp.float32)
    shape = wide.shape
    grouped = wide.reshape(shape[:-2] + (shape[-2] // 4, 4, shape[-1]))
    return jnp.mean(grouped, axis=-2).astype(jnp.bfloat16)


def block_pass(xvalue, gvalue, params, earlier, later, grad_earlier, grad_later):
    scale_in, shift_in, tap_weight_stack, scale_mid, shift_mid, out_weight, out_bias = params
    xfull = xvalue.astype(jnp.float32)
    first = xfull * scale_in + shift_in
    layer_activations = gelu_value(first).astype(jnp.bfloat16)
    middle_state = (
        product_over_rows(earlier(layer_activations), tap_weight_stack[0])
        + product_over_rows(layer_activations, tap_weight_stack[1])
        + product_over_rows(later(layer_activations), tap_weight_stack[2])
    )
    second = middle_state * scale_mid + shift_mid
    hidden = gelu_value(second).astype(jnp.bfloat16)
    block_out = (xfull + product_over_rows(hidden, out_weight) + out_bias).astype(jnp.bfloat16)
    hidden_grad = product_backward(gvalue, out_weight)
    middle_gradient = (hidden_grad * gelu_slope(second) * scale_mid).astype(jnp.bfloat16)
    activation_gradient = (
        product_backward(grad_later(middle_gradient), tap_weight_stack[0])
        + product_backward(middle_gradient, tap_weight_stack[1])
        + product_backward(grad_earlier(middle_gradient), tap_weight_stack[2])
    )
    seq_grad = (
        gvalue.astype(jnp.float32) + activation_gradient * gelu_slope(first) * scale_in
    ).astype(jnp.bfloat16)
    return (block_out, seq_grad)


def local(
    seqs_in,
    pooled_grad,
    scale_in,
    shift_in,
    tap_weight_stack,
    scale_mid,
    shift_mid,
    out_weight,
    out_bias,
):
    params = (scale_in, shift_in, tap_weight_stack, scale_mid, shift_mid, out_weight, out_bias)
    batch, rows, width = seqs_in.shape
    stride = DILATION_STEP // rows
    out_grad = spread_grad(pooled_grad)
    block_out, seq_grad = block_pass(
        seqs_in,
        out_grad,
        params,
        lambda v: shifted(v, "seq", stride),
        lambda v: shifted(v, "seq", -stride),
        lambda v: shifted(v, "seq", stride),
        lambda v: shifted(v, "seq", -stride),
    )
    pooled = pool_bins(block_out)
    return (pooled, seq_grad)


def solution(mesh):
    in_specs = (
        P("groups", "seq", None),
        P("groups", "seq", None),
        P(),
        P(),
        P(),
        P(),
        P(),
        P(),
        P(),
    )
    out_specs = (P("groups", "seq", None), P("groups", "seq", None))
    return jax.shard_map(local, mesh=mesh, in_specs=in_specs, out_specs=out_specs, check_vma=False)
```

profile of v0, /device:TPU:8, one launch (start us, length us, event | category | flops | bytes accessed | tf_op | source)
XLA Modules:
  0.0 133.5 jit_solution(7543144371456438454)
XLA Ops:
  0.6 0.0 copy-start
  0.7 4.0 %fusion.9 = bf16[2,256,1536]{2,1,0:T(8,128)(2,1)} fusion(bf16[2,256,1536]{2,1,0:T(8,128)(2,1)} %param.9, f32[1536]{0:T(1024)} %param.12, f32[1536]{0:T(1024)} %param.11), kind=kLoop, calls=%fused_computation.14 | loop fusion | flops 9437184 | bytes 3158016 | tf_op jit(solution)/shard_map/convert_element_type | solution.py:59
  4.7 3.4 %collective-permute-start = (bf16[2,256,1536]{2,1,0:T(8,128)(2,1)}, bf16[2,256,1536]{2,1,0:T(8,128)(2,1)}, u32[]{:S(2)}, u32[]{:S(2)}) collective-permute-start(bf16[2,256,1536]{2,1,0:T(8,128)(2,1)} %fusion.9), channel_id=1, source_target_pairs={{0,2},{1,3},{2,4},{3,5},{4,6},{5,7},{6,8},{7,9},{8,10},{9,11},{10,... | collective-permute-start | bytes 4718600 | tf_op jit(solution)/shard_map/ppermute | solution.py:15
  8.1 3.3 %collective-permute-start.1 = (bf16[2,256,1536]{2,1,0:T(8,128)(2,1)}, bf16[2,256,1536]{2,1,0:T(8,128)(2,1)}, u32[]{:S(2)}, u32[]{:S(2)}) collective-permute-start(bf16[2,256,1536]{2,1,0:T(8,128)(2,1)} %fusion.9), channel_id=1, source_target_pairs={{2,0},{3,1},{4,2},{5,3},{6,4},{7,5},{8,6},{9,7},{10,8},{11,9},{12,... | collective-permute-start | bytes 4718600 | tf_op jit(solution)/shard_map/ppermute | solution.py:15
  11.4 0.1 multiply_convert_fusion.2
  11.5 1.6 %broadcast_in_dim.2 = bf16[2,64,4,1536]{3,2,1,0:T(4,128)(2,1)} broadcast(bf16[2,64,1536]{2,1,0:T(8,128)(2,1)S(1)} %multiply_convert_fusion.2), dimensions={0,1,3} | broadcast | bytes 1966080 | tf_op jit(solution)/shard_map/broadcast_in_dim | solution.py:45
  13.1 3.7 %convert_element_type.48 = bf16[2,256,1536]{2,1,0:T(8,128)(2,1)} reshape(bf16[2,64,4,1536]{3,2,1,0:T(4,128)(2,1)} %broadcast_in_dim.2) | data formatting | bytes 3145728 | tf_op jit(solution)/shard_map/convert_element_type | solution.py:45
  16.8 3.5 %fusion.27 = f32[2,256,768]{2,1,0:T(8,128)S(1)} fusion(bf16[2,256,1536]{2,1,0:T(8,128)(2,1)} %fusion.9, bf16[3,1536,768]{2,1,0:T(8,128)(2,1)} %param.13), kind=kOutput, calls=%fused_computation.34 | convolution fusion | flops 1207959552 | bytes 5505024 | tf_op jit(solution)/shard_map/dot_general | solution.py:32
  20.3 0.0 copy-start.9
  20.3 0.0 copy-start.10
  20.3 55.4 %collective-permute-done = bf16[2,256,1536]{2,1,0:T(8,128)(2,1)} collective-permute-done((bf16[2,256,1536]{2,1,0:T(8,128)(2,1)}, bf16[2,256,1536]{2,1,0:T(8,128)(2,1)}, u32[]{:S(2)}, u32[]{:S(2)}) %collective-permute-start) | collective-permute-done | bytes 1572896 | tf_op jit(solution)/shard_map/ppermute | solution.py:15
  75.7 3.5 %fusion.30 = f32[2,256,768]{2,1,0:T(8,128)S(1)} fusion(bf16[2,256,1536]{2,1,0:T(8,128)(2,1)} %collective-permute-done, bf16[3,1536,768]{2,1,0:T(8,128)(2,1)} %param.13), kind=kOutput, calls=%fused_computation.37 | convolution fusion | flops 1207959552 | bytes 5505024 | tf_op jit(solution)/shard_map/dot_general | solution.py:32
  79.3 0.0 collective-permute-done.1
  79.3 0.0 copy-done.9
  79.3 3.7 %multiply_add_fusion.2 = f32[2,256,768]{2,1,0:T(8,128)S(1)} fusion(f32[2,256,768]{2,1,0:T(8,128)S(1)} %fusion.30, f32[2,256,768]{2,1,0:T(8,128)S(1)} %fusion.27, f32[768]{0:T(1024)S(1)} %copy-done.9, f32[768]{0:T(1024)S(1)} %copy-done.10, bf16[2,256,1536]{2,1,0:T(8,128)(2,1)} %collective-permute-done.1, bf16[3,1536,768]{2,1,0:T(8,128)(2,1)} %param.13), kind=kOutput, calls=%fused_computation.54 | convolution fusion | flops 1209532416 | bytes 8656896 | tf_op jit(solution)/shard_map/dot_general | solution.py:32
  83.0 0.0 copy-start.1
  83.0 0.0 copy-start.8
  83.0 3.0 %fusion.45 = bf16[2,256,768]{2,1,0:T(8,128)(2,1)} fusion(f32[2,256,768]{2,1,0:T(8,128)S(1)} %multiply_add_fusion.2, bf16[2,256,1536]{2,1,0:T(8,128)(2,1)S(1)} %copy-done.3, bf16[768,1536]{1,0:T(8,128)(2,1)S(1)} %copy-done, f32[768]{0:T(1024)S(1)} %copy-done.10), kind=kOutput, calls=%fused_computation.52 | convolution fusion | flops 1215823872 | bytes 6294528 | tf_op jit(solution)/shard_map/dot_general | solution.py:38
  86.0 4.4 %collective-permute-start.3 = (bf16[2,256,768]{2,1,0:T(8,128)(2,1)}, bf16[2,256,768]{2,1,0:T(8,128)(2,1)}, u32[]{:S(2)}, u32[]{:S(2)}) collective-permute-start(bf16[2,256,768]{2,1,0:T(8,128)(2,1)} %fusion.45), channel_id=1, source_target_pairs={{0,2},{1,3},{2,4},{3,5},{4,6},{5,7},{6,8},{7,9},{8,10},{9,11},{10,... | collective-permute-start | bytes 2359304 | tf_op jit(solution)/shard_map/ppermute | solution.py:15
  90.4 2.5 %collective-permute-start.2 = (bf16[2,256,768]{2,1,0:T(8,128)(2,1)}, bf16[2,256,768]{2,1,0:T(8,128)(2,1)}, u32[]{:S(2)}, u32[]{:S(2)}) collective-permute-start(bf16[2,256,768]{2,1,0:T(8,128)(2,1)} %fusion.45), channel_id=1, source_target_pairs={{2,0},{3,1},{4,2},{5,3},{6,4},{7,5},{8,6},{9,7},{10,8},{11,9},{12,... | collective-permute-start | bytes 2359304 | tf_op jit(solution)/shard_map/ppermute | solution.py:15
  92.9 2.7 %fusion.17 = bf16[2,256,1536]{2,1,0:T(8,128)(2,1)} fusion(bf16[2,256,1536]{2,1,0:T(8,128)(2,1)S(1)} %copy-done.1, bf16[768,1536]{1,0:T(8,128)(2,1)S(1)} %copy-done, f32[1536]{0:T(1024)S(1)} %copy-done.8, f32[2,256,768]{2,1,0:T(8,128)S(1)} %multiply_add_fusion.2), kind=kOutput, calls=%fused_computation.22 | convolution fusion | flops 1214644224 | bytes 7084032 | tf_op jit(solution)/shard_map/dot_general | solution.py:32
  95.6 4.2 %reshape.56 = f32[2,64,4,1536]{3,2,1,0:T(4,128)} reshape(bf16[2,256,1536]{2,1,0:T(8,128)(2,1)} %fusion.17) | data formatting | bytes 4718592 | tf_op jit(solution)/shard_map/reshape | solution.py:51
  99.8 3.8 %reduce_sum.9 = f32[2,64,1536]{2,1,0:T(8,128)S(1)} reduce(f32[2,64,4,1536]{3,2,1,0:T(4,128)} %reshape.56, f32[]{:T(128)} %constant.11.clone.1), dimensions={2}, to_apply=%region_0.0 | reduce | flops 589824 | bytes 3932164 | tf_op jit(solution)/shard_map/reduce_sum | solution.py:52
  103.5 0.8 multiply_convert_fusion.3
  104.3 3.3 %fusion.25 = f32[2,256,1536]{2,1,0:T(8,128)S(1)} fusion(bf16[2,256,768]{2,1,0:T(8,128)(2,1)} %fusion.45, bf16[3,1536,768]{2,1,0:T(8,128)(2,1)} %param.13), kind=kOutput, calls=%fused_computation.32 | convolution fusion | flops 1207959552 | bytes 6291456 | tf_op jit(solution)/shard_map/dot_general | solution.py:38
  107.7 0.0 copy-start.2
  107.7 0.0 copy-start.6
  107.7 0.0 copy-start.7
  107.7 15.7 %collective-permute-done.3 = bf16[2,256,768]{2,1,0:T(8,128)(2,1)} collective-permute-done((bf16[2,256,768]{2,1,0:T(8,128)(2,1)}, bf16[2,256,768]{2,1,0:T(8,128)(2,1)}, u32[]{:S(2)}, u32[]{:S(2)}) %collective-permute-start.3) | collective-permute-done | bytes 786464 | tf_op jit(solution)/shard_map/ppermute | solution.py:15
  123.5 3.3 %fusion.21 = f32[2,256,1536]{2,1,0:T(8,128)S(1)} fusion(bf16[2,256,768]{2,1,0:T(8,128)(2,1)} %collective-permute-done.3, bf16[3,1536,768]{2,1,0:T(8,128)(2,1)} %param.13), kind=kOutput, calls=%fused_computation.28 | convolution fusion | flops 1207959552 | bytes 6291456 | tf_op jit(solution)/shard_map/dot_general | solution.py:38
  126.8 0.0 collective-permute-done.2
  126.8 6.7 %fusion.16 = bf16[2,256,1536]{2,1,0:T(8,128)(2,1)} fusion(bf16[2,256,1536]{2,1,0:T(8,128)(2,1)S(1)} %copy-done.2, f32[2,256,1536]{2,1,0:T(8,128)S(1)} %fusion.21, f32[2,256,1536]{2,1,0:T(8,128)S(1)} %fusion.25, bf16[2,256,768]{2,1,0:T(8,128)(2,1)} %collective-permute-done.2, bf16[2,256,1536]{2,1,0:T(8,128)(2,1)S(1)} %copy-done.4, ...), kind=kOutput, calls=%fused_computation.21 | convolution fusion | flops 1229193216 | bytes 14168064 | tf_op jit(solution)/shard_map/dot_general | solution.py:38
  (13 shorter events, 0.0 us)
Async XLA Ops:
  0.6 82.4 %copy-start = (bf16[768,1536]{1,0:T(8,128)(2,1)S(1)}, bf16[768,1536]{1,0:T(8,128)(2,1)}, u32[]{:S(2)}) copy-start(bf16[768,1536]{1,0:T(8,128)(2,1)} %param.16) | copy-start | bytes 7077892
  0.6 10.8 %copy-start.5 = (bf16[2,64,1536]{2,1,0:T(8,128)(2,1)S(1)}, bf16[2,64,1536]{2,1,0:T(8,128)(2,1)}, u32[]{:S(2)}) copy-start(bf16[2,64,1536]{2,1,0:T(8,128)(2,1)} %param.10) | copy-start | bytes 1179652
  4.7 71.1 %collective-permute-start = (bf16[2,256,1536]{2,1,0:T(8,128)(2,1)}, bf16[2,256,1536]{2,1,0:T(8,128)(2,1)}, u32[]{:S(2)}, u32[]{:S(2)}) collective-permute-start(bf16[2,256,1536]{2,1,0:T(8,128)(2,1)} %fusion.9), channel_id=1, source_target_pairs={{0,2},{1,3},{2,4},{3,5},{4,6},{5,7},{6,8},{7,9},{8,10},{9,11},{10,... | collective-permute-start | bytes 4718600 | tf_op jit(solution)/shard_map/ppermute | solution.py:15
  8.1 71.2 %collective-permute-start.1 = (bf16[2,256,1536]{2,1,0:T(8,128)(2,1)}, bf16[2,256,1536]{2,1,0:T(8,128)(2,1)}, u32[]{:S(2)}, u32[]{:S(2)}) collective-permute-start(bf16[2,256,1536]{2,1,0:T(8,128)(2,1)} %fusion.9), channel_id=1, source_target_pairs={{2,0},{3,1},{4,2},{5,3},{6,4},{7,5},{8,6},{9,7},{10,8},{11,9},{12,... | collective-permute-start | bytes 4718600 | tf_op jit(solution)/shard_map/ppermute | solution.py:15
  20.3 59.0 %copy-start.9 = (f32[768]{0:T(1024)S(1)}, f32[768]{0:T(1024)}, u32[]{:S(2)}) copy-start(f32[768]{0:T(1024)} %param.15) | copy-start | bytes 9220
  20.3 59.0 %copy-start.10 = (f32[768]{0:T(1024)S(1)}, f32[768]{0:T(1024)}, u32[]{:S(2)}) copy-start(f32[768]{0:T(1024)} %param.14) | copy-start | bytes 9220
  79.3 3.7 %copy-start.3 = (bf16[2,256,1536]{2,1,0:T(8,128)(2,1)S(1)}, bf16[2,256,1536]{2,1,0:T(8,128)(2,1)}, u32[]{:S(2)}) copy-start(bf16[2,256,1536]{2,1,0:T(8,128)(2,1)} %convert_element_type.48) | copy-start | bytes 4718596
  83.0 9.9 %copy-start.1 = (bf16[2,256,1536]{2,1,0:T(8,128)(2,1)S(1)}, bf16[2,256,1536]{2,1,0:T(8,128)(2,1)}, u32[]{:S(2)}) copy-start(bf16[2,256,1536]{2,1,0:T(8,128)(2,1)} %param.9) | copy-start | bytes 4718596
  83.0 9.9 %copy-start.8 = (f32[1536]{0:T(1024)S(1)}, f32[1536]{0:T(1024)}, u32[]{:S(2)}) copy-start(f32[1536]{0:T(1024)} %param.17) | copy-start | bytes 18436
  86.0 37.5 %collective-permute-start.3 = (bf16[2,256,768]{2,1,0:T(8,128)(2,1)}, bf16[2,256,768]{2,1,0:T(8,128)(2,1)}, u32[]{:S(2)}, u32[]{:S(2)}) collective-permute-start(bf16[2,256,768]{2,1,0:T(8,128)(2,1)} %fusion.45), channel_id=1, source_target_pairs={{0,2},{1,3},{2,4},{3,5},{4,6},{5,7},{6,8},{7,9},{8,10},{9,11},{10,... | collective-permute-start | bytes 2359304 | tf_op jit(solution)/shard_map/ppermute | solution.py:15
  90.4 36.4 %collective-permute-start.2 = (bf16[2,256,768]{2,1,0:T(8,128)(2,1)}, bf16[2,256,768]{2,1,0:T(8,128)(2,1)}, u32[]{:S(2)}, u32[]{:S(2)}) collective-permute-start(bf16[2,256,768]{2,1,0:T(8,128)(2,1)} %fusion.45), channel_id=1, source_target_pairs={{2,0},{3,1},{4,2},{5,3},{6,4},{7,5},{8,6},{9,7},{10,8},{11,9},{12,... | collective-permute-start | bytes 2359304 | tf_op jit(solution)/shard_map/ppermute | solution.py:15
  107.7 19.1 %copy-start.2 = (bf16[2,256,1536]{2,1,0:T(8,128)(2,1)S(1)}, bf16[2,256,1536]{2,1,0:T(8,128)(2,1)}, u32[]{:S(2)}) copy-start(bf16[2,256,1536]{2,1,0:T(8,128)(2,1)} %param.9) | copy-start | bytes 4718596
  107.7 19.1 %copy-start.4 = (bf16[2,256,1536]{2,1,0:T(8,128)(2,1)S(1)}, bf16[2,256,1536]{2,1,0:T(8,128)(2,1)}, u32[]{:S(2)}) copy-start(bf16[2,256,1536]{2,1,0:T(8,128)(2,1)} %convert_element_type.48) | copy-start | bytes 4718596
  107.7 19.1 %copy-start.6 = (f32[1536]{0:T(1024)S(1)}, f32[1536]{0:T(1024)}, u32[]{:S(2)}) copy-start(f32[1536]{0:T(1024)} %param.12) | copy-start | bytes 18436
  107.7 19.1 %copy-start.7 = (f32[1536]{0:T(1024)S(1)}, f32[1536]{0:T(1024)}, u32[]{:S(2)}) copy-start(f32[1536]{0:T(1024)} %param.11) | copy-start | bytes 18436
where the time goes:
time: 135 us; the launch traced here: 133 us
  waiting for transfers between devices  71.2 us (53%)
  matrix products  29.6 us (22%)
  starting transfers between devices  13.6 us (10%)
  local copies, waits for them, and re-layouts  9.52 us (7%)
  other arithmetic  8.62 us (6%)
    ppermute x4, waiting for transfers between devices, shifted(): lax.ppermute(value, axis, [(source, source + steps) for source in range(f...  71.2 us
    dot_general x4, matrix products, product_backward(): lax.dot_general(flat, weight, (((1,), (1,)), ((), ())), preferred_element...  16.3 us
    ppermute x4, starting transfers between devices, shifted(): lax.ppermute(value, axis, [(source, source + steps) for source in range(f...  13.6 us
    dot_general x4, matrix products, product_over_rows(): prod = jnp.dot(flat, weight, preferred_element_type=jnp.float32)  13.4 us
    reshape x1, local copies, waits for them, and re-layouts, pool_bins(): grouped = wide.reshape(shape[:-2] + (shape[-2] // 4, 4, shape[-1]))  4.18 us
    convert_element_type x1, other arithmetic, block_pass(): layer_activations = gelu_value(first).astype(jnp.bfloat16)  4 us
    reduce_sum x1, other arithmetic, pool_bins(): return jnp.mean(grouped, axis=-2).astype(jnp.bfloat16)  3.76 us
    convert_element_type x1, local copies, waits for them, and re-layouts, spread_grad(): (jnp.repeat(binned, 4, axis=-2).astype(jnp.float32) * 0.25).astype(jnp.bf...  3.71 us
  transfers between devices with their start and end apart: 4, of which 2 were waited for; matrix products, arithmetic and copies ran while one was open for 23% of the time, Pallas kernels for 0%

commit v1 on v0

v1 whole, which is shorter than its diff:
```python
import functools

import jax
import jax.numpy as jnp
from jax import lax
from jax.experimental import pallas as pl
from jax.experimental.pallas import tpu as pltpu
from jax.sharding import PartitionSpec as P

DILATION_STEP = 512
BIN = 4
LANES = 128
AXIS = "seq"
GELU_COEF = 0.7978845608028654
F32 = jnp.float32
BF16 = jnp.bfloat16
LIMIT = 12 * 1024 * 1024


def gelu_value(v):
    inner = jnp.tanh(v * (GELU_COEF + (GELU_COEF * 0.044715) * v * v))
    half = 0.5 * v
    return half + half * inner


def gelu_both(v):
    square = v * v
    inner = jnp.tanh(v * (GELU_COEF + (GELU_COEF * 0.044715) * square))
    half = 0.5 * v
    value = half + half * inner
    slope = (0.5 + 0.5 * inner) + half * (1.0 - inner * inner) * (
        GELU_COEF + (GELU_COEF * 0.134145) * square
    )
    return value, slope


def gelu_slope(v):
    return gelu_both(v)[1]


def dot_nn(a, b):
    return jnp.dot(a, b, preferred_element_type=F32)


def dot_nt(a, b):
    return lax.dot_general(a, b, (((1,), (1,)), ((), ())), preferred_element_type=F32)


def averaging(bins, rows):
    row = lax.broadcasted_iota(jnp.int32, (bins, rows), 0)
    column = lax.broadcasted_iota(jnp.int32, (bins, rows), 1)
    inside = (column >= row * BIN) & (column < row * BIN + BIN)
    return jnp.where(inside, 1.0 / BIN, 0.0).astype(BF16)


def spreading(rows, bins):
    row = lax.broadcasted_iota(jnp.int32, (rows, bins), 0)
    column = lax.broadcasted_iota(jnp.int32, (rows, bins), 1)
    inside = (row >= column * BIN) & (row < column * BIN + BIN)
    return jnp.where(inside, 1.0 / BIN, 0.0).astype(BF16)


def near_tap(stride):
    return 2 * lax.rem(lax.div(lax.axis_index(AXIS), stride), 2)


def local_call(body, name, operands, outs, cost, scratch=()):
    flops, nbytes, trans = cost
    single = not isinstance(outs, list)
    space = pl.BlockSpec(memory_space=pltpu.VMEM)
    shapes = [pltpu.VMEM(s, d) for s, d in ([outs] if single else outs)]
    return pl.pallas_call(
        body,
        name=name,
        in_specs=[space] * len(operands),
        out_specs=space if single else [space] * len(outs),
        out_shape=shapes[0] if single else shapes,
        scratch_shapes=list(scratch),
        compiler_params=pltpu.CompilerParams(vmem_limit_bytes=LIMIT),
        cost_estimate=pl.CostEstimate(flops=flops, bytes_accessed=nbytes, transcendentals=trans),
    )(*[pltpu.with_memory_space_constraint(v, pltpu.VMEM) for v in operands])


def front_two_body(which, x_ref, s_ref, b_ref, w_ref, a_ref, p_ref, q_ref):
    a_ref[...] = gelu_value(x_ref[which].astype(F32) * s_ref[...] + b_ref[...]).astype(BF16)
    p_ref[...] = dot_nn(a_ref[...], w_ref[0]).astype(BF16)
    q_ref[...] = dot_nn(a_ref[...], w_ref[2]).astype(BF16)


def front_two(x, which, scale, shift, taps):
    _, rows, width = x.shape
    mid = taps.shape[2]
    return local_call(
        functools.partial(front_two_body, which),
        "front_two",
        [x, scale, shift, taps],
        [((rows, width), BF16), ((rows, mid), BF16), ((rows, mid), BF16)],
        (4 * rows * width * mid, 4 * rows * width, rows * width),
    )


def front_one_body(which, stride, x_ref, s_ref, b_ref, w_ref, a_ref, p_ref):
    a_ref[...] = gelu_value(x_ref[which].astype(F32) * s_ref[...] + b_ref[...]).astype(BF16)
    p_ref[...] = dot_nn(a_ref[...], w_ref[2 - near_tap(stride)]).astype(BF16)


def front_one(x, which, scale, shift, taps, stride):
    _, rows, width = x.shape
    mid = taps.shape[2]
    return local_call(
        functools.partial(front_one_body, which, stride),
        "front_one",
        [x, scale, shift, taps],
        [((rows, width), BF16), ((rows, mid), BF16)],
        (2 * rows * width * mid, 4 * rows * width, rows * width),
    )


def centre_body(stride, a_ref, b_ref, w_ref, p_ref, q_ref, k_ref):
    k_ref[...] = dot_nn(b_ref[...], w_ref[near_tap(stride)])
    p_ref[...] = dot_nn(a_ref[...], w_ref[1])
    q_ref[...] = dot_nn(b_ref[...], w_ref[1])


def centre(a, b, taps, stride):
    rows, width = a.shape
    mid = taps.shape[2]
    return local_call(
        functools.partial(centre_body, stride),
        "centre",
        [a, b, taps],
        [((rows, mid), F32)] * 3,
        (6 * rows * width * mid, 4 * rows * width, 0),
    )


def join_body(k_ref, r_ref, o_ref):
    o_ref[...] = (k_ref[...] + r_ref[...].astype(F32)).astype(BF16)


def join(kept, came):
    return local_call(
        join_body, "join", [kept, came], (kept.shape, BF16), (kept.size, 8 * kept.size, 0)
    )


def hidden_grad_body(g_ref, w_ref, o_ref):
    for n in range(g_ref.shape[0]):
        o_ref[n] = dot_nt((g_ref[n].astype(F32) * (1.0 / BIN)).astype(BF16), w_ref[...])


def hidden_grad(binned, weight):
    batch, bins, width = binned.shape
    mid = weight.shape[0]
    return local_call(
        hidden_grad_body,
        "hidden_grad",
        [binned, weight],
        ((batch, bins, mid), F32),
        (2 * batch * bins * width * mid, 2 * batch * bins * width, 0),
    )


def middle_body(count, which, *refs):
    parts = refs[:count]
    p_ref, s_ref, b_ref, hg_ref, g_ref, h_ref, wide_ref = refs[count:]
    _, bins, width = hg_ref.shape
    for lane in range(width // LANES):
        columns = slice(lane * LANES, lane * LANES + LANES)
        for k in range(BIN):
            wide_ref[lane, pl.ds(k, bins, stride=BIN), :] = hg_ref[which, :, columns]
    scales, shifts = s_ref[...].reshape(1, width), b_ref[...].reshape(1, width)
    for lane in range(width // LANES):
        columns = slice(lane * LANES, lane * LANES + LANES)
        mid = p_ref[:, columns]
        for part in parts:
            mid = mid + part[:, columns].astype(F32)
        scale = scales[:, columns]
        value, slope = gelu_both(mid * scale + shifts[:, columns])
        g_ref[:, columns] = (wide_ref[lane] * slope * scale).astype(BF16)
        h_ref[:, columns] = value.astype(BF16)


def middle(parts, centre_part, which, scale, shift, hidden_grads):
    rows, mid = centre_part.shape
    return local_call(
        functools.partial(middle_body, len(parts), which),
        "middle",
        [*parts, centre_part, scale, shift, hidden_grads],
        [((rows, mid), BF16), ((rows, mid), BF16)],
        (30 * rows * mid, 12 * rows * mid, rows * mid),
        scratch=[pltpu.VMEM((mid // LANES, rows, LANES), F32)],
    )


def pooled_body(count, *refs):
    hidden = refs[:count]
    x_ref, w_ref, b_ref, o_ref = refs[count:]
    _, bins, width = o_ref.shape
    average = averaging(bins, x_ref.shape[1])
    for n in range(count):
        mean = dot_nn(average, hidden[n][...]).astype(BF16)
        o_ref[n] = (
            dot_nn(average, x_ref[n]) + dot_nn(mean, w_ref[...]) + b_ref[...]
        ).astype(BF16)


def pooled_out(x, hidden, weight, bias):
    batch, rows, width = x.shape
    bins = rows // BIN
    mid = weight.shape[0]
    return local_call(
        functools.partial(pooled_body, batch),
        "pooled",
        [*hidden, x, weight, bias],
        ((batch, bins, width), BF16),
        (2 * batch * bins * width * (mid + rows), 2 * batch * rows * width, 0),
    )


def back_first_body(g_ref, w_ref, o_ref):
    o_ref[...] = dot_nt(g_ref[...], w_ref[1])


def back_first(g, taps):
    rows, mid = g.shape
    width = taps.shape[1]
    return local_call(
        back_first_body,
        "back_first",
        [g, taps],
        ((rows, width), F32),
        (2 * rows * width * mid, 4 * rows * width, 0),
    )


def back_near_body(stride, c_ref, g_ref, w_ref, o_ref):
    o_ref[...] = c_ref[...] + dot_nt(g_ref[...], w_ref[near_tap(stride)])


def back_near(total, g, taps, stride):
    rows, mid = g.shape
    width = taps.shape[1]
    return local_call(
        functools.partial(back_near_body, stride),
        "back_near",
        [total, g, taps],
        ((rows, width), F32),
        (2 * rows * width * mid, 8 * rows * width, 0),
    )


def final_body(count, which, stride, tiles, *refs):
    grads = refs[:count]
    c_ref, w_ref, x_ref, og_ref, s_ref, b_ref, _, o_ref, out_ref, sems = refs[count:]
    rows, width = c_ref.shape
    tile = width // tiles
    spread = spreading(rows, og_ref.shape[1])
    scales, shifts = s_ref[...].reshape(1, width), b_ref[...].reshape(1, width)
    taps = [2 - near_tap(stride)] if count == 1 else [0, 2]
    copies = []
    for n in range(tiles):
        columns = slice(n * tile, n * tile + tile)
        total = c_ref[:, columns]
        for g, tap in zip(grads, taps):
            total = total + dot_nt(g[...], w_ref[tap, columns, :])
        scale = scales[:, columns]
        slope = gelu_slope(x_ref[which, :, columns].astype(F32) * scale + shifts[:, columns])
        out_ref[:, columns] = (
            dot_nn(spread, og_ref[which, :, columns]) + total * slope * scale
        ).astype(BF16)
        copy = pltpu.make_async_copy(
            out_ref.at[:, columns], o_ref.at[which, :, columns], sems.at[n]
        )
        copy.start()
        copies.append(copy)
    for copy in copies:
        copy.wait()


def final(total, grads, taps, x, binned, which, scale, shift, stride, onto):
    batch, rows, width = x.shape
    mid = taps.shape[2]
    tiles = 3
    count = len(grads)
    operands = [*grads, total, taps, x, binned, scale, shift]
    space = pl.BlockSpec(memory_space=pltpu.VMEM)
    anywhere = pl.BlockSpec(memory_space=pltpu.HBM)
    operands = [pltpu.with_memory_space_constraint(v, pltpu.VMEM) for v in operands]
    specs = [space] * len(operands)
    body = functools.partial(final_body, count, which, stride, tiles)
    if onto is None:
        full = body
        body = lambda *refs: full(*refs[: len(specs)], None, *refs[len(specs) :])
        aliases = {}
        in_specs = specs
    else:
        aliases = {len(operands): 0}
        operands = operands + [onto]
        in_specs = specs + [anywhere]
    return pl.pallas_call(
        body,
        name="final",
        in_specs=in_specs,
        out_specs=anywhere,
        out_shape=jax.ShapeDtypeStruct((batch, rows, width), BF16),
        scratch_shapes=[pltpu.VMEM((rows, width), BF16), pltpu.SemaphoreType.DMA((tiles,))],
        input_output_aliases=aliases,
        compiler_params=pltpu.CompilerParams(vmem_limit_bytes=LIMIT),
        cost_estimate=pl.CostEstimate(
            flops=2 * count * rows * width * mid,
            bytes_accessed=8 * rows * width,
            transcendentals=rows * width,
        ),
    )(*operands)


def local(
    seqs_in,
    pooled_grad,
    scale_in,
    shift_in,
    tap_weight_stack,
    scale_mid,
    shift_mid,
    out_weight,
    out_bias,
):
    rows = seqs_in.shape[1]
    count = lax.axis_size(AXIS)
    stride = DILATION_STEP // rows
    blocks = count // stride
    taps = tap_weight_stack

    def hop(value, steps):
        return lax.ppermute(
            value, AXIS, [(i, i + steps) for i in range(count) if 0 <= i + steps < count]
        )

    def block_permute(value, move):
        pairs = []
        for b in range(blocks):
            to = move(b)
            if 0 <= to < blocks:
                pairs += [(b * stride + i, to * stride + i) for i in range(stride)]
        return lax.ppermute(value, AXIS, pairs)

    def swap(value):
        return block_permute(value, lambda b: b ^ 1)

    def inward(value):
        return block_permute(value, lambda b: b + 2 if b % 2 else b - 2)

    def outward(value):
        return block_permute(value, lambda b: b - 2 if b % 2 else b + 2)

    act0, first0, last0 = front_two(seqs_in, 0, scale_in, shift_in, taps)
    from_before0 = hop(first0, stride)
    from_after0 = hop(last0, -stride)
    act1, sent1 = front_one(seqs_in, 1, scale_in, shift_in, taps, stride)
    came1 = inward(sent1)
    centre0, centre1, kept1 = centre(act0, act1, taps, stride)
    hg = hidden_grad(pooled_grad, out_weight)
    both1 = swap(join(kept1, came1))
    grad0, hid0 = middle([from_before0, from_after0], centre0, 0, scale_mid, shift_mid, hg)
    near0 = swap(grad0)
    total0 = back_first(grad0, taps)
    grad1, hid1 = middle([both1], centre1, 1, scale_mid, shift_mid, hg)
    g_before1 = hop(grad1, stride)
    g_after1 = hop(grad1, -stride)
    far0 = outward(near0)
    total1 = back_first(grad1, taps)
    pooled = pooled_out(seqs_in, [hid0, hid1], out_weight, out_bias)
    total0 = back_near(total0, near0, taps, stride)
    grads = final(
        total0, [far0], taps, seqs_in, pooled_grad, 0, scale_in, shift_in, stride, None
    )
    grads = final(
        total1,
        [g_after1, g_before1],
        taps,
        seqs_in,
        pooled_grad,
        1,
        scale_in,
        shift_in,
        stride,
        grads,
    )
    return pooled, grads


def solution(mesh):
    in_specs = (
        P("groups", "seq", None),
        P("groups", "seq", None),
        P(),
        P(),
        P(),
        P(),
        P(),
        P(),
        P(),
    )
    out_specs = (P("groups", "seq", None), P("groups", "seq", None))
    return jax.shard_map(local, mesh=mesh, in_specs=in_specs, out_specs=out_specs, check_vma=False)
```

time: 135 us -> 75.6 us (0.56)
  waiting for transfers between devices: 71.2 us -> 31 us
  matrix products: 29.6 us -> 0 us
  Pallas kernels: 0 us -> 17.3 us
  other arithmetic: 8.62 us -> 0.01 us
  starting transfers between devices: 13.6 us -> 19.2 us
  local copies, waits for them, and re-layouts: 9.52 us -> 6.61 us
    ppermute x4 -> x8, waiting for transfers between devices: 71.2 us -> 31 us  [the longest x4 15.7 us: hop(): lax.ppermute(value, AXIS, [(i, i + steps) for i in range(count) if 0 <= i...]
    dot_general x8 -> x0, matrix products: 29.6 us -> none  [the longest x4 16.3 us: product_backward(): lax.dot_general(flat, weight, (((1,), (1,)), ((), ())), preferred_element...]
    pallas_call x0 -> x13, Pallas kernels: none -> 17.3 us  [the longest x11 12 us: local_call(): pl.pallas_call(body, name=name, in_specs=[space] * len(operands), out_spe...]
    unnamed x22 -> x29, local copies, waits for them, and re-layouts: 0.07 us -> 6.61 us
    ppermute x4 -> x8, starting transfers between devices: 13.6 us -> 19.2 us  [the longest x4 13.2 us: hop(): lax.ppermute(value, AXIS, [(i, i + steps) for i in range(count) if 0 <= i...]
    convert_element_type x3 -> x0, other arithmetic: 4.86 us -> none  [the longest x1 4 us: block_pass(): layer_activations = gelu_value(first).astype(jnp.bfloat16)]
    reshape x1 -> x0, local copies, waits for them, and re-layouts: 4.18 us -> none  [pool_bins(): grouped = wide.reshape(shape[:-2] + (shape[-2] // 4, 4, shape[-1]))]
    reduce_sum x1 -> x0, other arithmetic: 3.76 us -> none  [pool_bins(): return jnp.mean(grouped, axis=-2).astype(jnp.bfloat16)]
  transfers between devices with their start and end apart: 4 -> 8, of which waited for: 2 -> 6; matrix products, arithmetic and copies ran while one was open for 23% -> 1% of each run, Pallas kernels for 0% -> 17%
where the time goes in v1:
time: 75.6 us; the launch traced here: 75.3 us
  waiting for transfers between devices  31 us (41%)
  starting transfers between devices  19.2 us (25%)
  Pallas kernels  17.3 us (23%)
  local copies, waits for them, and re-layouts  6.61 us (9%)
  between operations  1.1 us (1%)
    ppermute x4, waiting for transfers between devices, hop(): lax.ppermute(value, AXIS, [(i, i + steps) for i in range(count) if 0 <= i...  15.7 us
    ppermute x4, waiting for transfers between devices, block_permute(): return lax.ppermute(value, AXIS, pairs)  15.3 us
    ppermute x4, starting transfers between devices, hop(): lax.ppermute(value, AXIS, [(i, i + steps) for i in range(count) if 0 <= i...  13.2 us
    pallas_call x11, Pallas kernels, local_call(): pl.pallas_call(body, name=name, in_specs=[space] * len(operands), out_spe...  12 us
    unnamed x29, local copies, waits for them, and re-layouts  6.61 us
    ppermute x4, starting transfers between devices, block_permute(): return lax.ppermute(value, AXIS, pairs)  6.08 us
    pallas_call x2, Pallas kernels, final(): pl.pallas_call(body, name='final', in_specs=in_specs, out_specs=anywhere,...  5.24 us
  transfers between devices with their start and end apart: 8, of which 6 were waited for; matrix products, arithmetic and copies ran while one was open for 1% of the time, Pallas kernels for 17%

profile of v1, /device:TPU:8, one launch (start us, length us, event | category | flops | bytes accessed | tf_op | source)
XLA Modules:
  0.0 75.3 jit_solution(8576941664828574991)
XLA Ops:
  0.6 3.0 %copy-done = bf16[3,1536,768]{2,1,0:T(8,128)(2,1)S(1)} copy-done((bf16[3,1536,768]{2,1,0:T(8,128)(2,1)S(1)}, bf16[3,1536,768]{2,1,0:T(8,128)(2,1)}, u32[]{:S(2)}) %copy-start) | copy-done | bytes 7077912
  3.6 1.4 %copy-done.1 = bf16[2,256,1536]{2,1,0:T(8,128)(2,1)S(1)} copy-done((bf16[2,256,1536]{2,1,0:T(8,128)(2,1)S(1)}, bf16[2,256,1536]{2,1,0:T(8,128)(2,1)}, u32[]{:S(2)}) %copy-start.1) | copy-done | bytes 1572888
  5.1 0.7 copy-done.5
  5.7 0.7 copy-done.7
  6.4 1.6 %front_two.1 = (bf16[256,1536]{1,0:T(8,128)(2,1)S(1)}, bf16[256,768]{1,0:T(8,128)(2,1)S(1)}, bf16[256,768]{1,0:T(8,128)(2,1)S(1)}) custom-call(bf16[2,256,1536]{2,1,0:T(8,128)(2,1)S(1)} %copy-done.1, f32[1536]{0:T(1024)S(1)} %copy-done.5, f32[1536]{0:T(1024)S(1)} %copy-done.7, bf16[3,1536,768]{2,1,0:T(8,128)(2,1)S(1)} %copy-done), custom_call_target="tpu_custom_call" | custom-call | flops 1207959552 | bytes 1572864 | tf_op jit(solution)/shard_map/front_two/pallas_call | solution.py:72
  8.1 3.4 %collective-permute-start = (bf16[256,768]{1,0:T(8,128)(2,1)S(1)}, bf16[256,768]{1,0:T(8,128)(2,1)S(1)}, u32[]{:S(2)}, u32[]{:S(2)}) collective-permute-start(bf16[256,768]{1,0:T(8,128)(2,1)S(1)} %get-tuple-element.14), channel_id=1, source_target_pairs={{0,2},{1,3},{2,4},{3,5},{4,6},{5,7},{6,8},{7,9},{8,10},{9,11},{10,... | collective-permute-start | bytes 1179656 | tf_op jit(solution)/shard_map/ppermute | solution.py:336
  11.5 3.6 %collective-permute-start.1 = (bf16[256,768]{1,0:T(8,128)(2,1)S(1)}, bf16[256,768]{1,0:T(8,128)(2,1)S(1)}, u32[]{:S(2)}, u32[]{:S(2)}) collective-permute-start(bf16[256,768]{1,0:T(8,128)(2,1)S(1)} %get-tuple-element.15), channel_id=1, source_target_pairs={{2,0},{3,1},{4,2},{5,3},{6,4},{7,5},{8,6},{9,7},{10,8},{11,9},{12,... | collective-permute-start | bytes 1179656 | tf_op jit(solution)/shard_map/ppermute | solution.py:336
  15.1 1.2 %front_one.1 = (bf16[256,1536]{1,0:T(8,128)(2,1)S(1)}, bf16[256,768]{1,0:T(8,128)(2,1)S(1)}) custom-call(bf16[2,256,1536]{2,1,0:T(8,128)(2,1)S(1)} %copy-done.1, f32[1536]{0:T(1024)S(1)} %copy-done.5, f32[1536]{0:T(1024)S(1)} %copy-done.7, bf16[3,1536,768]{2,1,0:T(8,128)(2,1)S(1)} %copy-done), custom_call_target="tpu_custom_call" | custom-call | flops 603979776 | bytes 1572864 | tf_op jit(solution)/shard_map/front_one/pallas_call | solution.py:72
  16.3 1.9 %collective-permute-start.2 = (bf16[256,768]{1,0:T(8,128)(2,1)S(1)}, bf16[256,768]{1,0:T(8,128)(2,1)S(1)}, u32[]{:S(2)}, u32[]{:S(2)}) collective-permute-start(bf16[256,768]{1,0:T(8,128)(2,1)S(1)} %get-tuple-element.21), channel_id=1, source_target_pairs={{2,6},{3,7},{4,0},{5,1},{6,10},{7,11},{8,4},{9,5},{10,14},{11,15},... | collective-permute-start | bytes 1179656 | tf_op jit(solution)/shard_map/ppermute | solution.py:346
  18.3 1.5 %hidden_grad.1.refs_5_.refs_4_ = f32[2,64,768]{2,1,0:T(8,128)S(1)} custom-call(bf16[2,64,1536]{2,1,0:T(8,128)(2,1)S(1)} %copy-done.4, bf16[768,1536]{1,0:T(8,128)(2,1)S(1)} %copy-done.3), custom_call_target="tpu_custom_call" | custom-call | flops 301989888 | bytes 393216 | tf_op jit(solution)/shard_map/hidden_grad/pallas_call | solution.py:72
  19.8 2.0 %centre.1 = (f32[256,768]{1,0:T(8,128)S(1)}, f32[256,768]{1,0:T(8,128)S(1)}, f32[256,768]{1,0:T(8,128)S(1)}) custom-call(bf16[256,1536]{1,0:T(8,128)(2,1)S(1)} %get-tuple-element.16.a_ref, bf16[256,1536]{1,0:T(8,128)(2,1)S(1)} %get-tuple-element.17.b_ref, bf16[3,1536,768]{2,1,0:T(8,128)(2,1)S(1)} %bitcast.1), custom_call_target="tpu_custom_call" | custom-call | flops 1811939328 | bytes 1572864 | tf_op jit(solution)/shard_map/centre/pallas_call | solution.py:72
  21.9 6.4 %collective-permute-done.refs_0_ = bf16[256,768]{1,0:T(8,128)(2,1)S(1)} collective-permute-done((bf16[256,768]{1,0:T(8,128)(2,1)S(1)}, bf16[256,768]{1,0:T(8,128)(2,1)S(1)}, u32[]{:S(2)}, u32[]{:S(2)}) %collective-permute-start) | collective-permute-done | bytes 393248 | tf_op jit(solution)/shard_map/ppermute | solution.py:336
  28.3 1.9 %collective-permute-done.1.refs_1_ = bf16[256,768]{1,0:T(8,128)(2,1)S(1)} collective-permute-done((bf16[256,768]{1,0:T(8,128)(2,1)S(1)}, bf16[256,768]{1,0:T(8,128)(2,1)S(1)}, u32[]{:S(2)}, u32[]{:S(2)}) %collective-permute-start.1) | collective-permute-done | bytes 393248 | tf_op jit(solution)/shard_map/ppermute | solution.py:336
  30.2 0.9 %middle.2 = (bf16[256,768]{1,0:T(8,128)(2,1)S(1)}, bf16[256,768]{1,0:T(8,128)(2,1)S(1)}) custom-call(bf16[256,768]{1,0:T(8,128)(2,1)S(1)} %collective-permute-done.refs_0_, bf16[256,768]{1,0:T(8,128)(2,1)S(1)} %collective-permute-done.1.refs_1_, f32[256,768]{1,0:T(8,128)S(1)} %get-tuple-element.18.refs_2_, f32[768]{0:T(1024)S(1)} %copy-done.9, ...), custom_call_target="tpu_custom_call" | custom-call | flops 5898240 | bytes 2359296 | tf_op jit(solution)/shard_map/middle/pallas_call | solution.py:72
  31.1 0.7 collective-permute-start.6
  31.8 1.9 %collective-permute-done.2.r_ref = bf16[256,768]{1,0:T(8,128)(2,1)S(1)} collective-permute-done((bf16[256,768]{1,0:T(8,128)(2,1)S(1)}, bf16[256,768]{1,0:T(8,128)(2,1)S(1)}, u32[]{:S(2)}, u32[]{:S(2)}) %collective-permute-start.2) | collective-permute-done | bytes 393248 | tf_op jit(solution)/shard_map/ppermute | solution.py:346
  33.7 0.1 join.1
  33.8 0.1 collective-permute-start.3
  33.8 9.3 %collective-permute-done.6.g_ref = bf16[256,768]{1,0:T(8,128)(2,1)S(1)} collective-permute-done((bf16[256,768]{1,0:T(8,128)(2,1)S(1)}, bf16[256,768]{1,0:T(8,128)(2,1)S(1)}, u32[]{:S(2)}, u32[]{:S(2)}) %collective-permute-start.6) | collective-permute-done | bytes 393248 | tf_op jit(solution)/shard_map/ppermute | solution.py:346
  43.2 3.4 %collective-permute-start.7 = (bf16[256,768]{1,0:T(8,128)(2,1)S(1)}, bf16[256,768]{1,0:T(8,128)(2,1)S(1)}, u32[]{:S(2)}, u32[]{:S(2)}) collective-permute-start(bf16[256,768]{1,0:T(8,128)(2,1)S(1)} %collective-permute-done.6.g_ref), channel_id=1, source_target_pairs={{0,4},{1,5},{4,8},{5,9},{6,2},{7,3},{8,12},{9,13},{10,6},{11,7},{1... | collective-permute-start | bytes 1179656 | tf_op jit(solution)/shard_map/ppermute | solution.py:346
  46.6 4.0 %collective-permute-done.3.refs_0_ = bf16[256,768]{1,0:T(8,128)(2,1)S(1)} collective-permute-done((bf16[256,768]{1,0:T(8,128)(2,1)S(1)}, bf16[256,768]{1,0:T(8,128)(2,1)S(1)}, u32[]{:S(2)}, u32[]{:S(2)}) %collective-permute-start.3) | collective-permute-done | bytes 393248 | tf_op jit(solution)/shard_map/ppermute | solution.py:346
  50.6 0.9 %middle.3 = (bf16[256,768]{1,0:T(8,128)(2,1)S(1)}, bf16[256,768]{1,0:T(8,128)(2,1)S(1)}) custom-call(bf16[256,768]{1,0:T(8,128)(2,1)S(1)} %collective-permute-done.3.refs_0_, f32[256,768]{1,0:T(8,128)S(1)} %get-tuple-element.22.refs_1_, f32[768]{0:T(1024)S(1)} %copy-done.9, f32[768]{0:T(1024)S(1)} %copy-done.10, f32[2,64,768]{2,1,0:T(8,128)S(1)} %hidden_grad.1.refs_5_.refs_4_), custom_call_target="tpu_custom_call" | custom-call | flops 5898240 | bytes 2359296 | tf_op jit(solution)/shard_map/middle/pallas_call | solution.py:72
  51.5 2.1 %collective-permute-start.4 = (bf16[256,768]{1,0:T(8,128)(2,1)S(1)}, bf16[256,768]{1,0:T(8,128)(2,1)S(1)}, u32[]{:S(2)}, u32[]{:S(2)}) collective-permute-start(bf16[256,768]{1,0:T(8,128)(2,1)S(1)} %get-tuple-element.24.g_ref), channel_id=1, source_target_pairs={{2,0},{3,1},{4,2},{5,3},{6,4},{7,5},{8,6},{9,7},{10,8},{11,9},{12,... | collective-permute-start | bytes 1179656 | tf_op jit(solution)/shard_map/ppermute | solution.py:336
  53.6 4.1 %collective-permute-start.5 = (bf16[256,768]{1,0:T(8,128)(2,1)S(1)}, bf16[256,768]{1,0:T(8,128)(2,1)S(1)}, u32[]{:S(2)}, u32[]{:S(2)}) collective-permute-start(bf16[256,768]{1,0:T(8,128)(2,1)S(1)} %get-tuple-element.24.g_ref), channel_id=1, source_target_pairs={{0,2},{1,3},{2,4},{3,5},{4,6},{5,7},{6,8},{7,9},{8,10},{9,11},{10,... | collective-permute-start | bytes 1179656 | tf_op jit(solution)/shard_map/ppermute | solution.py:336
  57.7 0.8 %back_first.3.c_ref = f32[256,1536]{1,0:T(8,128)S(1)} custom-call(bf16[256,768]{1,0:T(8,128)(2,1)S(1)} %get-tuple-element.25.g_ref, bf16[3,1536,768]{2,1,0:T(8,128)(2,1)S(1)} %bitcast.1), custom_call_target="tpu_custom_call" | custom-call | flops 603979776 | bytes 1572864 | tf_op jit(solution)/shard_map/back_first/pallas_call | solution.py:72
  58.5 1.4 %pooled.1 = bf16[2,64,1536]{2,1,0:T(8,128)(2,1)S(1)} custom-call(bf16[256,768]{1,0:T(8,128)(2,1)S(1)} %get-tuple-element.19.refs_0_, bf16[256,768]{1,0:T(8,128)(2,1)S(1)} %get-tuple-element.23.refs_1_, bf16[2,256,1536]{2,1,0:T(8,128)(2,1)S(1)} %copy-done.2, bf16[768,1536]{1,0:T(8,128)(2,1)S(1)} %copy-done.3, f32[1536]{0:T(1024)S(1)} %copy-done.11), custom_call_target="tpu_custom_call" | custom-call | flops 402653184 | bytes 1572864 | tf_op jit(solution)/shard_map/pooled/pallas_call | solution.py:72
  60.0 0.7 copy.13
  60.7 0.8 %back_first.2.refs_2_ = f32[256,1536]{1,0:T(8,128)S(1)} custom-call(bf16[256,768]{1,0:T(8,128)(2,1)S(1)} %get-tuple-element.24.g_ref, bf16[3,1536,768]{2,1,0:T(8,128)(2,1)S(1)} %bitcast.1), custom_call_target="tpu_custom_call" | custom-call | flops 603979776 | bytes 1572864 | tf_op jit(solution)/shard_map/back_first/pallas_call | solution.py:72
  61.6 0.8 %back_near.1.refs_1_ = f32[256,1536]{1,0:T(8,128)S(1)} custom-call(f32[256,1536]{1,0:T(8,128)S(1)} %back_first.3.c_ref, bf16[256,768]{1,0:T(8,128)(2,1)S(1)} %collective-permute-done.6.g_ref, bf16[3,1536,768]{2,1,0:T(8,128)(2,1)S(1)} %bitcast.1), custom_call_target="tpu_custom_call" | custom-call | flops 603979776 | bytes 3145728 | tf_op jit(solution)/shard_map/back_near/pallas_call | solution.py:72
  62.4 2.3 %final.2.refs_8_ = bf16[2,256,1536]{2,1,0:T(8,128)(2,1)} custom-call(bf16[256,768]{1,0:T(8,128)(2,1)S(1)} %collective-permute-done.7.refs_0_, f32[256,1536]{1,0:T(8,128)S(1)} %back_near.1.refs_1_, bf16[3,1536,768]{2,1,0:T(8,128)(2,1)S(1)} %bitcast.1, bf16[2,256,1536]{2,1,0:T(8,128)(2,1)S(1)} %copy-done.2, bf16[2,64,1536]{2,1,0:T(8,128)(2,1)S(1)} %copy-done.4, ...), custom_call_target="tpu_custom_call" | custom-call | flops 603979776 | bytes 3145728 | tf_op jit(solution)/shard_map/final/pallas_call | solution.py:301
  64.8 7.4 %collective-permute-done.4.refs_0_ = bf16[256,768]{1,0:T(8,128)(2,1)S(1)} collective-permute-done((bf16[256,768]{1,0:T(8,128)(2,1)S(1)}, bf16[256,768]{1,0:T(8,128)(2,1)S(1)}, u32[]{:S(2)}, u32[]{:S(2)}) %collective-permute-start.4) | collective-permute-done | bytes 393248 | tf_op jit(solution)/shard_map/ppermute | solution.py:336
  72.2 2.9 %final.3 = bf16[2,256,1536]{2,1,0:T(8,128)(2,1)} custom-call(bf16[256,768]{1,0:T(8,128)(2,1)S(1)} %collective-permute-done.4.refs_0_, bf16[256,768]{1,0:T(8,128)(2,1)S(1)} %collective-permute-done.5.refs_1_, f32[256,1536]{1,0:T(8,128)S(1)} %back_first.2.refs_2_, bf16[3,1536,768]{2,1,0:T(8,128)(2,1)S(1)} %bitcast.1, ...), custom_call_target="tpu_custom_call", output_to_operand_aliasing={{}: (8, {})} | custom-call | flops 1207959552 | bytes 3145728 | tf_op jit(solution)/shard_map/final/pallas_call | solution.py:301
  (27 shorter events, 0.1 us)
Async XLA Ops:
  0.6 3.0 %copy-start = (bf16[3,1536,768]{2,1,0:T(8,128)(2,1)S(1)}, bf16[3,1536,768]{2,1,0:T(8,128)(2,1)}, u32[]{:S(2)}) copy-start(bf16[3,1536,768]{2,1,0:T(8,128)(2,1)} %refs_3_.9) | copy-start | bytes 21233668
  3.6 1.4 %copy-start.1 = (bf16[2,256,1536]{2,1,0:T(8,128)(2,1)S(1)}, bf16[2,256,1536]{2,1,0:T(8,128)(2,1)}, u32[]{:S(2)}) copy-start(bf16[2,256,1536]{2,1,0:T(8,128)(2,1)} %refs_4_.7) | copy-start | bytes 4718596
  5.0 0.7 copy-start.5
  5.7 0.7 copy-start.7
  6.4 13.4 %slice-start = ((s8[7077888]{0:T(1024)(128)(4,1)}), s8[4194304]{0:T(1024)(128)(4,1)S(1)}, s32[]{:S(2)}) async-start(s8[7077888]{0:T(1024)(128)(4,1)} %bitcast), calls=%async_computation | async-start | bytes 8388608
  8.1 20.2 %collective-permute-start = (bf16[256,768]{1,0:T(8,128)(2,1)S(1)}, bf16[256,768]{1,0:T(8,128)(2,1)S(1)}, u32[]{:S(2)}, u32[]{:S(2)}) collective-permute-start(bf16[256,768]{1,0:T(8,128)(2,1)S(1)} %get-tuple-element.14), channel_id=1, source_target_pairs={{0,2},{1,3},{2,4},{3,5},{4,6},{5,7},{6,8},{7,9},{8,10},{9,11},{10,... | collective-permute-start | bytes 1179656 | tf_op jit(solution)/shard_map/ppermute | solution.py:336
  11.5 6.7 %copy-start.4 = (bf16[2,64,1536]{2,1,0:T(8,128)(2,1)S(1)}, bf16[2,64,1536]{2,1,0:T(8,128)(2,1)}, u32[]{:S(2)}) copy-start(bf16[2,64,1536]{2,1,0:T(8,128)(2,1)} %refs_5_.3) | copy-start | bytes 1179652
  11.5 8.3 %slice-start.1 = ((s8[7077888]{0:T(1024)(128)(4,1)}), s8[2883584]{0:T(1024)(128)(4,1)S(1)}, s32[]{:S(2)}) async-start(s8[7077888]{0:T(1024)(128)(4,1)} %bitcast), calls=%async_computation.1 | async-start | bytes 5767168
  11.5 18.7 %collective-permute-start.1 = (bf16[256,768]{1,0:T(8,128)(2,1)S(1)}, bf16[256,768]{1,0:T(8,128)(2,1)S(1)}, u32[]{:S(2)}, u32[]{:S(2)}) collective-permute-start(bf16[256,768]{1,0:T(8,128)(2,1)S(1)} %get-tuple-element.15), channel_id=1, source_target_pairs={{2,0},{3,1},{4,2},{5,3},{6,4},{7,5},{8,6},{9,7},{10,8},{11,9},{12,... | collective-permute-start | bytes 1179656 | tf_op jit(solution)/shard_map/ppermute | solution.py:336
  15.1 3.1 %copy-start.3 = (bf16[768,1536]{1,0:T(8,128)(2,1)S(1)}, bf16[768,1536]{1,0:T(8,128)(2,1)}, u32[]{:S(2)}) copy-start(bf16[768,1536]{1,0:T(8,128)(2,1)} %refs_3_.7) | copy-start | bytes 7077892
  16.3 17.4 %collective-permute-start.2 = (bf16[256,768]{1,0:T(8,128)(2,1)S(1)}, bf16[256,768]{1,0:T(8,128)(2,1)S(1)}, u32[]{:S(2)}, u32[]{:S(2)}) collective-permute-start(bf16[256,768]{1,0:T(8,128)(2,1)S(1)} %get-tuple-element.21), channel_id=1, source_target_pairs={{2,6},{3,7},{4,0},{5,1},{6,10},{7,11},{8,4},{9,5},{10,14},{11,15},... | collective-permute-start | bytes 1179656 | tf_op jit(solution)/shard_map/ppermute | solution.py:346
  19.8 10.4 %copy-start.9 = (f32[768]{0:T(1024)S(1)}, f32[768]{0:T(1024)}, u32[]{:S(2)}) copy-start(f32[768]{0:T(1024)} %refs_2_.3) | copy-start | bytes 9220
  19.8 10.3 %copy-start.10 = (f32[768]{0:T(1024)S(1)}, f32[768]{0:T(1024)}, u32[]{:S(2)}) copy-start(f32[768]{0:T(1024)} %refs_3_.6) | copy-start | bytes 9220
  31.1 12.0 %collective-permute-start.6 = (bf16[256,768]{1,0:T(8,128)(2,1)S(1)}, bf16[256,768]{1,0:T(8,128)(2,1)S(1)}, u32[]{:S(2)}, u32[]{:S(2)}) collective-permute-start(bf16[256,768]{1,0:T(8,128)(2,1)S(1)} %get-tuple-element.25.g_ref), channel_id=1, source_target_pairs={{0,2},{1,3},{2,0},{3,1},{4,6},{5,7},{6,4},{7,5},{8,10},{9,11},{10,... | collective-permute-start | bytes 1179656 | tf_op jit(solution)/shard_map/ppermute | solution.py:346
  33.8 16.9 %collective-permute-start.3 = (bf16[256,768]{1,0:T(8,128)(2,1)S(1)}, bf16[256,768]{1,0:T(8,128)(2,1)S(1)}, u32[]{:S(2)}, u32[]{:S(2)}) collective-permute-start(bf16[256,768]{1,0:T(8,128)(2,1)S(1)} %join.1), channel_id=1, source_target_pairs={{0,2},{1,3},{2,0},{3,1},{4,6},{5,7},{6,4},{7,5},{8,10},{9,11},{10,... | collective-permute-start | bytes 1179656 | tf_op jit(solution)/shard_map/ppermute | solution.py:346
  43.2 19.2 %collective-permute-start.7 = (bf16[256,768]{1,0:T(8,128)(2,1)S(1)}, bf16[256,768]{1,0:T(8,128)(2,1)S(1)}, u32[]{:S(2)}, u32[]{:S(2)}) collective-permute-start(bf16[256,768]{1,0:T(8,128)(2,1)S(1)} %collective-permute-done.6.g_ref), channel_id=1, source_target_pairs={{0,4},{1,5},{4,8},{5,9},{6,2},{7,3},{8,12},{9,13},{10,6},{11,7},{1... | collective-permute-start | bytes 1179656 | tf_op jit(solution)/shard_map/ppermute | solution.py:346
  51.5 7.0 %copy-start.2 = (bf16[2,256,1536]{2,1,0:T(8,128)(2,1)S(1)}, bf16[2,256,1536]{2,1,0:T(8,128)(2,1)}, u32[]{:S(2)}) copy-start(bf16[2,256,1536]{2,1,0:T(8,128)(2,1)} %refs_4_.7) | copy-start | bytes 4718596
  51.5 7.0 %copy-start.11 = (f32[1536]{0:T(1024)S(1)}, f32[1536]{0:T(1024)}, u32[]{:S(2)}) copy-start(f32[1536]{0:T(1024)} %refs_4_.5) | copy-start | bytes 18436
  51.5 20.6 %collective-permute-start.4 = (bf16[256,768]{1,0:T(8,128)(2,1)S(1)}, bf16[256,768]{1,0:T(8,128)(2,1)S(1)}, u32[]{:S(2)}, u32[]{:S(2)}) collective-permute-start(bf16[256,768]{1,0:T(8,128)(2,1)S(1)} %get-tuple-element.24.g_ref), channel_id=1, source_target_pairs={{2,0},{3,1},{4,2},{5,3},{6,4},{7,5},{8,6},{9,7},{10,8},{11,9},{12,... | collective-permute-start | bytes 1179656 | tf_op jit(solution)/shard_map/ppermute | solution.py:336
  53.6 18.6 %collective-permute-start.5 = (bf16[256,768]{1,0:T(8,128)(2,1)S(1)}, bf16[256,768]{1,0:T(8,128)(2,1)S(1)}, u32[]{:S(2)}, u32[]{:S(2)}) collective-permute-start(bf16[256,768]{1,0:T(8,128)(2,1)S(1)} %get-tuple-element.24.g_ref), channel_id=1, source_target_pairs={{0,2},{1,3},{2,4},{3,5},{4,6},{5,7},{6,8},{7,9},{8,10},{9,11},{10,... | collective-permute-start | bytes 1179656 | tf_op jit(solution)/shard_map/ppermute | solution.py:336
  61.5 0.9 %copy-start.6 = (f32[1536]{0:T(1024)S(1)}, f32[1536]{0:T(1024)}, u32[]{:S(2)}) copy-start(f32[1536]{0:T(1024)} %refs_6_.3) | copy-start | bytes 18436
  61.6 0.9 %copy-start.8 = (f32[1536]{0:T(1024)S(1)}, f32[1536]{0:T(1024)}, u32[]{:S(2)}) copy-start(f32[1536]{0:T(1024)} %refs_7_.1) | copy-start | bytes 18436

commit v2 on v1

v2 whole, which is shorter than its diff:
```python
import functools

import jax
import jax.numpy as jnp
from jax import lax
from jax.experimental import pallas as pl
from jax.experimental.pallas import tpu as pltpu
from jax.sharding import PartitionSpec as P

DILATION_STEP = 512
BIN = 4
LANES = 128
AXIS = "seq"
GELU_COEF = 0.7978845608028654
F32 = jnp.float32
BF16 = jnp.bfloat16
SHARE = 64
LIMIT = 12 * 1024 * 1024


def gelu_value(v):
    inner = jnp.tanh(v * (GELU_COEF + (GELU_COEF * 0.044715) * v * v))
    half = 0.5 * v
    return half + half * inner


def gelu_both(v):
    square = v * v
    inner = jnp.tanh(v * (GELU_COEF + (GELU_COEF * 0.044715) * square))
    half = 0.5 * v
    value = half + half * inner
    slope = (0.5 + 0.5 * inner) + half * (1.0 - inner * inner) * (
        GELU_COEF + (GELU_COEF * 0.134145) * square
    )
    return value, slope


def gelu_slope(v):
    return gelu_both(v)[1]


def dot_nn(a, b):
    return jnp.dot(a, b, preferred_element_type=F32)


def dot_nt(a, b):
    return lax.dot_general(a, b, (((1,), (1,)), ((), ())), preferred_element_type=F32)


def averaging(bins, rows):
    row = lax.broadcasted_iota(jnp.int32, (bins, rows), 0)
    column = lax.broadcasted_iota(jnp.int32, (bins, rows), 1)
    inside = (column >= row * BIN) & (column < row * BIN + BIN)
    return jnp.where(inside, 1.0 / BIN, 0.0).astype(BF16)


def spreading(rows, bins):
    row = lax.broadcasted_iota(jnp.int32, (rows, bins), 0)
    column = lax.broadcasted_iota(jnp.int32, (rows, bins), 1)
    inside = (row >= column * BIN) & (row < column * BIN + BIN)
    return jnp.where(inside, 1.0 / BIN, 0.0).astype(BF16)


def near_tap(stride):
    return 2 * lax.rem(lax.div(lax.axis_index(AXIS), stride), 2)


def cost_of(flops, nbytes, trans):
    return pl.CostEstimate(
        flops=flops // SHARE, bytes_accessed=nbytes // SHARE, transcendentals=trans // SHARE
    )


def local_call(body, name, operands, outs, cost, scratch=(), after=()):
    flops, nbytes, trans = cost
    single = not isinstance(outs, list)
    space = pl.BlockSpec(memory_space=pltpu.VMEM)
    if after:
        inner, skip = body, len(operands)
        body = lambda *refs: inner(*refs[:skip], *refs[skip + len(after) :])
        operands = [*operands, *after]
    shapes = [pltpu.VMEM(s, d) for s, d in ([outs] if single else outs)]
    return pl.pallas_call(
        body,
        name=name,
        in_specs=[space] * len(operands),
        out_specs=space if single else [space] * len(outs),
        out_shape=shapes[0] if single else shapes,
        scratch_shapes=list(scratch),
        compiler_params=pltpu.CompilerParams(vmem_limit_bytes=LIMIT),
        cost_estimate=cost_of(flops, nbytes, trans),
    )(*[pltpu.with_memory_space_constraint(v, pltpu.VMEM) for v in operands])

SPLITS = (256, 256, 256)


def bounds(n):
    return slice(sum(SPLITS[:n]), sum(SPLITS[: n + 1]))


def front_body(stride, x_hbm, s_hbm, b_hbm, w_hbm, x_ref, w_ref, a_ref, p_ref, s_ref, b_ref, sems):
    rows, width = x_ref.shape
    slabs = 4
    slab = rows // slabs
    copies = [
        pltpu.make_async_copy(s_hbm, s_ref, sems.at[0]),
        pltpu.make_async_copy(b_hbm, b_ref, sems.at[1]),
    ]
    copies += [
        pltpu.make_async_copy(
            x_hbm.at[pl.ds(n * slab, slab)], x_ref.at[pl.ds(n * slab, slab)], sems.at[2 + n]
        )
        for n in range(slabs)
    ]
    taps = pltpu.make_async_copy(w_hbm.at[2 - near_tap(stride)], w_ref, sems.at[2 + slabs])
    for copy in copies:
        copy.start()
    taps.start()
    copies[0].wait()
    copies[1].wait()
    scale = s_ref[...].reshape(1, width)
    shift = b_ref[...].reshape(1, width)
    for n, copy in enumerate(copies[2:]):
        copy.wait()
        part = slice(n * slab, n * slab + slab)
        a_ref[part, :] = gelu_value(x_ref[part, :].astype(F32) * scale + shift).astype(BF16)
    taps.wait()
    p_ref[...] = dot_nn(a_ref[...], w_ref[:, bounds(0)]).astype(BF16)


def front(x, scale, shift, taps, stride):
    rows, width = x.shape
    mid = SPLITS[0]
    space = pl.BlockSpec(memory_space=pltpu.VMEM)
    far = pl.BlockSpec(memory_space=pltpu.HBM)
    operands = [pltpu.with_memory_space_constraint(v, pltpu.HBM) for v in (x, scale, shift, taps)]
    return pl.pallas_call(
        functools.partial(front_body, stride),
        name="front",
        in_specs=[far] * 4,
        out_specs=[space] * 4,
        out_shape=[
            pltpu.VMEM(x.shape, BF16),
            pltpu.VMEM(taps.shape[1:], BF16),
            pltpu.VMEM((rows, width), BF16),
            pltpu.VMEM((rows, mid), BF16),
        ],
        scratch_shapes=[
            pltpu.VMEM((width,), F32),
            pltpu.VMEM((width,), F32),
            pltpu.SemaphoreType.DMA((7,)),
        ],
        compiler_params=pltpu.CompilerParams(vmem_limit_bytes=LIMIT),
        cost_estimate=cost_of(2 * rows * width * mid, 2 * (x.size + taps.size), x.size),
    )(*operands)


def side_body(which, a_ref, w_ref, o_ref):
    o_ref[...] = dot_nn(a_ref[...], w_ref[:, bounds(which)]).astype(BF16)


def side(act, far_tap, which, after=()):
    rows, width = act.shape
    return local_call(
        functools.partial(side_body, which),
        "side",
        [act, far_tap],
        ((rows, SPLITS[which]), BF16),
        (2 * rows * width * SPLITS[which], 2 * rows * width, 0),
        after=after,
    )


def keep_body(stride, which, a_ref, w_ref, *outs):
    for n, out in zip(which, outs):
        out[...] = dot_nn(a_ref[...], w_ref[near_tap(stride), :, bounds(n)])


def keep(act, taps, which, stride, after=()):
    rows, width = act.shape
    return local_call(
        functools.partial(keep_body, stride, which),
        "keep",
        [act, taps],
        [((rows, SPLITS[n]), F32) for n in which],
        (2 * rows * width * sum(SPLITS[n] for n in which), 2 * rows * width, 0),
        after=after,
    )


def centre_body(a_ref, w_ref, *outs):
    for n, out in enumerate(outs):
        out[...] = dot_nn(a_ref[...], w_ref[1, :, bounds(n)])


def centre(act, taps, after):
    rows, width = act.shape
    return local_call(
        centre_body,
        "centre",
        [act, taps],
        [((rows, c), F32) for c in SPLITS],
        (2 * rows * width * sum(SPLITS), 2 * rows * width, 0),
        after=after,
    )


def join_body(k_ref, r_ref, o_ref):
    o_ref[...] = (k_ref[...] + r_ref[...].astype(F32)).astype(BF16)


def join(kept, came, after=()):
    return local_call(
        join_body,
        "join",
        [kept, came],
        (kept.shape, BF16),
        (kept.size, 8 * kept.size, 0),
        after=after,
    )


def hidden_grad_body(g_ref, w_ref, *outs):
    grad = (g_ref[...].astype(F32) * (1.0 / BIN)).astype(BF16)
    for n, out in enumerate(outs):
        out[...] = dot_nt(grad, w_ref[bounds(n), :])


def hidden_grad(binned, weight, after):
    bins, width = binned.shape
    mid = weight.shape[0]
    return local_call(
        hidden_grad_body,
        "hidden_grad",
        [binned, weight],
        [((bins, c), F32) for c in SPLITS],
        (2 * bins * width * mid, 2 * bins * width, 0),
        after=after,
    )


def middle_body(which, t_ref, p_ref, s_ref, b_ref, hg_ref, g_ref, h_ref, wide_ref):
    bins, width = hg_ref.shape
    for lane in range(width // LANES):
        columns = slice(lane * LANES, lane * LANES + LANES)
        for k in range(BIN):
            wide_ref[lane, pl.ds(k, bins, stride=BIN), :] = hg_ref[:, columns]
    first = bounds(which).start
    scales = s_ref[...].reshape(1, s_ref.shape[0])
    shifts = b_ref[...].reshape(1, b_ref.shape[0])
    for lane in range(width // LANES):
        columns = slice(lane * LANES, lane * LANES + LANES)
        among = slice(first + lane * LANES, first + lane * LANES + LANES)
        mid = p_ref[:, columns] + t_ref[:, columns].astype(F32)
        scale = scales[:, among]
        value, slope = gelu_both(mid * scale + shifts[:, among])
        g_ref[:, columns] = (wide_ref[lane] * slope * scale).astype(BF16)
        h_ref[:, columns] = value.astype(BF16)


def middle(part, centre_part, which, scale, shift, hidden_grads, after=()):
    rows, mid = centre_part.shape
    return local_call(
        functools.partial(middle_body, which),
        "middle",
        [part, centre_part, scale, shift, hidden_grads],
        [((rows, mid), BF16), ((rows, mid), BF16)],
        (30 * rows * mid, 12 * rows * mid, rows * mid),
        scratch=[pltpu.VMEM((mid // LANES, rows, LANES), F32)],
        after=after,
    )


def pooled_base_body(x_ref, b_ref, o_ref):
    bins, width = o_ref.shape
    average = averaging(bins, x_ref.shape[0])
    o_ref[...] = dot_nn(average, x_ref[...]) + b_ref[...].reshape(1, width)


def pooled_base(x, bias, after):
    rows, width = x.shape
    bins = rows // BIN
    return local_call(
        pooled_base_body,
        "pooled_base",
        [x, bias],
        ((bins, width), F32),
        (2 * bins * width * rows, 2 * rows * width, 0),
        after=after,
    )


def pooled_body(*refs):
    count = len(SPLITS)
    hidden = refs[:count]
    base_ref, w_ref, o_ref, out_ref, sem = refs[count:]
    bins, width = out_ref.shape
    rows = hidden[0].shape[0]
    average = averaging(bins, rows)
    total = base_ref[...]
    for n in range(count):
        mean = dot_nn(average, hidden[n][...]).astype(BF16)
        total = total + dot_nn(mean, w_ref[bounds(n), :])
    out_ref[...] = total.astype(BF16)
    half = bins // o_ref.shape[0]
    for n in range(o_ref.shape[0]):
        copy = pltpu.make_async_copy(out_ref.at[pl.ds(n * half, half)], o_ref.at[n], sem.at[n])
        copy.start()
    for n in range(o_ref.shape[0]):
        copy = pltpu.make_async_copy(out_ref.at[pl.ds(n * half, half)], o_ref.at[n], sem.at[n])
        copy.wait()


def pooled_out(base, hidden, weight, batch):
    bins, width = base.shape
    mid = weight.shape[0]
    operands = [*hidden, base, weight]
    return pl.pallas_call(
        pooled_body,
        name="pooled",
        in_specs=[pl.BlockSpec(memory_space=pltpu.VMEM)] * len(operands),
        out_specs=pl.BlockSpec(memory_space=pltpu.HBM),
        out_shape=pltpu.HBM((batch, bins // batch, width), BF16),
        scratch_shapes=[pltpu.VMEM((bins, width), BF16), pltpu.SemaphoreType.DMA((batch,))],
        compiler_params=pltpu.CompilerParams(vmem_limit_bytes=LIMIT),
        cost_estimate=cost_of(2 * bins * width * mid, 6 * bins * width, 0),
    )(*[pltpu.with_memory_space_constraint(v, pltpu.VMEM) for v in operands])


def slope_body(x_ref, s_ref, b_ref, o_ref):
    width = x_ref.shape[1]
    scale = s_ref[...].reshape(1, width)
    shift = b_ref[...].reshape(1, width)
    o_ref[...] = gelu_slope(x_ref[...].astype(F32) * scale + shift) * scale


def slope_in(x, scale, shift, after):
    return local_call(
        slope_body,
        "slope",
        [x, scale, shift],
        (x.shape, F32),
        (30 * x.size, 6 * x.size, x.size),
        after=after,
    )


def back_sum(stride, refs, kinds, w_ref, columns=slice(None)):
    near = near_tap(stride)
    taps = dict(own=1, near=near, far=2 - near, before=2, later=0)
    total = None
    for ref, (kind, n) in zip(refs, kinds):
        term = dot_nt(ref[...], w_ref[taps[kind], columns, bounds(n)])
        total = term if total is None else total + term
    return total


def back_body(stride, kinds, started, *refs):
    grads = refs[: len(kinds)]
    rest = refs[len(kinds) :]
    w_ref, o_ref = rest[0], rest[-1]
    total = back_sum(stride, grads, kinds, w_ref)
    o_ref[...] = rest[1][...] + total if started else total


def back(total, terms, taps, stride, after=()):
    kinds = [(kind, n) for kind, n, _ in terms]
    grads = [g for _, _, g in terms]
    rows = grads[0].shape[0]
    width = taps.shape[1]
    started = total is not None
    return local_call(
        functools.partial(back_body, stride, kinds, started),
        "back",
        [*grads, taps] + ([total] if started else []),
        ((rows, width), F32),
        (2 * rows * width * sum(g.shape[1] for g in grads), 8 * rows * width, 0),
        after=after,
    )


def touch_body(a_ref, b_ref, o_ref):
    o_ref[...] = a_ref[:16, :LANES] + b_ref[:16, :LANES]


def touch(a, b):
    return local_call(touch_body, "touch", [a, b], ((16, LANES), BF16), (1, 1, 0))


def final_body(stride, kinds, tiles, *refs):
    grads = refs[: len(kinds)]
    c_ref, w_ref, d_ref, og_ref, _, o_ref, out_ref, sems = refs[len(kinds) :]
    rows, width = c_ref.shape
    tile = width // tiles
    spread = spreading(rows, og_ref.shape[0])
    copies = []
    for n in range(tiles):
        columns = slice(n * tile, n * tile + tile)
        total = c_ref[:, columns] + back_sum(stride, grads, kinds, w_ref, columns)
        out_ref[:, columns] = (
            dot_nn(spread, og_ref[:, columns]) + total * d_ref[:, columns]
        ).astype(BF16)
        copy = pltpu.make_async_copy(out_ref.at[:, columns], o_ref.at[:, columns], sems.at[n])
        copy.start()
        copies.append(copy)
    for copy in copies:
        copy.wait()


def final(total, terms, taps, slope, binned, stride, after):
    kinds = [(kind, n) for kind, n, _ in terms]
    grads = [g for _, _, g in terms]
    rows, width = slope.shape
    tiles = 3
    operands = [*grads, total, taps, slope, binned, *after]
    return pl.pallas_call(
        functools.partial(final_body, stride, kinds, tiles),
        name="final",
        in_specs=[pl.BlockSpec(memory_space=pltpu.VMEM)] * len(operands),
        out_specs=pl.BlockSpec(memory_space=pltpu.HBM),
        out_shape=pltpu.HBM((rows, width), BF16),
        scratch_shapes=[pltpu.VMEM((rows, width), BF16), pltpu.SemaphoreType.DMA((tiles,))],
        compiler_params=pltpu.CompilerParams(vmem_limit_bytes=LIMIT),
        cost_estimate=cost_of(
            2 * rows * width * sum(g.shape[1] for g in grads), 8 * rows * width, 0
        ),
    )(*[pltpu.with_memory_space_constraint(v, pltpu.VMEM) for v in operands])


def local(
    seqs_in,
    pooled_grad,
    scale_in,
    shift_in,
    tap_weight_stack,
    scale_mid,
    shift_mid,
    out_weight,
    out_bias,
):
    batch, rows, width = seqs_in.shape
    count = lax.axis_size(AXIS)
    stride = DILATION_STEP // rows
    blocks = count // stride

    def hop(value, steps):
        return lax.ppermute(
            value, AXIS, [(i, i + steps) for i in range(count) if 0 <= i + steps < count]
        )

    def block_permute(value, move):
        pairs = []
        for b in range(blocks):
            to = move(b)
            if 0 <= to < blocks:
                pairs += [(b * stride + i, to * stride + i) for i in range(stride)]
        return lax.ppermute(value, AXIS, pairs)

    def swap(value):
        return block_permute(value, lambda b: b ^ 1)

    def inward(value):
        return block_permute(value, lambda b: b + 2 if b % 2 else b - 2)

    def outward(value):
        return block_permute(value, lambda b: b - 2 if b % 2 else b + 2)

    flat = seqs_in.reshape(batch * rows, width)
    binned = pooled_grad.reshape(-1, width)
    x, far_tap, act, sent0 = front(flat, scale_in, shift_in, tap_weight_stack, stride)
    taps = lax.optimization_barrier((tap_weight_stack, sent0))[0]
    came0 = inward(sent0)
    def later_than(value, *others):
        return lax.optimization_barrier((value, *others))[0]

    sent1 = side(act, far_tap, 1)
    came1 = inward(sent1)
    kept0, kept1, kept2 = keep(act, taps, [0, 1, 2], stride, [sent1])
    own = centre(act, taps, [kept0])
    joined0 = join(kept0, came0, [own[0]])
    mids0 = swap(joined0)
    sent2 = side(act, far_tap, 2, [joined0])
    came2 = inward(sent2)
    joined1 = join(kept1, came1, [sent2])
    mids1 = swap(joined1)
    hg = hidden_grad(binned, out_weight, [joined1])
    grad0, hid0 = middle(mids0, own[0], 0, scale_mid, shift_mid, hg[0])
    near0 = swap(grad0)
    joined2 = join(kept2, came2, [grad0])
    mids2 = swap(joined2)
    slope = slope_in(x, scale_in, shift_in, [joined2])
    grad1, hid1 = middle(mids1, own[1], 1, scale_mid, shift_mid, hg[1], [slope])
    near1 = swap(grad1)
    base = pooled_base(x, out_bias, [grad1])
    total = back(None, [("own", 0, grad0), ("own", 1, grad1)], taps, stride, [base])
    near0 = later_than(near0, total)
    far0 = outward(near0)
    total = back(total, [("near", 0, near0)], taps, stride)
    grad2, hid2 = middle(mids2, own[2], 2, scale_mid, shift_mid, hg[2], [total])
    before2 = hop(grad2, stride)
    later2 = hop(grad2, -stride)
    near1 = later_than(near1, grad2)
    far1 = outward(near1)
    pooled = pooled_out(base, [hid0, hid1, hid2], out_weight, batch)
    total = back(
        total, [("own", 2, grad2), ("near", 1, near1), ("far", 0, far0)], taps, stride, [hid2]
    )
    arrived = touch(later2, before2)
    out = final(
        total,
        [("later", 2, later2), ("before", 2, before2), ("far", 1, far1)],
        taps,
        slope,
        binned,
        stride,
        [arrived],
    )
    return pooled, out.reshape(seqs_in.shape)


def solution(mesh):
    in_specs = (
        P("groups", "seq", None),
        P("groups", "seq", None),
        P(),
        P(),
        P(),
        P(),
        P(),
        P(),
        P(),
    )
    out_specs = (P("groups", "seq", None), P("groups", "seq", None))
    return jax.shard_map(local, mesh=mesh, in_specs=in_specs, out_specs=out_specs, check_vma=False)
```

time: 75.6 us -> 63.7 us (0.84)
  waiting for transfers between devices: 31 us -> 13 us
  starting transfers between devices: 19.2 us -> 28.6 us
  local copies, waits for them, and re-layouts: 6.61 us -> 0.05 us
  Pallas kernels: 17.3 us -> 20.2 us
    ppermute x4 -> x10, starting transfers between devices: 6.08 us -> 21.8 us  [block_permute(): return lax.ppermute(value, AXIS, pairs)]
    ppermute x4 -> x2, waiting for transfers between devices: 15.7 us -> 0.01 us  [hop(): lax.ppermute(value, AXIS, [(i, i + steps) for i in range(count) if 0 <= i...]
    unnamed x29 -> x18, local copies, waits for them, and re-layouts: 6.61 us -> 0.05 us
    ppermute x4 -> x2, starting transfers between devices: 13.2 us -> 6.74 us  [hop(): lax.ppermute(value, AXIS, [(i, i + steps) for i in range(count) if 0 <= i...]
    pallas_call x2 -> x3, Pallas kernels: 5.24 us -> 7.63 us  [the longest x1 3.02 us: front(): pl.pallas_call(functools.partial(front_body, stride), name='front', in_sp...]
    ppermute x4 -> x10, waiting for transfers between devices: 15.3 us -> 13 us  [block_permute(): return lax.ppermute(value, AXIS, pairs)]
    pallas_call x11 -> x17, Pallas kernels: 12 us -> 12.5 us  [local_call(): pl.pallas_call(body, name=name, in_specs=[space] * len(operands), out_spe...]
  transfers between devices with their start and end apart: 8 -> 12, of which waited for: 6 -> 8; matrix products, arithmetic and copies ran while one was open for 1% -> 0% of each run, Pallas kernels for 17% -> 23%
where the time goes in v2:
time: 63.7 us; the launch traced here: 62.9 us
  starting transfers between devices  28.6 us (45%)
  Pallas kernels  20.2 us (32%)
  waiting for transfers between devices  13 us (20%)
  between operations  1.1 us (2%)
    ppermute x10, starting transfers between devices, block_permute(): return lax.ppermute(value, AXIS, pairs)  21.8 us
    ppermute x10, waiting for transfers between devices, block_permute(): return lax.ppermute(value, AXIS, pairs)  13 us
    pallas_call x17, Pallas kernels, local_call(): pl.pallas_call(body, name=name, in_specs=[space] * len(operands), out_spe...  12.5 us
    ppermute x2, starting transfers between devices, hop(): lax.ppermute(value, AXIS, [(i, i + steps) for i in range(count) if 0 <= i...  6.74 us
    pallas_call x1, Pallas kernels, front(): pl.pallas_call(functools.partial(front_body, stride), name='front', in_sp...  3.02 us
    pallas_call x1, Pallas kernels, final(): pl.pallas_call(functools.partial(final_body, stride, kinds, tiles), name=...  2.87 us
    pallas_call x1, Pallas kernels, pooled_out(): pl.pallas_call(pooled_body, name='pooled', in_specs=[pl.BlockSpec(memory_...  1.73 us
  transfers between devices with their start and end apart: 12, of which 8 were waited for; matrix products, arithmetic and copies ran while one was open for 0% of the time, Pallas kernels for 23%

profile of v2, /device:TPU:8, one launch (start us, length us, event | category | flops | bytes accessed | tf_op | source)
XLA Modules:
  0.0 62.9 jit_solution(11355571293730665133)
XLA Ops:
  0.7 3.0 %front.1 = (bf16[512,1536]{1,0:T(8,128)(2,1)S(1)}, bf16[1536,768]{1,0:T(8,128)(2,1)S(1)}, bf16[512,1536]{1,0:T(8,128)(2,1)S(1)}, bf16[512,256]{1,0:T(8,128)(2,1)S(1)}) custom-call(bf16[512,1536]{1,0:T(8,128)(2,1)} %bitcast.8, f32[1536]{0:T(1024)} %refs_1_.6, f32[1536]{0:T(1024)} %refs_2_.3, bf16[3,1536,768]{2,1,0:T(8,128)(2,1)} %refs_4_.2), custom_call_target="tpu_custom_call" | custom-call | flops 6291456 | bytes 135168 | tf_op jit(solution)/shard_map/front/pallas_call | solution.py:137
  3.7 2.1 %collective-permute-start = (bf16[512,256]{1,0:T(8,128)(2,1)S(1)}, bf16[512,256]{1,0:T(8,128)(2,1)S(1)}, u32[]{:S(2)}, u32[]{:S(2)}) collective-permute-start(bf16[512,256]{1,0:T(8,128)(2,1)S(1)} %get-tuple-element.25), channel_id=1, source_target_pairs={{2,6},{3,7},{4,0},{5,1},{6,10},{7,11},{8,4},{9,5},{10,14},{11,15},... | collective-permute-start | bytes 786440 | tf_op jit(solution)/shard_map/ppermute | solution.py:457
  5.7 0.6 side.2.refs_2_
  6.3 1.9 %collective-permute-start.2 = (bf16[512,256]{1,0:T(8,128)(2,1)S(1)}, bf16[512,256]{1,0:T(8,128)(2,1)S(1)}, u32[]{:S(2)}, u32[]{:S(2)}) collective-permute-start(bf16[512,256]{1,0:T(8,128)(2,1)S(1)} %side.2.refs_2_), channel_id=1, source_target_pairs={{2,6},{3,7},{4,0},{5,1},{6,10},{7,11},{8,4},{9,5},{10,14},{11,15},... | collective-permute-start | bytes 786440 | tf_op jit(solution)/shard_map/ppermute | solution.py:457
  8.3 1.4 %keep.1 = (f32[512,256]{1,0:T(8,128)S(1)}, f32[512,256]{1,0:T(8,128)S(1)}, f32[512,256]{1,0:T(8,128)S(1)}) custom-call(bf16[512,1536]{1,0:T(8,128)(2,1)S(1)} %get-tuple-element.24.a_ref.refs_0_, bf16[3,1536,768]{2,1,0:T(8,128)(2,1)S(1)} %bitcast.4, bf16[512,256]{1,0:T(8,128)(2,1)S(1)} %side.2.refs_2_), custom_call_target="tpu_custom_call" | custom-call | flops 18874368 | bytes 24576 | tf_op jit(solution)/shard_map/keep/pallas_call | solution.py:83
  9.7 1.4 %centre.1 = (f32[512,256]{1,0:T(8,128)S(1)}, f32[512,256]{1,0:T(8,128)S(1)}, f32[512,256]{1,0:T(8,128)S(1)}) custom-call(bf16[512,1536]{1,0:T(8,128)(2,1)S(1)} %get-tuple-element.24.a_ref.refs_0_, bf16[3,1536,768]{2,1,0:T(8,128)(2,1)S(1)} %bitcast.4, f32[512,256]{1,0:T(8,128)S(1)} %get-tuple-element.28.refs_2_.refs_0_), custom_call_target="tpu_custom_call" | custom-call | flops 18874368 | bytes 24576 | tf_op jit(solution)/shard_map/centre/pallas_call | solution.py:83
  11.1 3.8 %collective-permute-done.refs_1_ = bf16[512,256]{1,0:T(8,128)(2,1)S(1)} collective-permute-done((bf16[512,256]{1,0:T(8,128)(2,1)S(1)}, bf16[512,256]{1,0:T(8,128)(2,1)S(1)}, u32[]{:S(2)}, u32[]{:S(2)}) %collective-permute-start) | collective-permute-done | bytes 262176 | tf_op jit(solution)/shard_map/ppermute | solution.py:457
  15.0 1.6 %collective-permute-start.1 = (bf16[512,256]{1,0:T(8,128)(2,1)S(1)}, bf16[512,256]{1,0:T(8,128)(2,1)S(1)}, u32[]{:S(2)}, u32[]{:S(2)}) collective-permute-start(bf16[512,256]{1,0:T(8,128)(2,1)S(1)} %join.3.refs_2_), channel_id=1, source_target_pairs={{0,2},{1,3},{2,0},{3,1},{4,6},{5,7},{6,4},{7,5},{8,10},{9,11},{10,... | collective-permute-start | bytes 786440 | tf_op jit(solution)/shard_map/ppermute | solution.py:457
  16.6 0.6 side.3.refs_2_
  17.2 1.9 %collective-permute-start.4 = (bf16[512,256]{1,0:T(8,128)(2,1)S(1)}, bf16[512,256]{1,0:T(8,128)(2,1)S(1)}, u32[]{:S(2)}, u32[]{:S(2)}) collective-permute-start(bf16[512,256]{1,0:T(8,128)(2,1)S(1)} %side.3.refs_2_), channel_id=1, source_target_pairs={{2,6},{3,7},{4,0},{5,1},{6,10},{7,11},{8,4},{9,5},{10,14},{11,15},... | collective-permute-start | bytes 786440 | tf_op jit(solution)/shard_map/ppermute | solution.py:457
  19.4 2.0 %collective-permute-start.3 = (bf16[512,256]{1,0:T(8,128)(2,1)S(1)}, bf16[512,256]{1,0:T(8,128)(2,1)S(1)}, u32[]{:S(2)}, u32[]{:S(2)}) collective-permute-start(bf16[512,256]{1,0:T(8,128)(2,1)S(1)} %join.4.refs_2_), channel_id=1, source_target_pairs={{0,2},{1,3},{2,0},{3,1},{4,6},{5,7},{6,4},{7,5},{8,10},{9,11},{10,... | collective-permute-start | bytes 786440 | tf_op jit(solution)/shard_map/ppermute | solution.py:457
  21.5 0.9 %hidden_grad.1 = (f32[128,256]{1,0:T(8,128)S(1)}, f32[128,256]{1,0:T(8,128)S(1)}, f32[128,256]{1,0:T(8,128)S(1)}) custom-call(bf16[128,1536]{1,0:T(8,128)(2,1)S(1)} %bitcast.5, bf16[768,1536]{1,0:T(8,128)(2,1)S(1)} %copy-done, bf16[512,256]{1,0:T(8,128)(2,1)S(1)} %join.4.refs_2_), custom_call_target="tpu_custom_call" | custom-call | flops 4718592 | bytes 6144 | tf_op jit(solution)/shard_map/hidden_grad/pallas_call | solution.py:83
  22.4 0.7 %middle.3 = (bf16[512,256]{1,0:T(8,128)(2,1)S(1)}, bf16[512,256]{1,0:T(8,128)(2,1)S(1)}) custom-call(bf16[512,256]{1,0:T(8,128)(2,1)S(1)} %collective-permute-done.1.t_ref, f32[512,256]{1,0:T(8,128)S(1)} %get-tuple-element.29.refs_2_.p_ref, f32[768]{0:T(1024)S(1)} %copy-done.2, f32[768]{0:T(1024)S(1)} %copy-done.3, f32[128,256]{1,0:T(8,128)S(1)} %get-tuple-element.31.hg_ref), custom_call_target="tpu_custom_call" | custom-call | flops 61440 | bytes 24576 | tf_op jit(solution)/shard_map/middle/pallas_call | solution.py:83
  23.1 1.8 %collective-permute-start.6 = (bf16[512,256]{1,0:T(8,128)(2,1)S(1)}, bf16[512,256]{1,0:T(8,128)(2,1)S(1)}, u32[]{:S(2)}, u32[]{:S(2)}) collective-permute-start(bf16[512,256]{1,0:T(8,128)(2,1)S(1)} %get-tuple-element.37.refs_2_.refs_0_), channel_id=1, source_target_pairs={{0,2},{1,3},{2,0},{3,1},{4,6},{5,7},{6,4},{7,5},{8,10},{9,11},{10,... | collective-permute-start | bytes 786440 | tf_op jit(solution)/shard_map/ppermute | solution.py:457
  24.9 0.7 %collective-permute-done.4.refs_1_ = bf16[512,256]{1,0:T(8,128)(2,1)S(1)} collective-permute-done((bf16[512,256]{1,0:T(8,128)(2,1)S(1)}, bf16[512,256]{1,0:T(8,128)(2,1)S(1)}, u32[]{:S(2)}, u32[]{:S(2)}) %collective-permute-start.4) | collective-permute-done | bytes 262176 | tf_op jit(solution)/shard_map/ppermute | solution.py:457
  25.6 1.0 %collective-permute-start.5 = (bf16[512,256]{1,0:T(8,128)(2,1)S(1)}, bf16[512,256]{1,0:T(8,128)(2,1)S(1)}, u32[]{:S(2)}, u32[]{:S(2)}) collective-permute-start(bf16[512,256]{1,0:T(8,128)(2,1)S(1)} %join.5.refs_3_), channel_id=1, source_target_pairs={{0,2},{1,3},{2,0},{3,1},{4,6},{5,7},{6,4},{7,5},{8,10},{9,11},{10,... | collective-permute-start | bytes 786440 | tf_op jit(solution)/shard_map/ppermute | solution.py:457
  26.6 1.9 %slope.1.refs_5_ = f32[512,1536]{1,0:T(8,128)S(1)} custom-call(bf16[512,1536]{1,0:T(8,128)(2,1)S(1)} %get-tuple-element.35.refs_0_, f32[1536]{0:T(1024)S(1)} %copy-done.4, f32[1536]{0:T(1024)S(1)} %copy-done.5, bf16[512,256]{1,0:T(8,128)(2,1)S(1)} %join.5.refs_3_), custom_call_target="tpu_custom_call" | custom-call | flops 368640 | bytes 73728 | tf_op jit(solution)/shard_map/slope/pallas_call | solution.py:83
  28.7 0.7 %middle.4 = (bf16[512,256]{1,0:T(8,128)(2,1)S(1)}, bf16[512,256]{1,0:T(8,128)(2,1)S(1)}) custom-call(bf16[512,256]{1,0:T(8,128)(2,1)S(1)} %collective-permute-done.3.refs_0_, f32[512,256]{1,0:T(8,128)S(1)} %get-tuple-element.33.refs_1_, f32[768]{0:T(1024)S(1)} %copy-done.2, f32[768]{0:T(1024)S(1)} %copy-done.3, f32[128,256]{1,0:T(8,128)S(1)} %get-tuple-element.34.refs_4_, ...), custom_call_target="tpu_custom_call" | custom-call | flops 61440 | bytes 24576 | tf_op jit(solution)/shard_map/middle/pallas_call | solution.py:83
  29.4 2.0 %collective-permute-start.9 = (bf16[512,256]{1,0:T(8,128)(2,1)S(1)}, bf16[512,256]{1,0:T(8,128)(2,1)S(1)}, u32[]{:S(2)}, u32[]{:S(2)}) collective-permute-start(bf16[512,256]{1,0:T(8,128)(2,1)S(1)} %get-tuple-element.41.refs_2_.refs_1_), channel_id=1, source_target_pairs={{0,2},{1,3},{2,0},{3,1},{4,6},{5,7},{6,4},{7,5},{8,10},{9,11},{10,... | collective-permute-start | bytes 786440 | tf_op jit(solution)/shard_map/ppermute | solution.py:457
  31.8 1.0 %back.3.refs_2_ = f32[512,1536]{1,0:T(8,128)S(1)} custom-call(bf16[512,256]{1,0:T(8,128)(2,1)S(1)} %get-tuple-element.37.refs_2_.refs_0_, bf16[512,256]{1,0:T(8,128)(2,1)S(1)} %get-tuple-element.41.refs_2_.refs_1_, bf16[3,1536,768]{2,1,0:T(8,128)(2,1)S(1)} %bitcast.4, f32[128,1536]{1,0:T(8,128)S(1)} %pooled_base.1.refs_3_), custom_call_target="tpu_custom_call" | custom-call | flops 12582912 | bytes 98304 | tf_op jit(solution)/shard_map/back/pallas_call | solution.py:83
  32.9 1.5 %collective-permute-done.6.refs_0_ = bf16[512,256]{1,0:T(8,128)(2,1)S(1)} collective-permute-done((bf16[512,256]{1,0:T(8,128)(2,1)S(1)}, bf16[512,256]{1,0:T(8,128)(2,1)S(1)}, u32[]{:S(2)}, u32[]{:S(2)}) %collective-permute-start.6) | collective-permute-done | bytes 262176 | tf_op jit(solution)/shard_map/ppermute | solution.py:457
  34.3 0.6 back.4.refs_5_.refs_4_
  35.0 5.0 %collective-permute-done.5.refs_0_ = bf16[512,256]{1,0:T(8,128)(2,1)S(1)} collective-permute-done((bf16[512,256]{1,0:T(8,128)(2,1)S(1)}, bf16[512,256]{1,0:T(8,128)(2,1)S(1)}, u32[]{:S(2)}, u32[]{:S(2)}) %collective-permute-start.5) | collective-permute-done | bytes 262176 | tf_op jit(solution)/shard_map/ppermute | solution.py:457
  40.0 0.7 %middle.5 = (bf16[512,256]{1,0:T(8,128)(2,1)S(1)}, bf16[512,256]{1,0:T(8,128)(2,1)S(1)}) custom-call(bf16[512,256]{1,0:T(8,128)(2,1)S(1)} %collective-permute-done.5.refs_0_, f32[512,256]{1,0:T(8,128)S(1)} %get-tuple-element.39.refs_1_, f32[768]{0:T(1024)S(1)} %copy-done.2, f32[768]{0:T(1024)S(1)} %copy-done.3, f32[128,256]{1,0:T(8,128)S(1)} %get-tuple-element.40.refs_4_, ...), custom_call_target="tpu_custom_call" | custom-call | flops 61440 | bytes 24576 | tf_op jit(solution)/shard_map/middle/pallas_call | solution.py:83
  40.7 3.9 %collective-permute-start.8 = (bf16[512,256]{1,0:T(8,128)(2,1)S(1)}, bf16[512,256]{1,0:T(8,128)(2,1)S(1)}, u32[]{:S(2)}, u32[]{:S(2)}) collective-permute-start(bf16[512,256]{1,0:T(8,128)(2,1)S(1)} %get-tuple-element.44.refs_0_), channel_id=1, source_target_pairs={{0,2},{1,3},{2,4},{3,5},{4,6},{5,7},{6,8},{7,9},{8,10},{9,11},{10,... | collective-permute-start | bytes 786440 | tf_op jit(solution)/shard_map/ppermute | solution.py:447
  44.5 2.9 %collective-permute-start.7 = (bf16[512,256]{1,0:T(8,128)(2,1)S(1)}, bf16[512,256]{1,0:T(8,128)(2,1)S(1)}, u32[]{:S(2)}, u32[]{:S(2)}) collective-permute-start(bf16[512,256]{1,0:T(8,128)(2,1)S(1)} %get-tuple-element.44.refs_0_), channel_id=1, source_target_pairs={{2,0},{3,1},{4,2},{5,3},{6,4},{7,5},{8,6},{9,7},{10,8},{11,9},{12,... | collective-permute-start | bytes 786440 | tf_op jit(solution)/shard_map/ppermute | solution.py:447
  47.4 4.1 %collective-permute-start.11 = (bf16[512,256]{1,0:T(8,128)(2,1)S(1)}, bf16[512,256]{1,0:T(8,128)(2,1)S(1)}, u32[]{:S(2)}, u32[]{:S(2)}) collective-permute-start(bf16[512,256]{1,0:T(8,128)(2,1)S(1)} %collective-permute-done.6.refs_0_), channel_id=1, source_target_pairs={{0,4},{1,5},{4,8},{5,9},{6,2},{7,3},{8,12},{9,13},{10,6},{11,7},{1... | collective-permute-start | bytes 786440 | tf_op jit(solution)/shard_map/ppermute | solution.py:457
  51.6 3.4 %collective-permute-start.10 = (bf16[512,256]{1,0:T(8,128)(2,1)S(1)}, bf16[512,256]{1,0:T(8,128)(2,1)S(1)}, u32[]{:S(2)}, u32[]{:S(2)}) collective-permute-start(bf16[512,256]{1,0:T(8,128)(2,1)S(1)} %collective-permute-done.9.refs_1_), channel_id=1, source_target_pairs={{0,4},{1,5},{4,8},{5,9},{6,2},{7,3},{8,12},{9,13},{10,6},{11,7},{1... | collective-permute-start | bytes 786440 | tf_op jit(solution)/shard_map/ppermute | solution.py:457
  55.0 1.7 %pooled.1 = bf16[2,64,1536]{2,1,0:T(8,128)(2,1)} custom-call(bf16[512,256]{1,0:T(8,128)(2,1)S(1)} %get-tuple-element.32.refs_0_, bf16[512,256]{1,0:T(8,128)(2,1)S(1)} %get-tuple-element.38.refs_1_, bf16[512,256]{1,0:T(8,128)(2,1)S(1)} %get-tuple-element.43.refs_2_.refs_5_, f32[128,1536]{1,0:T(8,128)S(1)} %pooled_base.1.refs_3_, bf16[768,1536]{1,0:T(8,128)(2,1)S(1)} %copy-done), custom_call_target="tpu_custom_call" | custom-call | flops 4718592 | bytes 18432 | tf_op jit(solution)/shard_map/pooled/pallas_call | solution.py:318
  56.9 1.5 %back.5.refs_3_ = f32[512,1536]{1,0:T(8,128)S(1)} custom-call(bf16[512,256]{1,0:T(8,128)(2,1)S(1)} %get-tuple-element.44.refs_0_, bf16[512,256]{1,0:T(8,128)(2,1)S(1)} %collective-permute-done.9.refs_1_, bf16[512,256]{1,0:T(8,128)(2,1)S(1)} %collective-permute-done.11.refs_2_, bf16[3,1536,768]{2,1,0:T(8,128)(2,1)S(1)} %bitcast.4, ...), custom_call_target="tpu_custom_call" | custom-call | flops 18874368 | bytes 98304 | tf_op jit(solution)/shard_map/back/pallas_call | solution.py:83
  58.4 1.4 %collective-permute-done.10.refs_2_ = bf16[512,256]{1,0:T(8,128)(2,1)S(1)} collective-permute-done((bf16[512,256]{1,0:T(8,128)(2,1)S(1)}, bf16[512,256]{1,0:T(8,128)(2,1)S(1)}, u32[]{:S(2)}, u32[]{:S(2)}) %collective-permute-start.10) | collective-permute-done | bytes 262176 | tf_op jit(solution)/shard_map/ppermute | solution.py:457
  59.8 2.9 %final.1 = bf16[512,1536]{1,0:T(8,128)(2,1)} custom-call(bf16[512,256]{1,0:T(8,128)(2,1)S(1)} %collective-permute-done.7.a_ref.refs_0_, bf16[512,256]{1,0:T(8,128)(2,1)S(1)} %collective-permute-done.8.b_ref.refs_1_, bf16[512,256]{1,0:T(8,128)(2,1)S(1)} %collective-permute-done.10.refs_2_, f32[512,1536]{1,0:T(8,128)S(1)} %back.5.refs_3_, ...), custom_call_target="tpu_custom_call" | custom-call | flops 18874368 | bytes 98304 | tf_op jit(solution)/shard_map/final/pallas_call | solution.py:416
  (31 shorter events, 1.2 us)
Async XLA Ops:
  0.6 7.6 %slice-start = ((s8[7077888]{0:T(1024)(128)(4,1)}), s8[4194304]{0:T(1024)(128)(4,1)S(1)}, s32[]{:S(2)}) async-start(s8[7077888]{0:T(1024)(128)(4,1)} %bitcast.3), calls=%async_computation | async-start | bytes 8388608
  0.6 7.6 %slice-start.1 = ((s8[7077888]{0:T(1024)(128)(4,1)}), s8[2883584]{0:T(1024)(128)(4,1)S(1)}, s32[]{:S(2)}) async-start(s8[7077888]{0:T(1024)(128)(4,1)} %bitcast.3), calls=%async_computation.1 | async-start | bytes 5767168
  3.7 11.2 %collective-permute-start = (bf16[512,256]{1,0:T(8,128)(2,1)S(1)}, bf16[512,256]{1,0:T(8,128)(2,1)S(1)}, u32[]{:S(2)}, u32[]{:S(2)}) collective-permute-start(bf16[512,256]{1,0:T(8,128)(2,1)S(1)} %get-tuple-element.25), channel_id=1, source_target_pairs={{2,6},{3,7},{4,0},{5,1},{6,10},{7,11},{8,4},{9,5},{10,14},{11,15},... | collective-permute-start | bytes 786440 | tf_op jit(solution)/shard_map/ppermute | solution.py:457
  6.3 13.0 %collective-permute-start.2 = (bf16[512,256]{1,0:T(8,128)(2,1)S(1)}, bf16[512,256]{1,0:T(8,128)(2,1)S(1)}, u32[]{:S(2)}, u32[]{:S(2)}) collective-permute-start(bf16[512,256]{1,0:T(8,128)(2,1)S(1)} %side.2.refs_2_), channel_id=1, source_target_pairs={{2,6},{3,7},{4,0},{5,1},{6,10},{7,11},{8,4},{9,5},{10,14},{11,15},... | collective-permute-start | bytes 786440 | tf_op jit(solution)/shard_map/ppermute | solution.py:457
  15.0 6.5 %copy-start = (bf16[768,1536]{1,0:T(8,128)(2,1)S(1)}, bf16[768,1536]{1,0:T(8,128)(2,1)}, u32[]{:S(2)}) copy-start(bf16[768,1536]{1,0:T(8,128)(2,1)} %refs_4_.1) | copy-start | bytes 7077892
  15.0 6.5 %copy-start.1 = (bf16[2,64,1536]{2,1,0:T(8,128)(2,1)S(1)}, bf16[2,64,1536]{2,1,0:T(8,128)(2,1)}, u32[]{:S(2)}) copy-start(bf16[2,64,1536]{2,1,0:T(8,128)(2,1)} %param.10) | copy-start | bytes 1179652
  15.0 7.3 %collective-permute-start.1 = (bf16[512,256]{1,0:T(8,128)(2,1)S(1)}, bf16[512,256]{1,0:T(8,128)(2,1)S(1)}, u32[]{:S(2)}, u32[]{:S(2)}) collective-permute-start(bf16[512,256]{1,0:T(8,128)(2,1)S(1)} %join.3.refs_2_), channel_id=1, source_target_pairs={{0,2},{1,3},{2,0},{3,1},{4,6},{5,7},{6,4},{7,5},{8,10},{9,11},{10,... | collective-permute-start | bytes 786440 | tf_op jit(solution)/shard_map/ppermute | solution.py:457
  17.2 5.2 %copy-start.2 = (f32[768]{0:T(1024)S(1)}, f32[768]{0:T(1024)}, u32[]{:S(2)}) copy-start(f32[768]{0:T(1024)} %refs_2_.6) | copy-start | bytes 9220
  17.2 5.2 %copy-start.3 = (f32[768]{0:T(1024)S(1)}, f32[768]{0:T(1024)}, u32[]{:S(2)}) copy-start(f32[768]{0:T(1024)} %refs_3_.3) | copy-start | bytes 9220
  17.2 8.4 %collective-permute-start.4 = (bf16[512,256]{1,0:T(8,128)(2,1)S(1)}, bf16[512,256]{1,0:T(8,128)(2,1)S(1)}, u32[]{:S(2)}, u32[]{:S(2)}) collective-permute-start(bf16[512,256]{1,0:T(8,128)(2,1)S(1)} %side.3.refs_2_), channel_id=1, source_target_pairs={{2,6},{3,7},{4,0},{5,1},{6,10},{7,11},{8,4},{9,5},{10,14},{11,15},... | collective-permute-start | bytes 786440 | tf_op jit(solution)/shard_map/ppermute | solution.py:457
  19.4 9.3 %collective-permute-start.3 = (bf16[512,256]{1,0:T(8,128)(2,1)S(1)}, bf16[512,256]{1,0:T(8,128)(2,1)S(1)}, u32[]{:S(2)}, u32[]{:S(2)}) collective-permute-start(bf16[512,256]{1,0:T(8,128)(2,1)S(1)} %join.4.refs_2_), channel_id=1, source_target_pairs={{0,2},{1,3},{2,0},{3,1},{4,6},{5,7},{6,4},{7,5},{8,10},{9,11},{10,... | collective-permute-start | bytes 786440 | tf_op jit(solution)/shard_map/ppermute | solution.py:457
  21.4 5.2 %copy-start.4 = (f32[1536]{0:T(1024)S(1)}, f32[1536]{0:T(1024)}, u32[]{:S(2)}) copy-start(f32[1536]{0:T(1024)} %refs_1_.6) | copy-start | bytes 18436
  21.4 5.2 %copy-start.5 = (f32[1536]{0:T(1024)S(1)}, f32[1536]{0:T(1024)}, u32[]{:S(2)}) copy-start(f32[1536]{0:T(1024)} %refs_2_.3) | copy-start | bytes 18436
  23.1 11.3 %collective-permute-start.6 = (bf16[512,256]{1,0:T(8,128)(2,1)S(1)}, bf16[512,256]{1,0:T(8,128)(2,1)S(1)}, u32[]{:S(2)}, u32[]{:S(2)}) collective-permute-start(bf16[512,256]{1,0:T(8,128)(2,1)S(1)} %get-tuple-element.37.refs_2_.refs_0_), channel_id=1, source_target_pairs={{0,2},{1,3},{2,0},{3,1},{4,6},{5,7},{6,4},{7,5},{8,10},{9,11},{10,... | collective-permute-start | bytes 786440 | tf_op jit(solution)/shard_map/ppermute | solution.py:457
  25.6 14.3 %collective-permute-start.5 = (bf16[512,256]{1,0:T(8,128)(2,1)S(1)}, bf16[512,256]{1,0:T(8,128)(2,1)S(1)}, u32[]{:S(2)}, u32[]{:S(2)}) collective-permute-start(bf16[512,256]{1,0:T(8,128)(2,1)S(1)} %join.5.refs_3_), channel_id=1, source_target_pairs={{0,2},{1,3},{2,0},{3,1},{4,6},{5,7},{6,4},{7,5},{8,10},{9,11},{10,... | collective-permute-start | bytes 786440 | tf_op jit(solution)/shard_map/ppermute | solution.py:457
  28.6 2.9 %copy-start.6 = (f32[1536]{0:T(1024)S(1)}, f32[1536]{0:T(1024)}, u32[]{:S(2)}) copy-start(f32[1536]{0:T(1024)} %refs_1_.7) | copy-start | bytes 18436
  29.4 22.1 %collective-permute-start.9 = (bf16[512,256]{1,0:T(8,128)(2,1)S(1)}, bf16[512,256]{1,0:T(8,128)(2,1)S(1)}, u32[]{:S(2)}, u32[]{:S(2)}) collective-permute-start(bf16[512,256]{1,0:T(8,128)(2,1)S(1)} %get-tuple-element.41.refs_2_.refs_1_), channel_id=1, source_target_pairs={{0,2},{1,3},{2,0},{3,1},{4,6},{5,7},{6,4},{7,5},{8,10},{9,11},{10,... | collective-permute-start | bytes 786440 | tf_op jit(solution)/shard_map/ppermute | solution.py:457
  40.7 16.0 %collective-permute-start.8 = (bf16[512,256]{1,0:T(8,128)(2,1)S(1)}, bf16[512,256]{1,0:T(8,128)(2,1)S(1)}, u32[]{:S(2)}, u32[]{:S(2)}) collective-permute-start(bf16[512,256]{1,0:T(8,128)(2,1)S(1)} %get-tuple-element.44.refs_0_), channel_id=1, source_target_pairs={{0,2},{1,3},{2,4},{3,5},{4,6},{5,7},{6,8},{7,9},{8,10},{9,11},{10,... | collective-permute-start | bytes 786440 | tf_op jit(solution)/shard_map/ppermute | solution.py:447
  44.5 12.2 %collective-permute-start.7 = (bf16[512,256]{1,0:T(8,128)(2,1)S(1)}, bf16[512,256]{1,0:T(8,128)(2,1)S(1)}, u32[]{:S(2)}, u32[]{:S(2)}) collective-permute-start(bf16[512,256]{1,0:T(8,128)(2,1)S(1)} %get-tuple-element.44.refs_0_), channel_id=1, source_target_pairs={{2,0},{3,1},{4,2},{5,3},{6,4},{7,5},{8,6},{9,7},{10,8},{11,9},{12,... | collective-permute-start | bytes 786440 | tf_op jit(solution)/shard_map/ppermute | solution.py:447
  47.4 9.5 %collective-permute-start.11 = (bf16[512,256]{1,0:T(8,128)(2,1)S(1)}, bf16[512,256]{1,0:T(8,128)(2,1)S(1)}, u32[]{:S(2)}, u32[]{:S(2)}) collective-permute-start(bf16[512,256]{1,0:T(8,128)(2,1)S(1)} %collective-permute-done.6.refs_0_), channel_id=1, source_target_pairs={{0,4},{1,5},{4,8},{5,9},{6,2},{7,3},{8,12},{9,13},{10,6},{11,7},{1... | collective-permute-start | bytes 786440 | tf_op jit(solution)/shard_map/ppermute | solution.py:457
  51.6 8.3 %collective-permute-start.10 = (bf16[512,256]{1,0:T(8,128)(2,1)S(1)}, bf16[512,256]{1,0:T(8,128)(2,1)S(1)}, u32[]{:S(2)}, u32[]{:S(2)}) collective-permute-start(bf16[512,256]{1,0:T(8,128)(2,1)S(1)} %collective-permute-done.9.refs_1_), channel_id=1, source_target_pairs={{0,4},{1,5},{4,8},{5,9},{6,2},{7,3},{8,12},{9,13},{10,6},{11,7},{1... | collective-permute-start | bytes 786440 | tf_op jit(solution)/shard_map/ppermute | solution.py:457

commit v3 on v2

--- a/solution.py
+++ b/solution.py
@@ -15,6 +15,7 @@
 F32 = jnp.float32
 BF16 = jnp.bfloat16
 SHARE = 64
+TILES = 6
 LIMIT = 12 * 1024 * 1024
 
 
@@ -293,7 +294,7 @@
 def pooled_body(*refs):
     count = len(SPLITS)
     hidden = refs[:count]
-    base_ref, w_ref, o_ref, out_ref, sem = refs[count:]
+    base_ref, w_ref, o_ref, mark_ref, out_ref, sem = refs[count:]
     bins, width = out_ref.shape
     rows = hidden[0].shape[0]
     average = averaging(bins, rows)
@@ -302,6 +303,7 @@
         mean = dot_nn(average, hidden[n][...]).astype(BF16)
         total = total + dot_nn(mean, w_ref[bounds(n), :])
     out_ref[...] = total.astype(BF16)
+    mark_ref[...] = out_ref[:16, :LANES]
     half = bins // o_ref.shape[0]
     for n in range(o_ref.shape[0]):
         copy = pltpu.make_async_copy(out_ref.at[pl.ds(n * half, half)], o_ref.at[n], sem.at[n])
@@ -319,8 +321,11 @@
         pooled_body,
         name="pooled",
         in_specs=[pl.BlockSpec(memory_space=pltpu.VMEM)] * len(operands),
-        out_specs=pl.BlockSpec(memory_space=pltpu.HBM),
-        out_shape=pltpu.HBM((batch, bins // batch, width), BF16),
+        out_specs=[pl.BlockSpec(memory_space=pltpu.HBM), pl.BlockSpec(memory_space=pltpu.VMEM)],
+        out_shape=[
+            pltpu.HBM((batch, bins // batch, width), BF16),
+            pltpu.VMEM((16, LANES), BF16),
+        ],
         scratch_shapes=[pltpu.VMEM((bins, width), BF16), pltpu.SemaphoreType.DMA((batch,))],
         compiler_params=pltpu.CompilerParams(vmem_limit_bytes=LIMIT),
         cost_estimate=cost_of(2 * bins * width * mid, 6 * bins * width, 0),
@@ -383,23 +388,41 @@
     o_ref[...] = a_ref[:16, :LANES] + b_ref[:16, :LANES]
 
 
-def touch(a, b):
-    return local_call(touch_body, "touch", [a, b], ((16, LANES), BF16), (1, 1, 0))
+def touch(a, b, after):
+    return local_call(touch_body, "touch", [a, b], ((16, LANES), BF16), (1, 1, 0), after=after)
+
+
+def settle_body(stride, kinds, *refs):
+    grads = refs[: len(kinds)]
+    c_ref, w_ref, d_ref, og_ref, o_ref = refs[len(kinds) :]
+    spread = spreading(c_ref.shape[0], og_ref.shape[0])
+    total = c_ref[...] + back_sum(stride, grads, kinds, w_ref)
+    o_ref[...] = dot_nn(spread, og_ref[...]) + total * d_ref[...]
+
+
+def settle(total, terms, taps, slope, binned, stride):
+    kinds = [(kind, n) for kind, n, _ in terms]
+    grads = [g for _, _, g in terms]
+    rows, width = slope.shape
+    return local_call(
+        functools.partial(settle_body, stride, kinds),
+        "settle",
+        [*grads, total, taps, slope, binned],
+        ((rows, width), F32),
+        (2 * rows * width * sum(g.shape[1] for g in grads), 8 * rows * width, 0),
+    )
 
 
 def final_body(stride, kinds, tiles, *refs):
     grads = refs[: len(kinds)]
-    c_ref, w_ref, d_ref, og_ref, _, o_ref, out_ref, sems = refs[len(kinds) :]
+    c_ref, w_ref, d_ref, o_ref, out_ref, sems = refs[len(kinds) :]
     rows, width = c_ref.shape
     tile = width // tiles
-    spread = spreading(rows, og_ref.shape[0])
     copies = []
     for n in range(tiles):
         columns = slice(n * tile, n * tile + tile)
-        total = c_ref[:, columns] + back_sum(stride, grads, kinds, w_ref, columns)
-        out_ref[:, columns] = (
-            dot_nn(spread, og_ref[:, columns]) + total * d_ref[:, columns]
-        ).astype(BF16)
+        last = back_sum(stride, grads, kinds, w_ref, columns)
+        out_ref[:, columns] = (c_ref[:, columns] + last * d_ref[:, columns]).astype(BF16)
         copy = pltpu.make_async_copy(out_ref.at[:, columns], o_ref.at[:, columns], sems.at[n])
         copy.start()
         copies.append(copy)
@@ -407,12 +430,12 @@
         copy.wait()
 
 
-def final(total, terms, taps, slope, binned, stride, after):
+def final(settled, terms, taps, slope, stride):
     kinds = [(kind, n) for kind, n, _ in terms]
     grads = [g for _, _, g in terms]
     rows, width = slope.shape
-    tiles = 3
-    operands = [*grads, total, taps, slope, binned, *after]
+    tiles = TILES
+    operands = [*grads, settled, taps, slope]
     return pl.pallas_call(
         functools.partial(final_body, stride, kinds, tiles),
         name="final",
@@ -473,11 +496,11 @@
     def later_than(value, *others):
         return lax.optimization_barrier((value, *others))[0]
 
-    sent1 = side(act, far_tap, 1)
+    kept0, kept1, kept2 = keep(act, taps, [0, 1, 2], stride)
+    own = centre(act, taps, [kept0])
+    sent1 = side(act, far_tap, 1, [own[0]])
     came1 = inward(sent1)
-    kept0, kept1, kept2 = keep(act, taps, [0, 1, 2], stride, [sent1])
-    own = centre(act, taps, [kept0])
-    joined0 = join(kept0, came0, [own[0]])
+    joined0 = join(kept0, came0, [sent1])
     mids0 = swap(joined0)
     sent2 = side(act, far_tap, 2, [joined0])
     came2 = inward(sent2)
@@ -497,24 +520,22 @@
     far0 = outward(near0)
     total = back(total, [("near", 0, near0)], taps, stride)
     grad2, hid2 = middle(mids2, own[2], 2, scale_mid, shift_mid, hg[2], [total])
-    before2 = hop(grad2, stride)
-    later2 = hop(grad2, -stride)
-    near1 = later_than(near1, grad2)
+    near2 = swap(grad2)
+    pooled, mean2 = pooled_out(base, [hid0, hid1, hid2], out_weight, batch)
+    near1, mean2 = lax.optimization_barrier((near1, mean2))
     far1 = outward(near1)
-    pooled = pooled_out(base, [hid0, hid1, hid2], out_weight, batch)
+    mark = touch(far0, near1, [mean2])
+    near2, mark = lax.optimization_barrier((near2, mark))
+    far2 = outward(near2)
     total = back(
-        total, [("own", 2, grad2), ("near", 1, near1), ("far", 0, far0)], taps, stride, [hid2]
-    )
-    arrived = touch(later2, before2)
-    out = final(
         total,
-        [("later", 2, later2), ("before", 2, before2), ("far", 1, far1)],
+        [("own", 2, grad2), ("far", 0, far0), ("near", 1, near1), ("near", 2, near2)],
         taps,
-        slope,
-        binned,
         stride,
-        [arrived],
-    )
+        [mark],
+    )
+    settled = settle(total, [("far", 1, far1)], taps, slope, binned, stride)
+    out = final(settled, [("far", 2, far2)], taps, slope, stride)
     return pooled, out.reshape(seqs_in.shape)
 
 

time: 63.7 us -> 62.3 us (0.978)
  waiting for transfers between devices: 13 us -> 11.6 us
    ppermute x10 -> x12, starting transfers between devices: 21.8 us -> 28.6 us  [block_permute(): return lax.ppermute(value, AXIS, pairs)]
    ppermute x2 -> x0, starting transfers between devices: 6.74 us -> none  [hop(): lax.ppermute(value, AXIS, [(i, i + steps) for i in range(count) if 0 <= i...]
    ppermute x10 -> x12, waiting for transfers between devices: 13 us -> 11.6 us  [block_permute(): return lax.ppermute(value, AXIS, pairs)]
    pallas_call x17 -> x18, Pallas kernels: 12.5 us -> 13.9 us  [local_call(): pl.pallas_call(body, name=name, in_specs=[space] * len(operands), out_spe...]
    pallas_call x1, Pallas kernels: 2.87 us -> 1.54 us  [final(): pl.pallas_call(functools.partial(final_body, stride, kinds, tiles), name=...]
  transfers between devices with their start and end apart: 12 -> 12, of which waited for: 8 -> 9; matrix products, arithmetic and copies ran while one was open for 0% -> 0% of each run, Pallas kernels for 23% -> 25%
where the time goes in v3:
time: 62.3 us; the launch traced here: 61.5 us
  starting transfers between devices  28.6 us (46%)
  Pallas kernels  20.2 us (32%)
  waiting for transfers between devices  11.6 us (19%)
  between operations  1.06 us (2%)
    ppermute x12, starting transfers between devices, block_permute(): return lax.ppermute(value, AXIS, pairs)  28.6 us
    pallas_call x18, Pallas kernels, local_call(): pl.pallas_call(body, name=name, in_specs=[space] * len(operands), out_spe...  13.9 us
    ppermute x12, waiting for transfers between devices, block_permute(): return lax.ppermute(value, AXIS, pairs)  11.6 us
    pallas_call x1, Pallas kernels, front(): pl.pallas_call(functools.partial(front_body, stride), name='front', in_sp...  3.03 us
    pallas_call x1, Pallas kernels, pooled_out(): pl.pallas_call(pooled_body, name='pooled', in_specs=[pl.BlockSpec(memory_...  1.73 us
    pallas_call x1, Pallas kernels, final(): pl.pallas_call(functools.partial(final_body, stride, kinds, tiles), name=...  1.54 us
  transfers between devices with their start and end apart: 12, of which 9 were waited for; matrix products, arithmetic and copies ran while one was open for 0% of the time, Pallas kernels for 25%

profile of v3, /device:TPU:8, one launch (start us, length us, event | category | flops | bytes accessed | tf_op | source)
XLA Modules:
  0.0 61.5 jit_solution(15496892872219694868)
XLA Ops:
  0.6 3.0 %front.1 = (bf16[512,1536]{1,0:T(8,128)(2,1)S(1)}, bf16[1536,768]{1,0:T(8,128)(2,1)S(1)}, bf16[512,1536]{1,0:T(8,128)(2,1)S(1)}, bf16[512,256]{1,0:T(8,128)(2,1)S(1)}) custom-call(bf16[512,1536]{1,0:T(8,128)(2,1)} %bitcast.6, f32[1536]{0:T(1024)} %refs_1_.5, f32[1536]{0:T(1024)} %refs_2_.3, bf16[3,1536,768]{2,1,0:T(8,128)(2,1)} %refs_2_.8), custom_call_target="tpu_custom_call" | custom-call | flops 6291456 | bytes 135168 | tf_op jit(solution)/shard_map/front/pallas_call | solution.py:138
  3.7 2.1 %collective-permute-start = (bf16[512,256]{1,0:T(8,128)(2,1)S(1)}, bf16[512,256]{1,0:T(8,128)(2,1)S(1)}, u32[]{:S(2)}, u32[]{:S(2)}) collective-permute-start(bf16[512,256]{1,0:T(8,128)(2,1)S(1)} %get-tuple-element.30), channel_id=1, source_target_pairs={{2,6},{3,7},{4,0},{5,1},{6,10},{7,11},{8,4},{9,5},{10,14},{11,15},... | collective-permute-start | bytes 786440 | tf_op jit(solution)/shard_map/ppermute | solution.py:480
  5.7 1.4 %keep.1 = (f32[512,256]{1,0:T(8,128)S(1)}, f32[512,256]{1,0:T(8,128)S(1)}, f32[512,256]{1,0:T(8,128)S(1)}) custom-call(bf16[512,1536]{1,0:T(8,128)(2,1)S(1)} %get-tuple-element.29.a_ref.refs_0_, bf16[3,1536,768]{2,1,0:T(8,128)(2,1)S(1)} %copy-done), custom_call_target="tpu_custom_call" | custom-call | flops 18874368 | bytes 24576 | tf_op jit(solution)/shard_map/keep/pallas_call | solution.py:84
  7.1 1.4 %centre.1 = (f32[512,256]{1,0:T(8,128)S(1)}, f32[512,256]{1,0:T(8,128)S(1)}, f32[512,256]{1,0:T(8,128)S(1)}) custom-call(bf16[512,1536]{1,0:T(8,128)(2,1)S(1)} %get-tuple-element.29.a_ref.refs_0_, bf16[3,1536,768]{2,1,0:T(8,128)(2,1)S(1)} %copy-done, f32[512,256]{1,0:T(8,128)S(1)} %get-tuple-element.32.refs_2_.refs_0_), custom_call_target="tpu_custom_call" | custom-call | flops 18874368 | bytes 24576 | tf_op jit(solution)/shard_map/centre/pallas_call | solution.py:84
  9.1 1.9 %collective-permute-start.2 = (bf16[512,256]{1,0:T(8,128)(2,1)S(1)}, bf16[512,256]{1,0:T(8,128)(2,1)S(1)}, u32[]{:S(2)}, u32[]{:S(2)}) collective-permute-start(bf16[512,256]{1,0:T(8,128)(2,1)S(1)} %side.2.refs_2_), channel_id=1, source_target_pairs={{2,6},{3,7},{4,0},{5,1},{6,10},{7,11},{8,4},{9,5},{10,14},{11,15},... | collective-permute-start | bytes 786440 | tf_op jit(solution)/shard_map/ppermute | solution.py:480
  11.0 2.9 %collective-permute-done.refs_1_ = bf16[512,256]{1,0:T(8,128)(2,1)S(1)} collective-permute-done((bf16[512,256]{1,0:T(8,128)(2,1)S(1)}, bf16[512,256]{1,0:T(8,128)(2,1)S(1)}, u32[]{:S(2)}, u32[]{:S(2)}) %collective-permute-start) | collective-permute-done | bytes 262176 | tf_op jit(solution)/shard_map/ppermute | solution.py:480
  14.1 1.8 %collective-permute-start.1 = (bf16[512,256]{1,0:T(8,128)(2,1)S(1)}, bf16[512,256]{1,0:T(8,128)(2,1)S(1)}, u32[]{:S(2)}, u32[]{:S(2)}) collective-permute-start(bf16[512,256]{1,0:T(8,128)(2,1)S(1)} %join.3.refs_2_), channel_id=1, source_target_pairs={{0,2},{1,3},{2,0},{3,1},{4,6},{5,7},{6,4},{7,5},{8,10},{9,11},{10,... | collective-permute-start | bytes 786440 | tf_op jit(solution)/shard_map/ppermute | solution.py:480
  16.4 2.4 %collective-permute-start.4 = (bf16[512,256]{1,0:T(8,128)(2,1)S(1)}, bf16[512,256]{1,0:T(8,128)(2,1)S(1)}, u32[]{:S(2)}, u32[]{:S(2)}) collective-permute-start(bf16[512,256]{1,0:T(8,128)(2,1)S(1)} %side.3.refs_2_), channel_id=1, source_target_pairs={{2,6},{3,7},{4,0},{5,1},{6,10},{7,11},{8,4},{9,5},{10,14},{11,15},... | collective-permute-start | bytes 786440 | tf_op jit(solution)/shard_map/ppermute | solution.py:480
  19.4 4.0 %collective-permute-start.3 = (bf16[512,256]{1,0:T(8,128)(2,1)S(1)}, bf16[512,256]{1,0:T(8,128)(2,1)S(1)}, u32[]{:S(2)}, u32[]{:S(2)}) collective-permute-start(bf16[512,256]{1,0:T(8,128)(2,1)S(1)} %join.4.refs_2_), channel_id=1, source_target_pairs={{0,2},{1,3},{2,0},{3,1},{4,6},{5,7},{6,4},{7,5},{8,10},{9,11},{10,... | collective-permute-start | bytes 786440 | tf_op jit(solution)/shard_map/ppermute | solution.py:480
  23.4 0.9 %hidden_grad.1 = (f32[128,256]{1,0:T(8,128)S(1)}, f32[128,256]{1,0:T(8,128)S(1)}, f32[128,256]{1,0:T(8,128)S(1)}) custom-call(bf16[128,1536]{1,0:T(8,128)(2,1)S(1)} %bitcast.3, bf16[768,1536]{1,0:T(8,128)(2,1)S(1)} %copy-done.1, bf16[512,256]{1,0:T(8,128)(2,1)S(1)} %join.4.refs_2_), custom_call_target="tpu_custom_call" | custom-call | flops 4718592 | bytes 6144 | tf_op jit(solution)/shard_map/hidden_grad/pallas_call | solution.py:84
  24.4 0.7 %middle.3 = (bf16[512,256]{1,0:T(8,128)(2,1)S(1)}, bf16[512,256]{1,0:T(8,128)(2,1)S(1)}) custom-call(bf16[512,256]{1,0:T(8,128)(2,1)S(1)} %collective-permute-done.1.t_ref, f32[512,256]{1,0:T(8,128)S(1)} %get-tuple-element.34.refs_2_.p_ref, f32[768]{0:T(1024)S(1)} %copy-done.3, f32[768]{0:T(1024)S(1)} %copy-done.4, f32[128,256]{1,0:T(8,128)S(1)} %get-tuple-element.36.hg_ref), custom_call_target="tpu_custom_call" | custom-call | flops 61440 | bytes 24576 | tf_op jit(solution)/shard_map/middle/pallas_call | solution.py:84
  25.6 2.0 %collective-permute-start.5 = (bf16[512,256]{1,0:T(8,128)(2,1)S(1)}, bf16[512,256]{1,0:T(8,128)(2,1)S(1)}, u32[]{:S(2)}, u32[]{:S(2)}) collective-permute-start(bf16[512,256]{1,0:T(8,128)(2,1)S(1)} %join.5.refs_3_), channel_id=1, source_target_pairs={{0,2},{1,3},{2,0},{3,1},{4,6},{5,7},{6,4},{7,5},{8,10},{9,11},{10,... | collective-permute-start | bytes 786440 | tf_op jit(solution)/shard_map/ppermute | solution.py:480
  27.6 1.9 %slope.1.refs_5_.refs_3_ = f32[512,1536]{1,0:T(8,128)S(1)} custom-call(bf16[512,1536]{1,0:T(8,128)(2,1)S(1)} %get-tuple-element.40.refs_0_, f32[1536]{0:T(1024)S(1)} %copy-done.5, f32[1536]{0:T(1024)S(1)} %copy-done.6, bf16[512,256]{1,0:T(8,128)(2,1)S(1)} %join.5.refs_3_), custom_call_target="tpu_custom_call" | custom-call | flops 368640 | bytes 73728 | tf_op jit(solution)/shard_map/slope/pallas_call | solution.py:84
  29.5 1.0 %collective-permute-done.3.refs_0_ = bf16[512,256]{1,0:T(8,128)(2,1)S(1)} collective-permute-done((bf16[512,256]{1,0:T(8,128)(2,1)S(1)}, bf16[512,256]{1,0:T(8,128)(2,1)S(1)}, u32[]{:S(2)}, u32[]{:S(2)}) %collective-permute-start.3) | collective-permute-done | bytes 262176 | tf_op jit(solution)/shard_map/ppermute | solution.py:480
  30.5 0.7 %middle.4 = (bf16[512,256]{1,0:T(8,128)(2,1)S(1)}, bf16[512,256]{1,0:T(8,128)(2,1)S(1)}) custom-call(bf16[512,256]{1,0:T(8,128)(2,1)S(1)} %collective-permute-done.3.refs_0_, f32[512,256]{1,0:T(8,128)S(1)} %get-tuple-element.38.refs_1_, f32[768]{0:T(1024)S(1)} %copy-done.3, f32[768]{0:T(1024)S(1)} %copy-done.4, f32[128,256]{1,0:T(8,128)S(1)} %get-tuple-element.39.refs_4_, ...), custom_call_target="tpu_custom_call" | custom-call | flops 61440 | bytes 24576 | tf_op jit(solution)/shard_map/middle/pallas_call | solution.py:84
  31.2 2.2 %collective-permute-start.9 = (bf16[512,256]{1,0:T(8,128)(2,1)S(1)}, bf16[512,256]{1,0:T(8,128)(2,1)S(1)}, u32[]{:S(2)}, u32[]{:S(2)}) collective-permute-start(bf16[512,256]{1,0:T(8,128)(2,1)S(1)} %get-tuple-element.46.refs_2_.refs_1_), channel_id=1, source_target_pairs={{0,2},{1,3},{2,0},{3,1},{4,6},{5,7},{6,4},{7,5},{8,10},{9,11},{10,... | collective-permute-start | bytes 786440 | tf_op jit(solution)/shard_map/ppermute | solution.py:480
  33.9 1.0 %back.3.refs_2_ = f32[512,1536]{1,0:T(8,128)S(1)} custom-call(bf16[512,256]{1,0:T(8,128)(2,1)S(1)} %get-tuple-element.42.refs_2_.refs_0_, bf16[512,256]{1,0:T(8,128)(2,1)S(1)} %get-tuple-element.46.refs_2_.refs_1_, bf16[3,1536,768]{2,1,0:T(8,128)(2,1)S(1)} %copy-done, f32[128,1536]{1,0:T(8,128)S(1)} %pooled_base.1.refs_3_), custom_call_target="tpu_custom_call" | custom-call | flops 12582912 | bytes 98304 | tf_op jit(solution)/shard_map/back/pallas_call | solution.py:84
  34.9 1.2 %collective-permute-done.6.refs_0_ = bf16[512,256]{1,0:T(8,128)(2,1)S(1)} collective-permute-done((bf16[512,256]{1,0:T(8,128)(2,1)S(1)}, bf16[512,256]{1,0:T(8,128)(2,1)S(1)}, u32[]{:S(2)}, u32[]{:S(2)}) %collective-permute-start.6) | collective-permute-done | bytes 262176 | tf_op jit(solution)/shard_map/ppermute | solution.py:480
  36.1 3.7 %collective-permute-start.8 = (bf16[512,256]{1,0:T(8,128)(2,1)S(1)}, bf16[512,256]{1,0:T(8,128)(2,1)S(1)}, u32[]{:S(2)}, u32[]{:S(2)}) collective-permute-start(bf16[512,256]{1,0:T(8,128)(2,1)S(1)} %collective-permute-done.6.refs_0_), channel_id=1, source_target_pairs={{0,4},{1,5},{4,8},{5,9},{6,2},{7,3},{8,12},{9,13},{10,6},{11,7},{1... | collective-permute-start | bytes 786440 | tf_op jit(solution)/shard_map/ppermute | solution.py:480
  39.8 0.6 %back.4.refs_5_ = f32[512,1536]{1,0:T(8,128)S(1)} custom-call(bf16[512,256]{1,0:T(8,128)(2,1)S(1)} %collective-permute-done.6.refs_0_, bf16[3,1536,768]{2,1,0:T(8,128)(2,1)S(1)} %copy-done, f32[512,1536]{1,0:T(8,128)S(1)} %back.3.refs_2_), custom_call_target="tpu_custom_call" | custom-call | flops 6291456 | bytes 98304 | tf_op jit(solution)/shard_map/back/pallas_call | solution.py:84
  40.4 1.3 %collective-permute-done.5.refs_0_ = bf16[512,256]{1,0:T(8,128)(2,1)S(1)} collective-permute-done((bf16[512,256]{1,0:T(8,128)(2,1)S(1)}, bf16[512,256]{1,0:T(8,128)(2,1)S(1)}, u32[]{:S(2)}, u32[]{:S(2)}) %collective-permute-start.5) | collective-permute-done | bytes 262176 | tf_op jit(solution)/shard_map/ppermute | solution.py:480
  41.7 0.7 %middle.5 = (bf16[512,256]{1,0:T(8,128)(2,1)S(1)}, bf16[512,256]{1,0:T(8,128)(2,1)S(1)}) custom-call(bf16[512,256]{1,0:T(8,128)(2,1)S(1)} %collective-permute-done.5.refs_0_, f32[512,256]{1,0:T(8,128)S(1)} %get-tuple-element.44.refs_1_, f32[768]{0:T(1024)S(1)} %copy-done.3, f32[768]{0:T(1024)S(1)} %copy-done.4, f32[128,256]{1,0:T(8,128)S(1)} %get-tuple-element.45.refs_4_, ...), custom_call_target="tpu_custom_call" | custom-call | flops 61440 | bytes 24576 | tf_op jit(solution)/shard_map/middle/pallas_call | solution.py:84
  42.5 2.2 %collective-permute-start.7 = (bf16[512,256]{1,0:T(8,128)(2,1)S(1)}, bf16[512,256]{1,0:T(8,128)(2,1)S(1)}, u32[]{:S(2)}, u32[]{:S(2)}) collective-permute-start(bf16[512,256]{1,0:T(8,128)(2,1)S(1)} %get-tuple-element.50.refs_0_), channel_id=1, source_target_pairs={{0,2},{1,3},{2,0},{3,1},{4,6},{5,7},{6,4},{7,5},{8,10},{9,11},{10,... | collective-permute-start | bytes 786440 | tf_op jit(solution)/shard_map/ppermute | solution.py:480
  44.7 1.7 %pooled.1 = (bf16[2,64,1536]{2,1,0:T(8,128)(2,1)}, bf16[16,128]{1,0:T(8,128)(2,1)S(1)}) custom-call(bf16[512,256]{1,0:T(8,128)(2,1)S(1)} %get-tuple-element.37.refs_0_, bf16[512,256]{1,0:T(8,128)(2,1)S(1)} %get-tuple-element.43.refs_1_, bf16[512,256]{1,0:T(8,128)(2,1)S(1)} %get-tuple-element.48.refs_2_, f32[128,1536]{1,0:T(8,128)S(1)} %pooled_base.1.refs_3_, ...), custom_call_target="tpu_custom_call" | custom-call | flops 4718592 | bytes 18432 | tf_op jit(solution)/shard_map/pooled/pallas_call | solution.py:320
  46.4 0.7 %collective-permute-done.9.refs_1_.refs_2_ = bf16[512,256]{1,0:T(8,128)(2,1)S(1)} collective-permute-done((bf16[512,256]{1,0:T(8,128)(2,1)S(1)}, bf16[512,256]{1,0:T(8,128)(2,1)S(1)}, u32[]{:S(2)}, u32[]{:S(2)}) %collective-permute-start.9) | collective-permute-done | bytes 262176 | tf_op jit(solution)/shard_map/ppermute | solution.py:480
  47.1 3.5 %collective-permute-start.11 = (bf16[512,256]{1,0:T(8,128)(2,1)S(1)}, bf16[512,256]{1,0:T(8,128)(2,1)S(1)}, u32[]{:S(2)}, u32[]{:S(2)}) collective-permute-start(bf16[512,256]{1,0:T(8,128)(2,1)S(1)} %collective-permute-done.9.refs_1_.refs_2_), channel_id=1, source_target_pairs={{0,4},{1,5},{4,8},{5,9},{6,2},{7,3},{8,12},{9,13},{10,6},{11,7},{1... | collective-permute-start | bytes 786440 | tf_op jit(solution)/shard_map/ppermute | solution.py:480
  50.6 2.8 %collective-permute-start.10 = (bf16[512,256]{1,0:T(8,128)(2,1)S(1)}, bf16[512,256]{1,0:T(8,128)(2,1)S(1)}, u32[]{:S(2)}, u32[]{:S(2)}) collective-permute-start(bf16[512,256]{1,0:T(8,128)(2,1)S(1)} %collective-permute-done.7.refs_3_), channel_id=1, source_target_pairs={{0,4},{1,5},{4,8},{5,9},{6,2},{7,3},{8,12},{9,13},{10,6},{11,7},{1... | collective-permute-start | bytes 786440 | tf_op jit(solution)/shard_map/ppermute | solution.py:480
  53.4 1.9 %back.5.refs_1_ = f32[512,1536]{1,0:T(8,128)S(1)} custom-call(bf16[512,256]{1,0:T(8,128)(2,1)S(1)} %get-tuple-element.50.refs_0_, bf16[512,256]{1,0:T(8,128)(2,1)S(1)} %collective-permute-done.8.refs_0_.refs_1_, bf16[512,256]{1,0:T(8,128)(2,1)S(1)} %collective-permute-done.9.refs_1_.refs_2_, bf16[512,256]{1,0:T(8,128)(2,1)S(1)} %collective-permute-done.7.refs_3_, ...), custom_call_target="tpu_custom_call" | custom-call | flops 25165824 | bytes 98304 | tf_op jit(solution)/shard_map/back/pallas_call | solution.py:84
  55.3 1.8 %collective-permute-done.11.refs_0_ = bf16[512,256]{1,0:T(8,128)(2,1)S(1)} collective-permute-done((bf16[512,256]{1,0:T(8,128)(2,1)S(1)}, bf16[512,256]{1,0:T(8,128)(2,1)S(1)}, u32[]{:S(2)}, u32[]{:S(2)}) %collective-permute-start.11) | collective-permute-done | bytes 262176 | tf_op jit(solution)/shard_map/ppermute | solution.py:480
  57.0 1.0 %settle.1.refs_1_ = f32[512,1536]{1,0:T(8,128)S(1)} custom-call(bf16[512,256]{1,0:T(8,128)(2,1)S(1)} %collective-permute-done.11.refs_0_, f32[512,1536]{1,0:T(8,128)S(1)} %back.5.refs_1_, bf16[3,1536,768]{2,1,0:T(8,128)(2,1)S(1)} %copy-done, f32[512,1536]{1,0:T(8,128)S(1)} %slope.1.refs_5_.refs_3_, bf16[128,1536]{1,0:T(8,128)(2,1)S(1)} %bitcast.4), custom_call_target="tpu_custom_call" | custom-call | flops 6291456 | bytes 98304 | tf_op jit(solution)/shard_map/settle/pallas_call | solution.py:84
  58.1 1.8 %collective-permute-done.10.refs_0_ = bf16[512,256]{1,0:T(8,128)(2,1)S(1)} collective-permute-done((bf16[512,256]{1,0:T(8,128)(2,1)S(1)}, bf16[512,256]{1,0:T(8,128)(2,1)S(1)}, u32[]{:S(2)}, u32[]{:S(2)}) %collective-permute-start.10) | collective-permute-done | bytes 262176 | tf_op jit(solution)/shard_map/ppermute | solution.py:480
  59.8 1.5 %final.1 = bf16[512,1536]{1,0:T(8,128)(2,1)} custom-call(bf16[512,256]{1,0:T(8,128)(2,1)S(1)} %collective-permute-done.10.refs_0_, f32[512,1536]{1,0:T(8,128)S(1)} %settle.1.refs_1_, bf16[3,1536,768]{2,1,0:T(8,128)(2,1)S(1)} %copy-done, f32[512,1536]{1,0:T(8,128)S(1)} %slope.1.refs_5_.refs_3_), custom_call_target="tpu_custom_call" | custom-call | flops 6291456 | bytes 98304 | tf_op jit(solution)/shard_map/final/pallas_call | solution.py:439
  (29 shorter events, 2.7 us)
Async XLA Ops:
  0.6 5.1 %copy-start = (bf16[3,1536,768]{2,1,0:T(8,128)(2,1)S(1)}, bf16[3,1536,768]{2,1,0:T(8,128)(2,1)}, u32[]{:S(2)}) copy-start(bf16[3,1536,768]{2,1,0:T(8,128)(2,1)} %refs_2_.8) | copy-start | bytes 21233668
  3.7 10.3 %collective-permute-start = (bf16[512,256]{1,0:T(8,128)(2,1)S(1)}, bf16[512,256]{1,0:T(8,128)(2,1)S(1)}, u32[]{:S(2)}, u32[]{:S(2)}) collective-permute-start(bf16[512,256]{1,0:T(8,128)(2,1)S(1)} %get-tuple-element.30), channel_id=1, source_target_pairs={{2,6},{3,7},{4,0},{5,1},{6,10},{7,11},{8,4},{9,5},{10,14},{11,15},... | collective-permute-start | bytes 786440 | tf_op jit(solution)/shard_map/ppermute | solution.py:480
  9.1 10.2 %collective-permute-start.2 = (bf16[512,256]{1,0:T(8,128)(2,1)S(1)}, bf16[512,256]{1,0:T(8,128)(2,1)S(1)}, u32[]{:S(2)}, u32[]{:S(2)}) collective-permute-start(bf16[512,256]{1,0:T(8,128)(2,1)S(1)} %side.2.refs_2_), channel_id=1, source_target_pairs={{2,6},{3,7},{4,0},{5,1},{6,10},{7,11},{8,4},{9,5},{10,14},{11,15},... | collective-permute-start | bytes 786440 | tf_op jit(solution)/shard_map/ppermute | solution.py:480
  14.0 9.4 %copy-start.1 = (bf16[768,1536]{1,0:T(8,128)(2,1)S(1)}, bf16[768,1536]{1,0:T(8,128)(2,1)}, u32[]{:S(2)}) copy-start(bf16[768,1536]{1,0:T(8,128)(2,1)} %refs_4_.1) | copy-start | bytes 7077892
  14.0 9.4 %copy-start.2 = (bf16[2,64,1536]{2,1,0:T(8,128)(2,1)S(1)}, bf16[2,64,1536]{2,1,0:T(8,128)(2,1)}, u32[]{:S(2)}) copy-start(bf16[2,64,1536]{2,1,0:T(8,128)(2,1)} %param.10) | copy-start | bytes 1179652
  14.1 10.3 %collective-permute-start.1 = (bf16[512,256]{1,0:T(8,128)(2,1)S(1)}, bf16[512,256]{1,0:T(8,128)(2,1)S(1)}, u32[]{:S(2)}, u32[]{:S(2)}) collective-permute-start(bf16[512,256]{1,0:T(8,128)(2,1)S(1)} %join.3.refs_2_), channel_id=1, source_target_pairs={{0,2},{1,3},{2,0},{3,1},{4,6},{5,7},{6,4},{7,5},{8,10},{9,11},{10,... | collective-permute-start | bytes 786440 | tf_op jit(solution)/shard_map/ppermute | solution.py:480
  16.4 7.9 %copy-start.3 = (f32[768]{0:T(1024)S(1)}, f32[768]{0:T(1024)}, u32[]{:S(2)}) copy-start(f32[768]{0:T(1024)} %refs_2_.6) | copy-start | bytes 9220
  16.4 7.9 %copy-start.4 = (f32[768]{0:T(1024)S(1)}, f32[768]{0:T(1024)}, u32[]{:S(2)}) copy-start(f32[768]{0:T(1024)} %refs_3_.3) | copy-start | bytes 9220
  16.4 9.1 %collective-permute-start.4 = (bf16[512,256]{1,0:T(8,128)(2,1)S(1)}, bf16[512,256]{1,0:T(8,128)(2,1)S(1)}, u32[]{:S(2)}, u32[]{:S(2)}) collective-permute-start(bf16[512,256]{1,0:T(8,128)(2,1)S(1)} %side.3.refs_2_), channel_id=1, source_target_pairs={{2,6},{3,7},{4,0},{5,1},{6,10},{7,11},{8,4},{9,5},{10,14},{11,15},... | collective-permute-start | bytes 786440 | tf_op jit(solution)/shard_map/ppermute | solution.py:480
  19.4 8.2 %copy-start.5 = (f32[1536]{0:T(1024)S(1)}, f32[1536]{0:T(1024)}, u32[]{:S(2)}) copy-start(f32[1536]{0:T(1024)} %refs_1_.5) | copy-start | bytes 18436
  19.4 8.2 %copy-start.6 = (f32[1536]{0:T(1024)S(1)}, f32[1536]{0:T(1024)}, u32[]{:S(2)}) copy-start(f32[1536]{0:T(1024)} %refs_2_.3) | copy-start | bytes 18436
  19.4 11.1 %collective-permute-start.3 = (bf16[512,256]{1,0:T(8,128)(2,1)S(1)}, bf16[512,256]{1,0:T(8,128)(2,1)S(1)}, u32[]{:S(2)}, u32[]{:S(2)}) collective-permute-start(bf16[512,256]{1,0:T(8,128)(2,1)S(1)} %join.4.refs_2_), channel_id=1, source_target_pairs={{0,2},{1,3},{2,0},{3,1},{4,6},{5,7},{6,4},{7,5},{8,10},{9,11},{10,... | collective-permute-start | bytes 786440 | tf_op jit(solution)/shard_map/ppermute | solution.py:480
  25.1 11.1 %collective-permute-start.6 = (bf16[512,256]{1,0:T(8,128)(2,1)S(1)}, bf16[512,256]{1,0:T(8,128)(2,1)S(1)}, u32[]{:S(2)}, u32[]{:S(2)}) collective-permute-start(bf16[512,256]{1,0:T(8,128)(2,1)S(1)} %get-tuple-element.42.refs_2_.refs_0_), channel_id=1, source_target_pairs={{0,2},{1,3},{2,0},{3,1},{4,6},{5,7},{6,4},{7,5},{8,10},{9,11},{10,... | collective-permute-start | bytes 786440 | tf_op jit(solution)/shard_map/ppermute | solution.py:480
  25.6 16.1 %collective-permute-start.5 = (bf16[512,256]{1,0:T(8,128)(2,1)S(1)}, bf16[512,256]{1,0:T(8,128)(2,1)S(1)}, u32[]{:S(2)}, u32[]{:S(2)}) collective-permute-start(bf16[512,256]{1,0:T(8,128)(2,1)S(1)} %join.5.refs_3_), channel_id=1, source_target_pairs={{0,2},{1,3},{2,0},{3,1},{4,6},{5,7},{6,4},{7,5},{8,10},{9,11},{10,... | collective-permute-start | bytes 786440 | tf_op jit(solution)/shard_map/ppermute | solution.py:480
  29.5 3.9 %copy-start.7 = (f32[1536]{0:T(1024)S(1)}, f32[1536]{0:T(1024)}, u32[]{:S(2)}) copy-start(f32[1536]{0:T(1024)} %refs_1_.6) | copy-start | bytes 18436
  31.2 15.9 %collective-permute-start.9 = (bf16[512,256]{1,0:T(8,128)(2,1)S(1)}, bf16[512,256]{1,0:T(8,128)(2,1)S(1)}, u32[]{:S(2)}, u32[]{:S(2)}) collective-permute-start(bf16[512,256]{1,0:T(8,128)(2,1)S(1)} %get-tuple-element.46.refs_2_.refs_1_), channel_id=1, source_target_pairs={{0,2},{1,3},{2,0},{3,1},{4,6},{5,7},{6,4},{7,5},{8,10},{9,11},{10,... | collective-permute-start | bytes 786440 | tf_op jit(solution)/shard_map/ppermute | solution.py:480
  36.1 14.5 %collective-permute-start.8 = (bf16[512,256]{1,0:T(8,128)(2,1)S(1)}, bf16[512,256]{1,0:T(8,128)(2,1)S(1)}, u32[]{:S(2)}, u32[]{:S(2)}) collective-permute-start(bf16[512,256]{1,0:T(8,128)(2,1)S(1)} %collective-permute-done.6.refs_0_), channel_id=1, source_target_pairs={{0,4},{1,5},{4,8},{5,9},{6,2},{7,3},{8,12},{9,13},{10,6},{11,7},{1... | collective-permute-start | bytes 786440 | tf_op jit(solution)/shard_map/ppermute | solution.py:480
  42.5 8.1 %collective-permute-start.7 = (bf16[512,256]{1,0:T(8,128)(2,1)S(1)}, bf16[512,256]{1,0:T(8,128)(2,1)S(1)}, u32[]{:S(2)}, u32[]{:S(2)}) collective-permute-start(bf16[512,256]{1,0:T(8,128)(2,1)S(1)} %get-tuple-element.50.refs_0_), channel_id=1, source_target_pairs={{0,2},{1,3},{2,0},{3,1},{4,6},{5,7},{6,4},{7,5},{8,10},{9,11},{10,... | collective-permute-start | bytes 786440 | tf_op jit(solution)/shard_map/ppermute | solution.py:480
  47.1 9.9 %collective-permute-start.11 = (bf16[512,256]{1,0:T(8,128)(2,1)S(1)}, bf16[512,256]{1,0:T(8,128)(2,1)S(1)}, u32[]{:S(2)}, u32[]{:S(2)}) collective-permute-start(bf16[512,256]{1,0:T(8,128)(2,1)S(1)} %collective-permute-done.9.refs_1_.refs_2_), channel_id=1, source_target_pairs={{0,4},{1,5},{4,8},{5,9},{6,2},{7,3},{8,12},{9,13},{10,6},{11,7},{1... | collective-permute-start | bytes 786440 | tf_op jit(solution)/shard_map/ppermute | solution.py:480
  50.6 9.2 %collective-permute-start.10 = (bf16[512,256]{1,0:T(8,128)(2,1)S(1)}, bf16[512,256]{1,0:T(8,128)(2,1)S(1)}, u32[]{:S(2)}, u32[]{:S(2)}) collective-permute-start(bf16[512,256]{1,0:T(8,128)(2,1)S(1)} %collective-permute-done.7.refs_3_), channel_id=1, source_target_pairs={{0,4},{1,5},{4,8},{5,9},{6,2},{7,3},{8,12},{9,13},{10,6},{11,7},{1... | collective-permute-start | bytes 786440 | tf_op jit(solution)/shard_map/ppermute | solution.py:480

commit v4 on v3

--- a/solution.py
+++ b/solution.py
@@ -172,6 +172,21 @@
     )
 
 
+def near_side_body(which, stride, a_ref, w_ref, o_ref):
+    o_ref[...] = dot_nn(a_ref[...], w_ref[near_tap(stride), :, bounds(which)]).astype(BF16)
+
+
+def near_side(act, taps, which, stride):
+    rows, width = act.shape
+    return local_call(
+        functools.partial(near_side_body, which, stride),
+        "near_side",
+        [act, taps],
+        ((rows, SPLITS[which]), BF16),
+        (2 * rows * width * SPLITS[which], 2 * rows * width, 0),
+    )
+
+
 def keep_body(stride, which, a_ref, w_ref, *outs):
     for n, out in zip(which, outs):
         out[...] = dot_nn(a_ref[...], w_ref[near_tap(stride), :, bounds(n)])
@@ -189,19 +204,19 @@
     )
 
 
-def centre_body(a_ref, w_ref, *outs):
-    for n, out in enumerate(outs):
+def centre_body(which, a_ref, w_ref, *outs):
+    for n, out in zip(which, outs):
         out[...] = dot_nn(a_ref[...], w_ref[1, :, bounds(n)])
 
 
-def centre(act, taps, after):
+def centre(act, taps, which, after):
     rows, width = act.shape
     return local_call(
-        centre_body,
+        functools.partial(centre_body, which),
         "centre",
         [act, taps],
-        [((rows, c), F32) for c in SPLITS],
-        (2 * rows * width * sum(SPLITS), 2 * rows * width, 0),
+        [((rows, SPLITS[n]), F32) for n in which],
+        (2 * rows * width * sum(SPLITS[n] for n in which), 2 * rows * width, 0),
         after=after,
     )
 
@@ -240,7 +255,9 @@
     )
 
 
-def middle_body(which, t_ref, p_ref, s_ref, b_ref, hg_ref, g_ref, h_ref, wide_ref):
+def middle_body(count, which, *refs):
+    parts = refs[:count]
+    p_ref, s_ref, b_ref, hg_ref, g_ref, h_ref, wide_ref = refs[count:]
     bins, width = hg_ref.shape
     for lane in range(width // LANES):
         columns = slice(lane * LANES, lane * LANES + LANES)
@@ -252,19 +269,21 @@
     for lane in range(width // LANES):
         columns = slice(lane * LANES, lane * LANES + LANES)
         among = slice(first + lane * LANES, first + lane * LANES + LANES)
-        mid = p_ref[:, columns] + t_ref[:, columns].astype(F32)
+        mid = p_ref[:, columns]
+        for part in parts:
+            mid = mid + part[:, columns].astype(F32)
         scale = scales[:, among]
         value, slope = gelu_both(mid * scale + shifts[:, among])
         g_ref[:, columns] = (wide_ref[lane] * slope * scale).astype(BF16)
         h_ref[:, columns] = value.astype(BF16)
 
 
-def middle(part, centre_part, which, scale, shift, hidden_grads, after=()):
+def middle(parts, centre_part, which, scale, shift, hidden_grads, after=()):
     rows, mid = centre_part.shape
     return local_call(
-        functools.partial(middle_body, which),
+        functools.partial(middle_body, len(parts), which),
         "middle",
-        [part, centre_part, scale, shift, hidden_grads],
+        [*parts, centre_part, scale, shift, hidden_grads],
         [((rows, mid), BF16), ((rows, mid), BF16)],
         (30 * rows * mid, 12 * rows * mid, rows * mid),
         scratch=[pltpu.VMEM((mid // LANES, rows, LANES), F32)],
@@ -482,6 +501,9 @@
     def swap(value):
         return block_permute(value, lambda b: b ^ 1)
 
+    def across(value):
+        return block_permute(value, lambda b: b + 1 if b % 2 else b - 1)
+
     def inward(value):
         return block_permute(value, lambda b: b + 2 if b % 2 else b - 2)
 
@@ -492,48 +514,44 @@
     binned = pooled_grad.reshape(-1, width)
     x, far_tap, act, sent0 = front(flat, scale_in, shift_in, tap_weight_stack, stride)
     taps = lax.optimization_barrier((tap_weight_stack, sent0))[0]
-    came0 = inward(sent0)
-    def later_than(value, *others):
-        return lax.optimization_barrier((value, *others))[0]
-
-    kept0, kept1, kept2 = keep(act, taps, [0, 1, 2], stride)
-    own = centre(act, taps, [kept0])
-    sent1 = side(act, far_tap, 1, [own[0]])
+    far_part0 = across(sent0)
+    near_side0 = near_side(act, taps, 0, stride)
+    near_part0 = swap(near_side0)
+    sent1 = side(act, far_tap, 1, [near_side0])
     came1 = inward(sent1)
-    joined0 = join(kept0, came0, [sent1])
-    mids0 = swap(joined0)
-    sent2 = side(act, far_tap, 2, [joined0])
+    own0, own1, own2 = centre(act, taps, [0, 1, 2], [sent1])
+    hg = hidden_grad(binned, out_weight, [own0])
+    kept1, kept2 = keep(act, taps, [1, 2], stride, [hg[0]])
+    grad0, hid0 = middle(
+        [near_part0, far_part0], own0, 0, scale_mid, shift_mid, hg[0], [kept1]
+    )
+    near0 = swap(grad0)
+    sent2 = side(act, far_tap, 2, [grad0])
     came2 = inward(sent2)
     joined1 = join(kept1, came1, [sent2])
     mids1 = swap(joined1)
-    hg = hidden_grad(binned, out_weight, [joined1])
-    grad0, hid0 = middle(mids0, own[0], 0, scale_mid, shift_mid, hg[0])
-    near0 = swap(grad0)
-    joined2 = join(kept2, came2, [grad0])
+    slope = slope_in(x, scale_in, shift_in, [joined1])
+    total = back(None, [("own", 0, grad0), ("near", 0, near0)], taps, stride, [slope])
+    joined2 = join(kept2, came2, [total])
     mids2 = swap(joined2)
-    slope = slope_in(x, scale_in, shift_in, [joined2])
-    grad1, hid1 = middle(mids1, own[1], 1, scale_mid, shift_mid, hg[1], [slope])
+    base = pooled_base(x, out_bias, [joined2])
+    grad1, hid1 = middle([mids1], own1, 1, scale_mid, shift_mid, hg[1], [base])
     near1 = swap(grad1)
-    base = pooled_base(x, out_bias, [grad1])
-    total = back(None, [("own", 0, grad0), ("own", 1, grad1)], taps, stride, [base])
-    near0 = later_than(near0, total)
     far0 = outward(near0)
-    total = back(total, [("near", 0, near0)], taps, stride)
-    grad2, hid2 = middle(mids2, own[2], 2, scale_mid, shift_mid, hg[2], [total])
+    grad2, hid2 = middle([mids2], own2, 2, scale_mid, shift_mid, hg[2], [grad1])
     near2 = swap(grad2)
+    far2 = across(grad2)
     pooled, mean2 = pooled_out(base, [hid0, hid1, hid2], out_weight, batch)
-    near1, mean2 = lax.optimization_barrier((near1, mean2))
-    far1 = outward(near1)
-    mark = touch(far0, near1, [mean2])
-    near2, mark = lax.optimization_barrier((near2, mark))
-    far2 = outward(near2)
     total = back(
         total,
-        [("own", 2, grad2), ("far", 0, far0), ("near", 1, near1), ("near", 2, near2)],
+        [("own", 1, grad1), ("own", 2, grad2), ("far", 0, far0)],
         taps,
         stride,
-        [mark],
-    )
+        [mean2],
+    )
+    near1, total = lax.optimization_barrier((near1, total))
+    far1 = outward(near1)
+    total = back(total, [("near", 1, near1), ("near", 2, near2)], taps, stride)
     settled = settle(total, [("far", 1, far1)], taps, slope, binned, stride)
     out = final(settled, [("far", 2, far2)], taps, slope, stride)
     return pooled, out.reshape(seqs_in.shape)

time: 62.3 us -> 60.6 us (0.973)
  starting transfers between devices: 28.6 us -> 22.8 us
  waiting for transfers between devices: 11.6 us -> 14.9 us
  local copies, waits for them, and re-layouts: 0.04 us -> 1.23 us
    ppermute x12, starting transfers between devices: 28.6 us -> 22.8 us  [block_permute(): return lax.ppermute(value, AXIS, pairs)]
    ppermute x12, waiting for transfers between devices: 11.6 us -> 14.9 us  [block_permute(): return lax.ppermute(value, AXIS, pairs)]
    unnamed x16, local copies, waits for them, and re-layouts: 0.04 us -> 1.23 us
    pallas_call x18 -> x17, Pallas kernels: 13.9 us -> 14.1 us  [local_call(): pl.pallas_call(body, name=name, in_specs=[space] * len(operands), out_spe...]
  transfers between devices with their start and end apart: 12 -> 12, of which waited for: 9 -> 6; matrix products, arithmetic and copies ran while one was open for 0% -> 0% of each run, Pallas kernels for 25% -> 25%
where the time goes in v4:
time: 60.6 us; the launch traced here: 60.4 us
  starting transfers between devices  22.8 us (38%)
  Pallas kernels  20.4 us (34%)
  waiting for transfers between devices  14.9 us (25%)
  local copies, waits for them, and re-layouts  1.23 us (2%)
  between operations  1.09 us (2%)
    ppermute x12, starting transfers between devices, block_permute(): return lax.ppermute(value, AXIS, pairs)  22.8 us
    ppermute x12, waiting for transfers between devices, block_permute(): return lax.ppermute(value, AXIS, pairs)  14.9 us
    pallas_call x17, Pallas kernels, local_call(): pl.pallas_call(body, name=name, in_specs=[space] * len(operands), out_spe...  14.1 us
    pallas_call x1, Pallas kernels, front(): pl.pallas_call(functools.partial(front_body, stride), name='front', in_sp...  3.03 us
    pallas_call x1, Pallas kernels, pooled_out(): pl.pallas_call(pooled_body, name='pooled', in_specs=[pl.BlockSpec(memory_...  1.73 us
    pallas_call x1, Pallas kernels, final(): pl.pallas_call(functools.partial(final_body, stride, kinds, tiles), name=...  1.54 us
    unnamed x16, local copies, waits for them, and re-layouts  1.23 us
  transfers between devices with their start and end apart: 12, of which 6 were waited for; matrix products, arithmetic and copies ran while one was open for 0% of the time, Pallas kernels for 25%

profile of v4, /device:TPU:8, one launch (start us, length us, event | category | flops | bytes accessed | tf_op | source)
XLA Modules:
  0.0 60.4 jit_solution(783317325335983614)
XLA Ops:
  0.6 3.0 %front.1 = (bf16[512,1536]{1,0:T(8,128)(2,1)S(1)}, bf16[1536,768]{1,0:T(8,128)(2,1)S(1)}, bf16[512,1536]{1,0:T(8,128)(2,1)S(1)}, bf16[512,256]{1,0:T(8,128)(2,1)S(1)}) custom-call(bf16[512,1536]{1,0:T(8,128)(2,1)} %bitcast.6, f32[1536]{0:T(1024)} %refs_1_.6, f32[1536]{0:T(1024)} %refs_2_.3, bf16[3,1536,768]{2,1,0:T(8,128)(2,1)} %refs_2_.9), custom_call_target="tpu_custom_call" | custom-call | flops 6291456 | bytes 135168 | tf_op jit(solution)/shard_map/front/pallas_call | solution.py:138
  3.7 1.2 %copy-done = bf16[3,1536,768]{2,1,0:T(8,128)(2,1)S(1)} copy-done((bf16[3,1536,768]{2,1,0:T(8,128)(2,1)S(1)}, bf16[3,1536,768]{2,1,0:T(8,128)(2,1)}, u32[]{:S(2)}) %copy-start) | copy-done | bytes 7077912
  4.9 0.6 near_side.1.refs_2_
  5.4 1.6 %collective-permute-start = (bf16[512,256]{1,0:T(8,128)(2,1)S(1)}, bf16[512,256]{1,0:T(8,128)(2,1)S(1)}, u32[]{:S(2)}, u32[]{:S(2)}) collective-permute-start(bf16[512,256]{1,0:T(8,128)(2,1)S(1)} %near_side.1.refs_2_), channel_id=1, source_target_pairs={{0,2},{1,3},{2,0},{3,1},{4,6},{5,7},{6,4},{7,5},{8,10},{9,11},{10,... | collective-permute-start | bytes 786440 | tf_op jit(solution)/shard_map/ppermute | solution.py:499
  7.0 1.9 %collective-permute-start.1 = (bf16[512,256]{1,0:T(8,128)(2,1)S(1)}, bf16[512,256]{1,0:T(8,128)(2,1)S(1)}, u32[]{:S(2)}, u32[]{:S(2)}) collective-permute-start(bf16[512,256]{1,0:T(8,128)(2,1)S(1)} %get-tuple-element.26), channel_id=1, source_target_pairs={{2,4},{3,5},{4,2},{5,3},{6,8},{7,9},{8,6},{9,7},{10,12},{11,13},{1... | collective-permute-start | bytes 786440 | tf_op jit(solution)/shard_map/ppermute | solution.py:499
  8.9 0.6 side.2.refs_2_
  9.5 2.2 %collective-permute-start.2 = (bf16[512,256]{1,0:T(8,128)(2,1)S(1)}, bf16[512,256]{1,0:T(8,128)(2,1)S(1)}, u32[]{:S(2)}, u32[]{:S(2)}) collective-permute-start(bf16[512,256]{1,0:T(8,128)(2,1)S(1)} %side.2.refs_2_), channel_id=1, source_target_pairs={{2,6},{3,7},{4,0},{5,1},{6,10},{7,11},{8,4},{9,5},{10,14},{11,15},... | collective-permute-start | bytes 786440 | tf_op jit(solution)/shard_map/ppermute | solution.py:499
  11.7 1.4 %centre.1 = (f32[512,256]{1,0:T(8,128)S(1)}, f32[512,256]{1,0:T(8,128)S(1)}, f32[512,256]{1,0:T(8,128)S(1)}) custom-call(bf16[512,1536]{1,0:T(8,128)(2,1)S(1)} %get-tuple-element.25.a_ref.refs_0_, bf16[3,1536,768]{2,1,0:T(8,128)(2,1)S(1)} %copy-done, bf16[512,256]{1,0:T(8,128)(2,1)S(1)} %side.2.refs_2_), custom_call_target="tpu_custom_call" | custom-call | flops 18874368 | bytes 24576 | tf_op jit(solution)/shard_map/centre/pallas_call | solution.py:84
  13.1 0.9 %hidden_grad.1 = (f32[128,256]{1,0:T(8,128)S(1)}, f32[128,256]{1,0:T(8,128)S(1)}, f32[128,256]{1,0:T(8,128)S(1)}) custom-call(bf16[128,1536]{1,0:T(8,128)(2,1)S(1)} %bitcast.3, bf16[768,1536]{1,0:T(8,128)(2,1)S(1)} %copy-done.1, f32[512,256]{1,0:T(8,128)S(1)} %get-tuple-element.29.refs_2_), custom_call_target="tpu_custom_call" | custom-call | flops 4718592 | bytes 6144 | tf_op jit(solution)/shard_map/hidden_grad/pallas_call | solution.py:84
  14.0 1.0 %keep.1 = (f32[512,256]{1,0:T(8,128)S(1)}, f32[512,256]{1,0:T(8,128)S(1)}) custom-call(bf16[512,1536]{1,0:T(8,128)(2,1)S(1)} %get-tuple-element.25.a_ref.refs_0_, bf16[3,1536,768]{2,1,0:T(8,128)(2,1)S(1)} %copy-done, f32[128,256]{1,0:T(8,128)S(1)} %get-tuple-element.30.refs_2_.refs_5_), custom_call_target="tpu_custom_call" | custom-call | flops 12582912 | bytes 24576 | tf_op jit(solution)/shard_map/keep/pallas_call | solution.py:84
  15.0 4.1 %collective-permute-done.refs_0_ = bf16[512,256]{1,0:T(8,128)(2,1)S(1)} collective-permute-done((bf16[512,256]{1,0:T(8,128)(2,1)S(1)}, bf16[512,256]{1,0:T(8,128)(2,1)S(1)}, u32[]{:S(2)}, u32[]{:S(2)}) %collective-permute-start) | collective-permute-done | bytes 262176 | tf_op jit(solution)/shard_map/ppermute | solution.py:499
  19.2 0.8 %middle.3 = (bf16[512,256]{1,0:T(8,128)(2,1)S(1)}, bf16[512,256]{1,0:T(8,128)(2,1)S(1)}) custom-call(bf16[512,256]{1,0:T(8,128)(2,1)S(1)} %collective-permute-done.refs_0_, bf16[512,256]{1,0:T(8,128)(2,1)S(1)} %collective-permute-done.1.refs_1_, f32[512,256]{1,0:T(8,128)S(1)} %get-tuple-element.29.refs_2_, f32[768]{0:T(1024)S(1)} %copy-done.3, ...), custom_call_target="tpu_custom_call" | custom-call | flops 61440 | bytes 24576 | tf_op jit(solution)/shard_map/middle/pallas_call | solution.py:84
  20.0 1.6 %collective-permute-start.5 = (bf16[512,256]{1,0:T(8,128)(2,1)S(1)}, bf16[512,256]{1,0:T(8,128)(2,1)S(1)}, u32[]{:S(2)}, u32[]{:S(2)}) collective-permute-start(bf16[512,256]{1,0:T(8,128)(2,1)S(1)} %get-tuple-element.33.refs_2_.refs_0_), channel_id=1, source_target_pairs={{0,2},{1,3},{2,0},{3,1},{4,6},{5,7},{6,4},{7,5},{8,10},{9,11},{10,... | collective-permute-start | bytes 786440 | tf_op jit(solution)/shard_map/ppermute | solution.py:499
  22.1 2.4 %collective-permute-start.4 = (bf16[512,256]{1,0:T(8,128)(2,1)S(1)}, bf16[512,256]{1,0:T(8,128)(2,1)S(1)}, u32[]{:S(2)}, u32[]{:S(2)}) collective-permute-start(bf16[512,256]{1,0:T(8,128)(2,1)S(1)} %side.3.refs_2_), channel_id=1, source_target_pairs={{2,6},{3,7},{4,0},{5,1},{6,10},{7,11},{8,4},{9,5},{10,14},{11,15},... | collective-permute-start | bytes 786440 | tf_op jit(solution)/shard_map/ppermute | solution.py:499
  24.6 1.7 %collective-permute-start.3 = (bf16[512,256]{1,0:T(8,128)(2,1)S(1)}, bf16[512,256]{1,0:T(8,128)(2,1)S(1)}, u32[]{:S(2)}, u32[]{:S(2)}) collective-permute-start(bf16[512,256]{1,0:T(8,128)(2,1)S(1)} %join.2.refs_3_), channel_id=1, source_target_pairs={{0,2},{1,3},{2,0},{3,1},{4,6},{5,7},{6,4},{7,5},{8,10},{9,11},{10,... | collective-permute-start | bytes 786440 | tf_op jit(solution)/shard_map/ppermute | solution.py:499
  26.3 1.9 %slope.1.refs_3_ = f32[512,1536]{1,0:T(8,128)S(1)} custom-call(bf16[512,1536]{1,0:T(8,128)(2,1)S(1)} %get-tuple-element.36.refs_0_, f32[1536]{0:T(1024)S(1)} %copy-done.5, f32[1536]{0:T(1024)S(1)} %copy-done.6, bf16[512,256]{1,0:T(8,128)(2,1)S(1)} %join.2.refs_3_), custom_call_target="tpu_custom_call" | custom-call | flops 368640 | bytes 73728 | tf_op jit(solution)/shard_map/slope/pallas_call | solution.py:84
  28.2 1.0 %back.3.refs_2_.refs_4_ = f32[512,1536]{1,0:T(8,128)S(1)} custom-call(bf16[512,256]{1,0:T(8,128)(2,1)S(1)} %get-tuple-element.33.refs_2_.refs_0_, bf16[512,256]{1,0:T(8,128)(2,1)S(1)} %collective-permute-done.5.refs_1_, bf16[3,1536,768]{2,1,0:T(8,128)(2,1)S(1)} %copy-done, f32[512,1536]{1,0:T(8,128)S(1)} %slope.1.refs_3_), custom_call_target="tpu_custom_call" | custom-call | flops 12582912 | bytes 98304 | tf_op jit(solution)/shard_map/back/pallas_call | solution.py:84
  29.3 1.6 %collective-permute-done.4.refs_1_ = bf16[512,256]{1,0:T(8,128)(2,1)S(1)} collective-permute-done((bf16[512,256]{1,0:T(8,128)(2,1)S(1)}, bf16[512,256]{1,0:T(8,128)(2,1)S(1)}, u32[]{:S(2)}, u32[]{:S(2)}) %collective-permute-start.4) | collective-permute-done | bytes 262176 | tf_op jit(solution)/shard_map/ppermute | solution.py:499
  31.5 4.1 %collective-permute-start.9 = (bf16[512,256]{1,0:T(8,128)(2,1)S(1)}, bf16[512,256]{1,0:T(8,128)(2,1)S(1)}, u32[]{:S(2)}, u32[]{:S(2)}) collective-permute-start(bf16[512,256]{1,0:T(8,128)(2,1)S(1)} %collective-permute-done.5.refs_1_), channel_id=1, source_target_pairs={{0,4},{1,5},{4,8},{5,9},{6,2},{7,3},{8,12},{9,13},{10,6},{11,7},{1... | collective-permute-start | bytes 786440 | tf_op jit(solution)/shard_map/ppermute | solution.py:499
  36.0 0.7 %middle.4 = (bf16[512,256]{1,0:T(8,128)(2,1)S(1)}, bf16[512,256]{1,0:T(8,128)(2,1)S(1)}) custom-call(bf16[512,256]{1,0:T(8,128)(2,1)S(1)} %collective-permute-done.3.refs_0_, f32[512,256]{1,0:T(8,128)S(1)} %get-tuple-element.34.refs_1_, f32[768]{0:T(1024)S(1)} %copy-done.3, f32[768]{0:T(1024)S(1)} %copy-done.4, f32[128,256]{1,0:T(8,128)S(1)} %get-tuple-element.35.refs_4_, ...), custom_call_target="tpu_custom_call" | custom-call | flops 61440 | bytes 24576 | tf_op jit(solution)/shard_map/middle/pallas_call | solution.py:84
  36.8 3.4 %collective-permute-done.6.refs_0_ = bf16[512,256]{1,0:T(8,128)(2,1)S(1)} collective-permute-done((bf16[512,256]{1,0:T(8,128)(2,1)S(1)}, bf16[512,256]{1,0:T(8,128)(2,1)S(1)}, u32[]{:S(2)}, u32[]{:S(2)}) %collective-permute-start.6) | collective-permute-done | bytes 262176 | tf_op jit(solution)/shard_map/ppermute | solution.py:499
  40.3 0.7 %middle.5 = (bf16[512,256]{1,0:T(8,128)(2,1)S(1)}, bf16[512,256]{1,0:T(8,128)(2,1)S(1)}) custom-call(bf16[512,256]{1,0:T(8,128)(2,1)S(1)} %collective-permute-done.6.refs_0_, f32[512,256]{1,0:T(8,128)S(1)} %get-tuple-element.39.refs_1_, f32[768]{0:T(1024)S(1)} %copy-done.3, f32[768]{0:T(1024)S(1)} %copy-done.4, f32[128,256]{1,0:T(8,128)S(1)} %get-tuple-element.40.refs_4_, ...), custom_call_target="tpu_custom_call" | custom-call | flops 61440 | bytes 24576 | tf_op jit(solution)/shard_map/middle/pallas_call | solution.py:84
  41.0 1.4 %collective-permute-start.11 = (bf16[512,256]{1,0:T(8,128)(2,1)S(1)}, bf16[512,256]{1,0:T(8,128)(2,1)S(1)}, u32[]{:S(2)}, u32[]{:S(2)}) collective-permute-start(bf16[512,256]{1,0:T(8,128)(2,1)S(1)} %get-tuple-element.44.refs_1_), channel_id=1, source_target_pairs={{0,2},{1,3},{2,0},{3,1},{4,6},{5,7},{6,4},{7,5},{8,10},{9,11},{10,... | collective-permute-start | bytes 786440 | tf_op jit(solution)/shard_map/ppermute | solution.py:499
  42.3 1.7 %pooled.1 = (bf16[2,64,1536]{2,1,0:T(8,128)(2,1)}, bf16[16,128]{1,0:T(8,128)(2,1)S(1)}) custom-call(bf16[512,256]{1,0:T(8,128)(2,1)S(1)} %get-tuple-element.32.refs_0_, bf16[512,256]{1,0:T(8,128)(2,1)S(1)} %get-tuple-element.38.refs_1_, bf16[512,256]{1,0:T(8,128)(2,1)S(1)} %get-tuple-element.42.refs_2_, f32[128,1536]{1,0:T(8,128)S(1)} %pooled_base.1.refs_5_.refs_3_, ...), custom_call_target="tpu_custom_call" | custom-call | flops 4718592 | bytes 18432 | tf_op jit(solution)/shard_map/pooled/pallas_call | solution.py:339
  44.1 1.4 %back.4.refs_3_ = f32[512,1536]{1,0:T(8,128)S(1)} custom-call(bf16[512,256]{1,0:T(8,128)(2,1)S(1)} %get-tuple-element.41.refs_5_.refs_0_, bf16[512,256]{1,0:T(8,128)(2,1)S(1)} %get-tuple-element.44.refs_1_, bf16[512,256]{1,0:T(8,128)(2,1)S(1)} %collective-permute-done.9.refs_2_, bf16[3,1536,768]{2,1,0:T(8,128)(2,1)S(1)} %copy-done, ...), custom_call_target="tpu_custom_call" | custom-call | flops 18874368 | bytes 98304 | tf_op jit(solution)/shard_map/back/pallas_call | solution.py:84
  46.0 3.4 %collective-permute-start.10 = (bf16[512,256]{1,0:T(8,128)(2,1)S(1)}, bf16[512,256]{1,0:T(8,128)(2,1)S(1)}, u32[]{:S(2)}, u32[]{:S(2)}) collective-permute-start(bf16[512,256]{1,0:T(8,128)(2,1)S(1)} %collective-permute-done.8.refs_0_), channel_id=1, source_target_pairs={{0,4},{1,5},{4,8},{5,9},{6,2},{7,3},{8,12},{9,13},{10,6},{11,7},{1... | collective-permute-start | bytes 786440 | tf_op jit(solution)/shard_map/ppermute | solution.py:499
  49.5 1.9 %collective-permute-start.7 = (bf16[512,256]{1,0:T(8,128)(2,1)S(1)}, bf16[512,256]{1,0:T(8,128)(2,1)S(1)}, u32[]{:S(2)}, u32[]{:S(2)}) collective-permute-start(bf16[512,256]{1,0:T(8,128)(2,1)S(1)} %get-tuple-element.44.refs_1_), channel_id=1, source_target_pairs={{2,4},{3,5},{4,2},{5,3},{6,8},{7,9},{8,6},{9,7},{10,12},{11,13},{1... | collective-permute-start | bytes 786440 | tf_op jit(solution)/shard_map/ppermute | solution.py:499
  51.4 1.1 %back.5.refs_1_ = f32[512,1536]{1,0:T(8,128)S(1)} custom-call(bf16[512,256]{1,0:T(8,128)(2,1)S(1)} %collective-permute-done.8.refs_0_, bf16[512,256]{1,0:T(8,128)(2,1)S(1)} %collective-permute-done.11.refs_1_, bf16[3,1536,768]{2,1,0:T(8,128)(2,1)S(1)} %copy-done, f32[512,1536]{1,0:T(8,128)S(1)} %back.4.refs_3_), custom_call_target="tpu_custom_call" | custom-call | flops 12582912 | bytes 98304 | tf_op jit(solution)/shard_map/back/pallas_call | solution.py:84
  52.5 1.8 %collective-permute-done.10.refs_0_ = bf16[512,256]{1,0:T(8,128)(2,1)S(1)} collective-permute-done((bf16[512,256]{1,0:T(8,128)(2,1)S(1)}, bf16[512,256]{1,0:T(8,128)(2,1)S(1)}, u32[]{:S(2)}, u32[]{:S(2)}) %collective-permute-start.10) | collective-permute-done | bytes 262176 | tf_op jit(solution)/shard_map/ppermute | solution.py:499
  54.3 1.0 %settle.1.refs_1_ = f32[512,1536]{1,0:T(8,128)S(1)} custom-call(bf16[512,256]{1,0:T(8,128)(2,1)S(1)} %collective-permute-done.10.refs_0_, f32[512,1536]{1,0:T(8,128)S(1)} %back.5.refs_1_, bf16[3,1536,768]{2,1,0:T(8,128)(2,1)S(1)} %copy-done, f32[512,1536]{1,0:T(8,128)S(1)} %slope.1.refs_3_, bf16[128,1536]{1,0:T(8,128)(2,1)S(1)} %bitcast.4), custom_call_target="tpu_custom_call" | custom-call | flops 6291456 | bytes 98304 | tf_op jit(solution)/shard_map/settle/pallas_call | solution.py:84
  55.3 3.3 %collective-permute-done.7.refs_0_ = bf16[512,256]{1,0:T(8,128)(2,1)S(1)} collective-permute-done((bf16[512,256]{1,0:T(8,128)(2,1)S(1)}, bf16[512,256]{1,0:T(8,128)(2,1)S(1)}, u32[]{:S(2)}, u32[]{:S(2)}) %collective-permute-start.7) | collective-permute-done | bytes 262176 | tf_op jit(solution)/shard_map/ppermute | solution.py:499
  58.7 1.5 %final.1 = bf16[512,1536]{1,0:T(8,128)(2,1)} custom-call(bf16[512,256]{1,0:T(8,128)(2,1)S(1)} %collective-permute-done.7.refs_0_, f32[512,1536]{1,0:T(8,128)S(1)} %settle.1.refs_1_, bf16[3,1536,768]{2,1,0:T(8,128)(2,1)S(1)} %copy-done, f32[512,1536]{1,0:T(8,128)S(1)} %slope.1.refs_3_), custom_call_target="tpu_custom_call" | custom-call | flops 6291456 | bytes 98304 | tf_op jit(solution)/shard_map/final/pallas_call | solution.py:458
  (28 shorter events, 2.3 us)
Async XLA Ops:
  0.6 4.2 %copy-start = (bf16[3,1536,768]{2,1,0:T(8,128)(2,1)S(1)}, bf16[3,1536,768]{2,1,0:T(8,128)(2,1)}, u32[]{:S(2)}) copy-start(bf16[3,1536,768]{2,1,0:T(8,128)(2,1)} %refs_2_.9) | copy-start | bytes 21233668
  5.4 13.7 %collective-permute-start = (bf16[512,256]{1,0:T(8,128)(2,1)S(1)}, bf16[512,256]{1,0:T(8,128)(2,1)S(1)}, u32[]{:S(2)}, u32[]{:S(2)}) collective-permute-start(bf16[512,256]{1,0:T(8,128)(2,1)S(1)} %near_side.1.refs_2_), channel_id=1, source_target_pairs={{0,2},{1,3},{2,0},{3,1},{4,6},{5,7},{6,4},{7,5},{8,10},{9,11},{10,... | collective-permute-start | bytes 786440 | tf_op jit(solution)/shard_map/ppermute | solution.py:499
  7.0 12.1 %collective-permute-start.1 = (bf16[512,256]{1,0:T(8,128)(2,1)S(1)}, bf16[512,256]{1,0:T(8,128)(2,1)S(1)}, u32[]{:S(2)}, u32[]{:S(2)}) collective-permute-start(bf16[512,256]{1,0:T(8,128)(2,1)S(1)} %get-tuple-element.26), channel_id=1, source_target_pairs={{2,4},{3,5},{4,2},{5,3},{6,8},{7,9},{8,6},{9,7},{10,12},{11,13},{1... | collective-permute-start | bytes 786440 | tf_op jit(solution)/shard_map/ppermute | solution.py:499
  9.5 3.6 %copy-start.1 = (bf16[768,1536]{1,0:T(8,128)(2,1)S(1)}, bf16[768,1536]{1,0:T(8,128)(2,1)}, u32[]{:S(2)}) copy-start(bf16[768,1536]{1,0:T(8,128)(2,1)} %refs_4_.3) | copy-start | bytes 7077892
  9.5 3.6 %copy-start.2 = (bf16[2,64,1536]{2,1,0:T(8,128)(2,1)S(1)}, bf16[2,64,1536]{2,1,0:T(8,128)(2,1)}, u32[]{:S(2)}) copy-start(bf16[2,64,1536]{2,1,0:T(8,128)(2,1)} %param.10) | copy-start | bytes 1179652
  9.5 14.9 %collective-permute-start.2 = (bf16[512,256]{1,0:T(8,128)(2,1)S(1)}, bf16[512,256]{1,0:T(8,128)(2,1)S(1)}, u32[]{:S(2)}, u32[]{:S(2)}) collective-permute-start(bf16[512,256]{1,0:T(8,128)(2,1)S(1)} %side.2.refs_2_), channel_id=1, source_target_pairs={{2,6},{3,7},{4,0},{5,1},{6,10},{7,11},{8,4},{9,5},{10,14},{11,15},... | collective-permute-start | bytes 786440 | tf_op jit(solution)/shard_map/ppermute | solution.py:499
  14.0 5.1 %copy-start.3 = (f32[768]{0:T(1024)S(1)}, f32[768]{0:T(1024)}, u32[]{:S(2)}) copy-start(f32[768]{0:T(1024)} %refs_2_.6) | copy-start | bytes 9220
  14.0 5.1 %copy-start.4 = (f32[768]{0:T(1024)S(1)}, f32[768]{0:T(1024)}, u32[]{:S(2)}) copy-start(f32[768]{0:T(1024)} %refs_3_.5) | copy-start | bytes 9220
  19.9 6.3 %copy-start.5 = (f32[1536]{0:T(1024)S(1)}, f32[1536]{0:T(1024)}, u32[]{:S(2)}) copy-start(f32[1536]{0:T(1024)} %refs_1_.6) | copy-start | bytes 18436
  19.9 6.3 %copy-start.6 = (f32[1536]{0:T(1024)S(1)}, f32[1536]{0:T(1024)}, u32[]{:S(2)}) copy-start(f32[1536]{0:T(1024)} %refs_2_.3) | copy-start | bytes 18436
  20.0 8.3 %collective-permute-start.5 = (bf16[512,256]{1,0:T(8,128)(2,1)S(1)}, bf16[512,256]{1,0:T(8,128)(2,1)S(1)}, u32[]{:S(2)}, u32[]{:S(2)}) collective-permute-start(bf16[512,256]{1,0:T(8,128)(2,1)S(1)} %get-tuple-element.33.refs_2_.refs_0_), channel_id=1, source_target_pairs={{0,2},{1,3},{2,0},{3,1},{4,6},{5,7},{6,4},{7,5},{8,10},{9,11},{10,... | collective-permute-start | bytes 786440 | tf_op jit(solution)/shard_map/ppermute | solution.py:499
  22.1 8.8 %collective-permute-start.4 = (bf16[512,256]{1,0:T(8,128)(2,1)S(1)}, bf16[512,256]{1,0:T(8,128)(2,1)S(1)}, u32[]{:S(2)}, u32[]{:S(2)}) collective-permute-start(bf16[512,256]{1,0:T(8,128)(2,1)S(1)} %side.3.refs_2_), channel_id=1, source_target_pairs={{2,6},{3,7},{4,0},{5,1},{6,10},{7,11},{8,4},{9,5},{10,14},{11,15},... | collective-permute-start | bytes 786440 | tf_op jit(solution)/shard_map/ppermute | solution.py:499
  24.6 11.5 %collective-permute-start.3 = (bf16[512,256]{1,0:T(8,128)(2,1)S(1)}, bf16[512,256]{1,0:T(8,128)(2,1)S(1)}, u32[]{:S(2)}, u32[]{:S(2)}) collective-permute-start(bf16[512,256]{1,0:T(8,128)(2,1)S(1)} %join.2.refs_3_), channel_id=1, source_target_pairs={{0,2},{1,3},{2,0},{3,1},{4,6},{5,7},{6,4},{7,5},{8,10},{9,11},{10,... | collective-permute-start | bytes 786440 | tf_op jit(solution)/shard_map/ppermute | solution.py:499
  29.3 6.3 %copy-start.7 = (f32[1536]{0:T(1024)S(1)}, f32[1536]{0:T(1024)}, u32[]{:S(2)}) copy-start(f32[1536]{0:T(1024)} %refs_1_.7) | copy-start | bytes 18436
  30.9 9.3 %collective-permute-start.6 = (bf16[512,256]{1,0:T(8,128)(2,1)S(1)}, bf16[512,256]{1,0:T(8,128)(2,1)S(1)}, u32[]{:S(2)}, u32[]{:S(2)}) collective-permute-start(bf16[512,256]{1,0:T(8,128)(2,1)S(1)} %join.3.refs_2_), channel_id=1, source_target_pairs={{0,2},{1,3},{2,0},{3,1},{4,6},{5,7},{6,4},{7,5},{8,10},{9,11},{10,... | collective-permute-start | bytes 786440 | tf_op jit(solution)/shard_map/ppermute | solution.py:499
  31.5 12.6 %collective-permute-start.9 = (bf16[512,256]{1,0:T(8,128)(2,1)S(1)}, bf16[512,256]{1,0:T(8,128)(2,1)S(1)}, u32[]{:S(2)}, u32[]{:S(2)}) collective-permute-start(bf16[512,256]{1,0:T(8,128)(2,1)S(1)} %collective-permute-done.5.refs_1_), channel_id=1, source_target_pairs={{0,4},{1,5},{4,8},{5,9},{6,2},{7,3},{8,12},{9,13},{10,6},{11,7},{1... | collective-permute-start | bytes 786440 | tf_op jit(solution)/shard_map/ppermute | solution.py:499
  36.7 9.3 %collective-permute-start.8 = (bf16[512,256]{1,0:T(8,128)(2,1)S(1)}, bf16[512,256]{1,0:T(8,128)(2,1)S(1)}, u32[]{:S(2)}, u32[]{:S(2)}) collective-permute-start(bf16[512,256]{1,0:T(8,128)(2,1)S(1)} %get-tuple-element.41.refs_5_.refs_0_), channel_id=1, source_target_pairs={{0,2},{1,3},{2,0},{3,1},{4,6},{5,7},{6,4},{7,5},{8,10},{9,11},{10,... | collective-permute-start | bytes 786440 | tf_op jit(solution)/shard_map/ppermute | solution.py:499
  41.0 10.5 %collective-permute-start.11 = (bf16[512,256]{1,0:T(8,128)(2,1)S(1)}, bf16[512,256]{1,0:T(8,128)(2,1)S(1)}, u32[]{:S(2)}, u32[]{:S(2)}) collective-permute-start(bf16[512,256]{1,0:T(8,128)(2,1)S(1)} %get-tuple-element.44.refs_1_), channel_id=1, source_target_pairs={{0,2},{1,3},{2,0},{3,1},{4,6},{5,7},{6,4},{7,5},{8,10},{9,11},{10,... | collective-permute-start | bytes 786440 | tf_op jit(solution)/shard_map/ppermute | solution.py:499
  46.0 8.3 %collective-permute-start.10 = (bf16[512,256]{1,0:T(8,128)(2,1)S(1)}, bf16[512,256]{1,0:T(8,128)(2,1)S(1)}, u32[]{:S(2)}, u32[]{:S(2)}) collective-permute-start(bf16[512,256]{1,0:T(8,128)(2,1)S(1)} %collective-permute-done.8.refs_0_), channel_id=1, source_target_pairs={{0,4},{1,5},{4,8},{5,9},{6,2},{7,3},{8,12},{9,13},{10,6},{11,7},{1... | collective-permute-start | bytes 786440 | tf_op jit(solution)/shard_map/ppermute | solution.py:499
  49.5 9.2 %collective-permute-start.7 = (bf16[512,256]{1,0:T(8,128)(2,1)S(1)}, bf16[512,256]{1,0:T(8,128)(2,1)S(1)}, u32[]{:S(2)}, u32[]{:S(2)}) collective-permute-start(bf16[512,256]{1,0:T(8,128)(2,1)S(1)} %get-tuple-element.44.refs_1_), channel_id=1, source_target_pairs={{2,4},{3,5},{4,2},{5,3},{6,8},{7,9},{8,6},{9,7},{10,12},{11,13},{1... | collective-permute-start | bytes 786440 | tf_op jit(solution)/shard_map/ppermute | solution.py:499

commit v5 on v4

--- a/solution.py
+++ b/solution.py
@@ -99,7 +99,7 @@
     return slice(sum(SPLITS[:n]), sum(SPLITS[: n + 1]))
 
 
-def front_body(stride, x_hbm, s_hbm, b_hbm, w_hbm, x_ref, w_ref, a_ref, p_ref, s_ref, b_ref, sems):
+def front_body(stride, x_hbm, s_hbm, b_hbm, w_hbm, x_ref, a_ref, p_ref, w_ref, s_ref, b_ref, sems):
     rows, width = x_ref.shape
     slabs = 4
     slab = rows // slabs
@@ -113,7 +113,7 @@
         )
         for n in range(slabs)
     ]
-    taps = pltpu.make_async_copy(w_hbm.at[2 - near_tap(stride)], w_ref, sems.at[2 + slabs])
+    taps = pltpu.make_async_copy(w_hbm.at[near_tap(stride)], w_ref, sems.at[2 + slabs])
     for copy in copies:
         copy.start()
     taps.start()
@@ -139,14 +139,14 @@
         functools.partial(front_body, stride),
         name="front",
         in_specs=[far] * 4,
-        out_specs=[space] * 4,
+        out_specs=[space] * 3,
         out_shape=[
             pltpu.VMEM(x.shape, BF16),
-            pltpu.VMEM(taps.shape[1:], BF16),
             pltpu.VMEM((rows, width), BF16),
             pltpu.VMEM((rows, mid), BF16),
         ],
         scratch_shapes=[
+            pltpu.VMEM(taps.shape[1:], BF16),
             pltpu.VMEM((width,), F32),
             pltpu.VMEM((width,), F32),
             pltpu.SemaphoreType.DMA((7,)),
@@ -156,34 +156,19 @@
     )(*operands)
 
 
-def side_body(which, a_ref, w_ref, o_ref):
-    o_ref[...] = dot_nn(a_ref[...], w_ref[:, bounds(which)]).astype(BF16)
-
-
-def side(act, far_tap, which, after=()):
+def side_body(which, stride, a_ref, w_ref, o_ref):
+    o_ref[...] = dot_nn(a_ref[...], w_ref[2 - near_tap(stride), :, bounds(which)]).astype(BF16)
+
+
+def side(act, taps, which, stride, after=()):
     rows, width = act.shape
     return local_call(
-        functools.partial(side_body, which),
+        functools.partial(side_body, which, stride),
         "side",
-        [act, far_tap],
-        ((rows, SPLITS[which]), BF16),
-        (2 * rows * width * SPLITS[which], 2 * rows * width, 0),
-        after=after,
-    )
-
-
-def near_side_body(which, stride, a_ref, w_ref, o_ref):
-    o_ref[...] = dot_nn(a_ref[...], w_ref[near_tap(stride), :, bounds(which)]).astype(BF16)
-
-
-def near_side(act, taps, which, stride):
-    rows, width = act.shape
-    return local_call(
-        functools.partial(near_side_body, which, stride),
-        "near_side",
         [act, taps],
         ((rows, SPLITS[which]), BF16),
         (2 * rows * width * SPLITS[which], 2 * rows * width, 0),
+        after=after,
     )
 
 
@@ -512,21 +497,23 @@
 
     flat = seqs_in.reshape(batch * rows, width)
     binned = pooled_grad.reshape(-1, width)
-    x, far_tap, act, sent0 = front(flat, scale_in, shift_in, tap_weight_stack, stride)
-    taps = lax.optimization_barrier((tap_weight_stack, sent0))[0]
+    x, act, kept0 = front(flat, scale_in, shift_in, tap_weight_stack, stride)
+    taps, kept0 = lax.optimization_barrier((tap_weight_stack, kept0))
+    near_part0 = swap(kept0)
+    sent0 = side(act, taps, 0, stride)
     far_part0 = across(sent0)
-    near_side0 = near_side(act, taps, 0, stride)
-    near_part0 = swap(near_side0)
-    sent1 = side(act, far_tap, 1, [near_side0])
+    sent1 = side(act, taps, 1, stride, [sent0])
     came1 = inward(sent1)
     own0, own1, own2 = centre(act, taps, [0, 1, 2], [sent1])
     hg = hidden_grad(binned, out_weight, [own0])
     kept1, kept2 = keep(act, taps, [1, 2], stride, [hg[0]])
+    arrived = touch(near_part0, sent1, [kept1])
+    far_part0, arrived = lax.optimization_barrier((far_part0, arrived))
     grad0, hid0 = middle(
-        [near_part0, far_part0], own0, 0, scale_mid, shift_mid, hg[0], [kept1]
+        [near_part0, far_part0], own0, 0, scale_mid, shift_mid, hg[0], [arrived]
     )
     near0 = swap(grad0)
-    sent2 = side(act, far_tap, 2, [grad0])
+    sent2 = side(act, taps, 2, stride, [grad0])
     came2 = inward(sent2)
     joined1 = join(kept1, came1, [sent2])
     mids1 = swap(joined1)

time: 60.6 us -> 58.9 us (0.972)
  waiting for transfers between devices: 14.9 us -> 11.7 us
  starting transfers between devices: 22.8 us -> 24.8 us
  local copies, waits for them, and re-layouts: 1.23 us -> 0.05 us
    ppermute x12, waiting for transfers between devices: 14.9 us -> 11.7 us  [block_permute(): return lax.ppermute(value, AXIS, pairs)]
    ppermute x12, starting transfers between devices: 22.8 us -> 24.8 us  [block_permute(): return lax.ppermute(value, AXIS, pairs)]
    unnamed x16, local copies, waits for them, and re-layouts: 1.23 us -> 0.05 us
    pallas_call x17 -> x18, Pallas kernels: 14.1 us -> 14.1 us  [local_call(): pl.pallas_call(body, name=name, in_specs=[space] * len(operands), out_spe...]
  transfers between devices with their start and end apart: 12 -> 12, of which waited for: 6 -> 6; matrix products, arithmetic and copies ran while one was open for 0% -> 0% of each run, Pallas kernels for 25% -> 27%
where the time goes in v5:
time: 58.9 us; the launch traced here: 58.1 us
  starting transfers between devices  24.8 us (42%)
  Pallas kernels  20.4 us (35%)
  waiting for transfers between devices  11.7 us (20%)
  between operations  1.1 us (2%)
    ppermute x12, starting transfers between devices, block_permute(): return lax.ppermute(value, AXIS, pairs)  24.8 us
    pallas_call x18, Pallas kernels, local_call(): pl.pallas_call(body, name=name, in_specs=[space] * len(operands), out_spe...  14.1 us
    ppermute x12, waiting for transfers between devices, block_permute(): return lax.ppermute(value, AXIS, pairs)  11.7 us
    pallas_call x1, Pallas kernels, front(): pl.pallas_call(functools.partial(front_body, stride), name='front', in_sp...  3.02 us
    pallas_call x1, Pallas kernels, pooled_out(): pl.pallas_call(pooled_body, name='pooled', in_specs=[pl.BlockSpec(memory_...  1.73 us
    pallas_call x1, Pallas kernels, final(): pl.pallas_call(functools.partial(final_body, stride, kinds, tiles), name=...  1.54 us
  transfers between devices with their start and end apart: 12, of which 6 were waited for; matrix products, arithmetic and copies ran while one was open for 0% of the time, Pallas kernels for 27%

profile of v5, /device:TPU:8, one launch (start us, length us, event | category | flops | bytes accessed | tf_op | source)
XLA Modules:
  0.0 58.1 jit_solution(16950699074091748723)
XLA Ops:
  0.6 3.0 %front.1 = (bf16[512,1536]{1,0:T(8,128)(2,1)S(1)}, bf16[512,1536]{1,0:T(8,128)(2,1)S(1)}, bf16[512,256]{1,0:T(8,128)(2,1)S(1)}) custom-call(bf16[512,1536]{1,0:T(8,128)(2,1)} %bitcast.6, f32[1536]{0:T(1024)} %refs_1_.8, f32[1536]{0:T(1024)} %refs_2_.3, bf16[3,1536,768]{2,1,0:T(8,128)(2,1)} %refs_2_.9), custom_call_target="tpu_custom_call" | custom-call | flops 6291456 | bytes 135168 | tf_op jit(solution)/shard_map/front/pallas_call | solution.py:138
  3.7 1.6 %collective-permute-start = (bf16[512,256]{1,0:T(8,128)(2,1)S(1)}, bf16[512,256]{1,0:T(8,128)(2,1)S(1)}, u32[]{:S(2)}, u32[]{:S(2)}) collective-permute-start(bf16[512,256]{1,0:T(8,128)(2,1)S(1)} %get-tuple-element.28), channel_id=1, source_target_pairs={{0,2},{1,3},{2,0},{3,1},{4,6},{5,7},{6,4},{7,5},{8,10},{9,11},{10,... | collective-permute-start | bytes 786440 | tf_op jit(solution)/shard_map/ppermute | solution.py:484
  5.8 2.9 %collective-permute-start.1 = (bf16[512,256]{1,0:T(8,128)(2,1)S(1)}, bf16[512,256]{1,0:T(8,128)(2,1)S(1)}, u32[]{:S(2)}, u32[]{:S(2)}) collective-permute-start(bf16[512,256]{1,0:T(8,128)(2,1)S(1)} %side.3.refs_2_), channel_id=1, source_target_pairs={{2,4},{3,5},{4,2},{5,3},{6,8},{7,9},{8,6},{9,7},{10,12},{11,13},{1... | collective-permute-start | bytes 786440 | tf_op jit(solution)/shard_map/ppermute | solution.py:484
  9.4 2.2 %collective-permute-start.2 = (bf16[512,256]{1,0:T(8,128)(2,1)S(1)}, bf16[512,256]{1,0:T(8,128)(2,1)S(1)}, u32[]{:S(2)}, u32[]{:S(2)}) collective-permute-start(bf16[512,256]{1,0:T(8,128)(2,1)S(1)} %side.4.refs_2_.refs_1_), channel_id=1, source_target_pairs={{2,6},{3,7},{4,0},{5,1},{6,10},{7,11},{8,4},{9,5},{10,14},{11,15},... | collective-permute-start | bytes 786440 | tf_op jit(solution)/shard_map/ppermute | solution.py:484
  11.6 1.4 %centre.1 = (f32[512,256]{1,0:T(8,128)S(1)}, f32[512,256]{1,0:T(8,128)S(1)}, f32[512,256]{1,0:T(8,128)S(1)}) custom-call(bf16[512,1536]{1,0:T(8,128)(2,1)S(1)} %get-tuple-element.29.a_ref.refs_0_, bf16[3,1536,768]{2,1,0:T(8,128)(2,1)S(1)} %copy-done, bf16[512,256]{1,0:T(8,128)(2,1)S(1)} %side.4.refs_2_.refs_1_), custom_call_target="tpu_custom_call" | custom-call | flops 18874368 | bytes 24576 | tf_op jit(solution)/shard_map/centre/pallas_call | solution.py:84
  13.0 0.9 %hidden_grad.1 = (f32[128,256]{1,0:T(8,128)S(1)}, f32[128,256]{1,0:T(8,128)S(1)}, f32[128,256]{1,0:T(8,128)S(1)}) custom-call(bf16[128,1536]{1,0:T(8,128)(2,1)S(1)} %bitcast.3, bf16[768,1536]{1,0:T(8,128)(2,1)S(1)} %copy-done.1, f32[512,256]{1,0:T(8,128)S(1)} %get-tuple-element.31.refs_2_), custom_call_target="tpu_custom_call" | custom-call | flops 4718592 | bytes 6144 | tf_op jit(solution)/shard_map/hidden_grad/pallas_call | solution.py:84
  13.9 1.0 %keep.1 = (f32[512,256]{1,0:T(8,128)S(1)}, f32[512,256]{1,0:T(8,128)S(1)}) custom-call(bf16[512,1536]{1,0:T(8,128)(2,1)S(1)} %get-tuple-element.29.a_ref.refs_0_, bf16[3,1536,768]{2,1,0:T(8,128)(2,1)S(1)} %copy-done, f32[128,256]{1,0:T(8,128)S(1)} %get-tuple-element.32.refs_2_.refs_5_), custom_call_target="tpu_custom_call" | custom-call | flops 12582912 | bytes 24576 | tf_op jit(solution)/shard_map/keep/pallas_call | solution.py:84
  14.9 2.1 %collective-permute-done.refs_0_ = bf16[512,256]{1,0:T(8,128)(2,1)S(1)} collective-permute-done((bf16[512,256]{1,0:T(8,128)(2,1)S(1)}, bf16[512,256]{1,0:T(8,128)(2,1)S(1)}, u32[]{:S(2)}, u32[]{:S(2)}) %collective-permute-start) | collective-permute-done | bytes 262176 | tf_op jit(solution)/shard_map/ppermute | solution.py:484
  16.9 0.9 %collective-permute-done.1.refs_1_ = bf16[512,256]{1,0:T(8,128)(2,1)S(1)} collective-permute-done((bf16[512,256]{1,0:T(8,128)(2,1)S(1)}, bf16[512,256]{1,0:T(8,128)(2,1)S(1)}, u32[]{:S(2)}, u32[]{:S(2)}) %collective-permute-start.1) | collective-permute-done | bytes 262176 | tf_op jit(solution)/shard_map/ppermute | solution.py:484
  17.9 0.8 %middle.3 = (bf16[512,256]{1,0:T(8,128)(2,1)S(1)}, bf16[512,256]{1,0:T(8,128)(2,1)S(1)}) custom-call(bf16[512,256]{1,0:T(8,128)(2,1)S(1)} %collective-permute-done.refs_0_, bf16[512,256]{1,0:T(8,128)(2,1)S(1)} %collective-permute-done.1.refs_1_, f32[512,256]{1,0:T(8,128)S(1)} %get-tuple-element.31.refs_2_, f32[768]{0:T(1024)S(1)} %copy-done.3, ...), custom_call_target="tpu_custom_call" | custom-call | flops 61440 | bytes 24576 | tf_op jit(solution)/shard_map/middle/pallas_call | solution.py:84
  18.7 1.1 %collective-permute-start.5 = (bf16[512,256]{1,0:T(8,128)(2,1)S(1)}, bf16[512,256]{1,0:T(8,128)(2,1)S(1)}, u32[]{:S(2)}, u32[]{:S(2)}) collective-permute-start(bf16[512,256]{1,0:T(8,128)(2,1)S(1)} %get-tuple-element.37.refs_2_.refs_0_), channel_id=1, source_target_pairs={{0,2},{1,3},{2,0},{3,1},{4,6},{5,7},{6,4},{7,5},{8,10},{9,11},{10,... | collective-permute-start | bytes 786440 | tf_op jit(solution)/shard_map/ppermute | solution.py:484
  20.4 2.4 %collective-permute-start.4 = (bf16[512,256]{1,0:T(8,128)(2,1)S(1)}, bf16[512,256]{1,0:T(8,128)(2,1)S(1)}, u32[]{:S(2)}, u32[]{:S(2)}) collective-permute-start(bf16[512,256]{1,0:T(8,128)(2,1)S(1)} %side.5.refs_2_), channel_id=1, source_target_pairs={{2,6},{3,7},{4,0},{5,1},{6,10},{7,11},{8,4},{9,5},{10,14},{11,15},... | collective-permute-start | bytes 786440 | tf_op jit(solution)/shard_map/ppermute | solution.py:484
  22.8 2.1 %collective-permute-start.3 = (bf16[512,256]{1,0:T(8,128)(2,1)S(1)}, bf16[512,256]{1,0:T(8,128)(2,1)S(1)}, u32[]{:S(2)}, u32[]{:S(2)}) collective-permute-start(bf16[512,256]{1,0:T(8,128)(2,1)S(1)} %join.2.refs_3_), channel_id=1, source_target_pairs={{0,2},{1,3},{2,0},{3,1},{4,6},{5,7},{6,4},{7,5},{8,10},{9,11},{10,... | collective-permute-start | bytes 786440 | tf_op jit(solution)/shard_map/ppermute | solution.py:484
  25.0 1.9 %slope.1.refs_3_ = f32[512,1536]{1,0:T(8,128)S(1)} custom-call(bf16[512,1536]{1,0:T(8,128)(2,1)S(1)} %get-tuple-element.40.refs_0_, f32[1536]{0:T(1024)S(1)} %copy-done.5, f32[1536]{0:T(1024)S(1)} %copy-done.6, bf16[512,256]{1,0:T(8,128)(2,1)S(1)} %join.2.refs_3_), custom_call_target="tpu_custom_call" | custom-call | flops 368640 | bytes 73728 | tf_op jit(solution)/shard_map/slope/pallas_call | solution.py:84
  26.9 1.0 %back.3.refs_2_.refs_4_ = f32[512,1536]{1,0:T(8,128)S(1)} custom-call(bf16[512,256]{1,0:T(8,128)(2,1)S(1)} %get-tuple-element.37.refs_2_.refs_0_, bf16[512,256]{1,0:T(8,128)(2,1)S(1)} %collective-permute-done.5.refs_1_, bf16[3,1536,768]{2,1,0:T(8,128)(2,1)S(1)} %copy-done, f32[512,1536]{1,0:T(8,128)S(1)} %slope.1.refs_3_), custom_call_target="tpu_custom_call" | custom-call | flops 12582912 | bytes 98304 | tf_op jit(solution)/shard_map/back/pallas_call | solution.py:84
  27.9 0.8 %collective-permute-done.4.refs_1_ = bf16[512,256]{1,0:T(8,128)(2,1)S(1)} collective-permute-done((bf16[512,256]{1,0:T(8,128)(2,1)S(1)}, bf16[512,256]{1,0:T(8,128)(2,1)S(1)}, u32[]{:S(2)}, u32[]{:S(2)}) %collective-permute-start.4) | collective-permute-done | bytes 262176 | tf_op jit(solution)/shard_map/ppermute | solution.py:484
  28.8 1.3 %collective-permute-start.6 = (bf16[512,256]{1,0:T(8,128)(2,1)S(1)}, bf16[512,256]{1,0:T(8,128)(2,1)S(1)}, u32[]{:S(2)}, u32[]{:S(2)}) collective-permute-start(bf16[512,256]{1,0:T(8,128)(2,1)S(1)} %join.3.refs_2_), channel_id=1, source_target_pairs={{0,2},{1,3},{2,0},{3,1},{4,6},{5,7},{6,4},{7,5},{8,10},{9,11},{10,... | collective-permute-start | bytes 786440 | tf_op jit(solution)/shard_map/ppermute | solution.py:484
  30.1 3.3 %collective-permute-start.9 = (bf16[512,256]{1,0:T(8,128)(2,1)S(1)}, bf16[512,256]{1,0:T(8,128)(2,1)S(1)}, u32[]{:S(2)}, u32[]{:S(2)}) collective-permute-start(bf16[512,256]{1,0:T(8,128)(2,1)S(1)} %collective-permute-done.5.refs_1_), channel_id=1, source_target_pairs={{0,4},{1,5},{4,8},{5,9},{6,2},{7,3},{8,12},{9,13},{10,6},{11,7},{1... | collective-permute-start | bytes 786440 | tf_op jit(solution)/shard_map/ppermute | solution.py:484
  33.8 0.7 %middle.4 = (bf16[512,256]{1,0:T(8,128)(2,1)S(1)}, bf16[512,256]{1,0:T(8,128)(2,1)S(1)}) custom-call(bf16[512,256]{1,0:T(8,128)(2,1)S(1)} %collective-permute-done.3.refs_0_, f32[512,256]{1,0:T(8,128)S(1)} %get-tuple-element.38.refs_1_, f32[768]{0:T(1024)S(1)} %copy-done.3, f32[768]{0:T(1024)S(1)} %copy-done.4, f32[128,256]{1,0:T(8,128)S(1)} %get-tuple-element.39.refs_4_, ...), custom_call_target="tpu_custom_call" | custom-call | flops 61440 | bytes 24576 | tf_op jit(solution)/shard_map/middle/pallas_call | solution.py:84
  34.5 0.8 %collective-permute-start.8 = (bf16[512,256]{1,0:T(8,128)(2,1)S(1)}, bf16[512,256]{1,0:T(8,128)(2,1)S(1)}, u32[]{:S(2)}, u32[]{:S(2)}) collective-permute-start(bf16[512,256]{1,0:T(8,128)(2,1)S(1)} %get-tuple-element.45.refs_5_.refs_0_), channel_id=1, source_target_pairs={{0,2},{1,3},{2,0},{3,1},{4,6},{5,7},{6,4},{7,5},{8,10},{9,11},{10,... | collective-permute-start | bytes 786440 | tf_op jit(solution)/shard_map/ppermute | solution.py:484
  35.3 2.8 %collective-permute-done.6.refs_0_ = bf16[512,256]{1,0:T(8,128)(2,1)S(1)} collective-permute-done((bf16[512,256]{1,0:T(8,128)(2,1)S(1)}, bf16[512,256]{1,0:T(8,128)(2,1)S(1)}, u32[]{:S(2)}, u32[]{:S(2)}) %collective-permute-start.6) | collective-permute-done | bytes 262176 | tf_op jit(solution)/shard_map/ppermute | solution.py:484
  38.1 0.7 %middle.5 = (bf16[512,256]{1,0:T(8,128)(2,1)S(1)}, bf16[512,256]{1,0:T(8,128)(2,1)S(1)}) custom-call(bf16[512,256]{1,0:T(8,128)(2,1)S(1)} %collective-permute-done.6.refs_0_, f32[512,256]{1,0:T(8,128)S(1)} %get-tuple-element.43.refs_1_, f32[768]{0:T(1024)S(1)} %copy-done.3, f32[768]{0:T(1024)S(1)} %copy-done.4, f32[128,256]{1,0:T(8,128)S(1)} %get-tuple-element.44.refs_4_, ...), custom_call_target="tpu_custom_call" | custom-call | flops 61440 | bytes 24576 | tf_op jit(solution)/shard_map/middle/pallas_call | solution.py:84
  38.8 2.1 %collective-permute-start.11 = (bf16[512,256]{1,0:T(8,128)(2,1)S(1)}, bf16[512,256]{1,0:T(8,128)(2,1)S(1)}, u32[]{:S(2)}, u32[]{:S(2)}) collective-permute-start(bf16[512,256]{1,0:T(8,128)(2,1)S(1)} %get-tuple-element.48.refs_1_), channel_id=1, source_target_pairs={{0,2},{1,3},{2,0},{3,1},{4,6},{5,7},{6,4},{7,5},{8,10},{9,11},{10,... | collective-permute-start | bytes 786440 | tf_op jit(solution)/shard_map/ppermute | solution.py:484
  40.9 1.7 %pooled.1 = (bf16[2,64,1536]{2,1,0:T(8,128)(2,1)}, bf16[16,128]{1,0:T(8,128)(2,1)S(1)}) custom-call(bf16[512,256]{1,0:T(8,128)(2,1)S(1)} %get-tuple-element.36.refs_0_, bf16[512,256]{1,0:T(8,128)(2,1)S(1)} %get-tuple-element.42.refs_1_, bf16[512,256]{1,0:T(8,128)(2,1)S(1)} %get-tuple-element.46.refs_2_, f32[128,1536]{1,0:T(8,128)S(1)} %pooled_base.1.refs_5_.refs_3_, ...), custom_call_target="tpu_custom_call" | custom-call | flops 4718592 | bytes 18432 | tf_op jit(solution)/shard_map/pooled/pallas_call | solution.py:324
  42.7 1.4 %back.4.refs_3_ = f32[512,1536]{1,0:T(8,128)S(1)} custom-call(bf16[512,256]{1,0:T(8,128)(2,1)S(1)} %get-tuple-element.45.refs_5_.refs_0_, bf16[512,256]{1,0:T(8,128)(2,1)S(1)} %get-tuple-element.48.refs_1_, bf16[512,256]{1,0:T(8,128)(2,1)S(1)} %collective-permute-done.9.refs_2_, bf16[3,1536,768]{2,1,0:T(8,128)(2,1)S(1)} %copy-done, ...), custom_call_target="tpu_custom_call" | custom-call | flops 18874368 | bytes 98304 | tf_op jit(solution)/shard_map/back/pallas_call | solution.py:84
  44.1 3.1 %collective-permute-start.10 = (bf16[512,256]{1,0:T(8,128)(2,1)S(1)}, bf16[512,256]{1,0:T(8,128)(2,1)S(1)}, u32[]{:S(2)}, u32[]{:S(2)}) collective-permute-start(bf16[512,256]{1,0:T(8,128)(2,1)S(1)} %collective-permute-done.8.refs_0_), channel_id=1, source_target_pairs={{0,4},{1,5},{4,8},{5,9},{6,2},{7,3},{8,12},{9,13},{10,6},{11,7},{1... | collective-permute-start | bytes 786440 | tf_op jit(solution)/shard_map/ppermute | solution.py:484
  47.3 1.9 %collective-permute-start.7 = (bf16[512,256]{1,0:T(8,128)(2,1)S(1)}, bf16[512,256]{1,0:T(8,128)(2,1)S(1)}, u32[]{:S(2)}, u32[]{:S(2)}) collective-permute-start(bf16[512,256]{1,0:T(8,128)(2,1)S(1)} %get-tuple-element.48.refs_1_), channel_id=1, source_target_pairs={{2,4},{3,5},{4,2},{5,3},{6,8},{7,9},{8,6},{9,7},{10,12},{11,13},{1... | collective-permute-start | bytes 786440 | tf_op jit(solution)/shard_map/ppermute | solution.py:484
  49.2 1.1 %back.5.refs_1_ = f32[512,1536]{1,0:T(8,128)S(1)} custom-call(bf16[512,256]{1,0:T(8,128)(2,1)S(1)} %collective-permute-done.8.refs_0_, bf16[512,256]{1,0:T(8,128)(2,1)S(1)} %collective-permute-done.11.refs_1_, bf16[3,1536,768]{2,1,0:T(8,128)(2,1)S(1)} %copy-done, f32[512,1536]{1,0:T(8,128)S(1)} %back.4.refs_3_), custom_call_target="tpu_custom_call" | custom-call | flops 12582912 | bytes 98304 | tf_op jit(solution)/shard_map/back/pallas_call | solution.py:84
  50.3 2.1 %collective-permute-done.10.refs_0_ = bf16[512,256]{1,0:T(8,128)(2,1)S(1)} collective-permute-done((bf16[512,256]{1,0:T(8,128)(2,1)S(1)}, bf16[512,256]{1,0:T(8,128)(2,1)S(1)}, u32[]{:S(2)}, u32[]{:S(2)}) %collective-permute-start.10) | collective-permute-done | bytes 262176 | tf_op jit(solution)/shard_map/ppermute | solution.py:484
  52.4 1.0 %settle.1.refs_1_ = f32[512,1536]{1,0:T(8,128)S(1)} custom-call(bf16[512,256]{1,0:T(8,128)(2,1)S(1)} %collective-permute-done.10.refs_0_, f32[512,1536]{1,0:T(8,128)S(1)} %back.5.refs_1_, bf16[3,1536,768]{2,1,0:T(8,128)(2,1)S(1)} %copy-done, f32[512,1536]{1,0:T(8,128)S(1)} %slope.1.refs_3_, bf16[128,1536]{1,0:T(8,128)(2,1)S(1)} %bitcast.4), custom_call_target="tpu_custom_call" | custom-call | flops 6291456 | bytes 98304 | tf_op jit(solution)/shard_map/settle/pallas_call | solution.py:84
  53.5 3.0 %collective-permute-done.7.refs_0_ = bf16[512,256]{1,0:T(8,128)(2,1)S(1)} collective-permute-done((bf16[512,256]{1,0:T(8,128)(2,1)S(1)}, bf16[512,256]{1,0:T(8,128)(2,1)S(1)}, u32[]{:S(2)}, u32[]{:S(2)}) %collective-permute-start.7) | collective-permute-done | bytes 262176 | tf_op jit(solution)/shard_map/ppermute | solution.py:484
  56.4 1.5 %final.1 = bf16[512,1536]{1,0:T(8,128)(2,1)} custom-call(bf16[512,256]{1,0:T(8,128)(2,1)S(1)} %collective-permute-done.7.refs_0_, f32[512,1536]{1,0:T(8,128)S(1)} %settle.1.refs_1_, bf16[3,1536,768]{2,1,0:T(8,128)(2,1)S(1)} %copy-done, f32[512,1536]{1,0:T(8,128)S(1)} %slope.1.refs_3_), custom_call_target="tpu_custom_call" | custom-call | flops 6291456 | bytes 98304 | tf_op jit(solution)/shard_map/final/pallas_call | solution.py:443
  (29 shorter events, 2.3 us)
Async XLA Ops:
  0.6 4.6 %copy-start = (bf16[3,1536,768]{2,1,0:T(8,128)(2,1)S(1)}, bf16[3,1536,768]{2,1,0:T(8,128)(2,1)}, u32[]{:S(2)}) copy-start(bf16[3,1536,768]{2,1,0:T(8,128)(2,1)} %refs_2_.9) | copy-start | bytes 21233668
  3.7 13.3 %collective-permute-start = (bf16[512,256]{1,0:T(8,128)(2,1)S(1)}, bf16[512,256]{1,0:T(8,128)(2,1)S(1)}, u32[]{:S(2)}, u32[]{:S(2)}) collective-permute-start(bf16[512,256]{1,0:T(8,128)(2,1)S(1)} %get-tuple-element.28), channel_id=1, source_target_pairs={{0,2},{1,3},{2,0},{3,1},{4,6},{5,7},{6,4},{7,5},{8,10},{9,11},{10,... | collective-permute-start | bytes 786440 | tf_op jit(solution)/shard_map/ppermute | solution.py:484
  5.8 12.0 %collective-permute-start.1 = (bf16[512,256]{1,0:T(8,128)(2,1)S(1)}, bf16[512,256]{1,0:T(8,128)(2,1)S(1)}, u32[]{:S(2)}, u32[]{:S(2)}) collective-permute-start(bf16[512,256]{1,0:T(8,128)(2,1)S(1)} %side.3.refs_2_), channel_id=1, source_target_pairs={{2,4},{3,5},{4,2},{5,3},{6,8},{7,9},{8,6},{9,7},{10,12},{11,13},{1... | collective-permute-start | bytes 786440 | tf_op jit(solution)/shard_map/ppermute | solution.py:484
  9.3 3.6 %copy-start.1 = (bf16[768,1536]{1,0:T(8,128)(2,1)S(1)}, bf16[768,1536]{1,0:T(8,128)(2,1)}, u32[]{:S(2)}) copy-start(bf16[768,1536]{1,0:T(8,128)(2,1)} %refs_4_.3) | copy-start | bytes 7077892
  9.4 3.6 %copy-start.2 = (bf16[2,64,1536]{2,1,0:T(8,128)(2,1)S(1)}, bf16[2,64,1536]{2,1,0:T(8,128)(2,1)}, u32[]{:S(2)}) copy-start(bf16[2,64,1536]{2,1,0:T(8,128)(2,1)} %param.10) | copy-start | bytes 1179652
  9.4 13.4 %collective-permute-start.2 = (bf16[512,256]{1,0:T(8,128)(2,1)S(1)}, bf16[512,256]{1,0:T(8,128)(2,1)S(1)}, u32[]{:S(2)}, u32[]{:S(2)}) collective-permute-start(bf16[512,256]{1,0:T(8,128)(2,1)S(1)} %side.4.refs_2_.refs_1_), channel_id=1, source_target_pairs={{2,6},{3,7},{4,0},{5,1},{6,10},{7,11},{8,4},{9,5},{10,14},{11,15},... | collective-permute-start | bytes 786440 | tf_op jit(solution)/shard_map/ppermute | solution.py:484
  13.8 4.0 %copy-start.3 = (f32[768]{0:T(1024)S(1)}, f32[768]{0:T(1024)}, u32[]{:S(2)}) copy-start(f32[768]{0:T(1024)} %refs_2_.6) | copy-start | bytes 9220
  13.9 4.0 %copy-start.4 = (f32[768]{0:T(1024)S(1)}, f32[768]{0:T(1024)}, u32[]{:S(2)}) copy-start(f32[768]{0:T(1024)} %refs_3_.5) | copy-start | bytes 9220
  18.6 6.3 %copy-start.5 = (f32[1536]{0:T(1024)S(1)}, f32[1536]{0:T(1024)}, u32[]{:S(2)}) copy-start(f32[1536]{0:T(1024)} %refs_1_.8) | copy-start | bytes 18436
  18.6 6.3 %copy-start.6 = (f32[1536]{0:T(1024)S(1)}, f32[1536]{0:T(1024)}, u32[]{:S(2)}) copy-start(f32[1536]{0:T(1024)} %refs_2_.3) | copy-start | bytes 18436
  18.7 8.2 %collective-permute-start.5 = (bf16[512,256]{1,0:T(8,128)(2,1)S(1)}, bf16[512,256]{1,0:T(8,128)(2,1)S(1)}, u32[]{:S(2)}, u32[]{:S(2)}) collective-permute-start(bf16[512,256]{1,0:T(8,128)(2,1)S(1)} %get-tuple-element.37.refs_2_.refs_0_), channel_id=1, source_target_pairs={{0,2},{1,3},{2,0},{3,1},{4,6},{5,7},{6,4},{7,5},{8,10},{9,11},{10,... | collective-permute-start | bytes 786440 | tf_op jit(solution)/shard_map/ppermute | solution.py:484
  20.4 8.4 %collective-permute-start.4 = (bf16[512,256]{1,0:T(8,128)(2,1)S(1)}, bf16[512,256]{1,0:T(8,128)(2,1)S(1)}, u32[]{:S(2)}, u32[]{:S(2)}) collective-permute-start(bf16[512,256]{1,0:T(8,128)(2,1)S(1)} %side.5.refs_2_), channel_id=1, source_target_pairs={{2,6},{3,7},{4,0},{5,1},{6,10},{7,11},{8,4},{9,5},{10,14},{11,15},... | collective-permute-start | bytes 786440 | tf_op jit(solution)/shard_map/ppermute | solution.py:484
  22.8 11.0 %collective-permute-start.3 = (bf16[512,256]{1,0:T(8,128)(2,1)S(1)}, bf16[512,256]{1,0:T(8,128)(2,1)S(1)}, u32[]{:S(2)}, u32[]{:S(2)}) collective-permute-start(bf16[512,256]{1,0:T(8,128)(2,1)S(1)} %join.2.refs_3_), channel_id=1, source_target_pairs={{0,2},{1,3},{2,0},{3,1},{4,6},{5,7},{6,4},{7,5},{8,10},{9,11},{10,... | collective-permute-start | bytes 786440 | tf_op jit(solution)/shard_map/ppermute | solution.py:484
  27.9 5.4 %copy-start.7 = (f32[1536]{0:T(1024)S(1)}, f32[1536]{0:T(1024)}, u32[]{:S(2)}) copy-start(f32[1536]{0:T(1024)} %refs_1_.9) | copy-start | bytes 18436
  28.8 9.3 %collective-permute-start.6 = (bf16[512,256]{1,0:T(8,128)(2,1)S(1)}, bf16[512,256]{1,0:T(8,128)(2,1)S(1)}, u32[]{:S(2)}, u32[]{:S(2)}) collective-permute-start(bf16[512,256]{1,0:T(8,128)(2,1)S(1)} %join.3.refs_2_), channel_id=1, source_target_pairs={{0,2},{1,3},{2,0},{3,1},{4,6},{5,7},{6,4},{7,5},{8,10},{9,11},{10,... | collective-permute-start | bytes 786440 | tf_op jit(solution)/shard_map/ppermute | solution.py:484
  30.1 12.6 %collective-permute-start.9 = (bf16[512,256]{1,0:T(8,128)(2,1)S(1)}, bf16[512,256]{1,0:T(8,128)(2,1)S(1)}, u32[]{:S(2)}, u32[]{:S(2)}) collective-permute-start(bf16[512,256]{1,0:T(8,128)(2,1)S(1)} %collective-permute-done.5.refs_1_), channel_id=1, source_target_pairs={{0,4},{1,5},{4,8},{5,9},{6,2},{7,3},{8,12},{9,13},{10,6},{11,7},{1... | collective-permute-start | bytes 786440 | tf_op jit(solution)/shard_map/ppermute | solution.py:484
  34.5 9.6 %collective-permute-start.8 = (bf16[512,256]{1,0:T(8,128)(2,1)S(1)}, bf16[512,256]{1,0:T(8,128)(2,1)S(1)}, u32[]{:S(2)}, u32[]{:S(2)}) collective-permute-start(bf16[512,256]{1,0:T(8,128)(2,1)S(1)} %get-tuple-element.45.refs_5_.refs_0_), channel_id=1, source_target_pairs={{0,2},{1,3},{2,0},{3,1},{4,6},{5,7},{6,4},{7,5},{8,10},{9,11},{10,... | collective-permute-start | bytes 786440 | tf_op jit(solution)/shard_map/ppermute | solution.py:484
  38.8 10.4 %collective-permute-start.11 = (bf16[512,256]{1,0:T(8,128)(2,1)S(1)}, bf16[512,256]{1,0:T(8,128)(2,1)S(1)}, u32[]{:S(2)}, u32[]{:S(2)}) collective-permute-start(bf16[512,256]{1,0:T(8,128)(2,1)S(1)} %get-tuple-element.48.refs_1_), channel_id=1, source_target_pairs={{0,2},{1,3},{2,0},{3,1},{4,6},{5,7},{6,4},{7,5},{8,10},{9,11},{10,... | collective-permute-start | bytes 786440 | tf_op jit(solution)/shard_map/ppermute | solution.py:484
  44.1 8.3 %collective-permute-start.10 = (bf16[512,256]{1,0:T(8,128)(2,1)S(1)}, bf16[512,256]{1,0:T(8,128)(2,1)S(1)}, u32[]{:S(2)}, u32[]{:S(2)}) collective-permute-start(bf16[512,256]{1,0:T(8,128)(2,1)S(1)} %collective-permute-done.8.refs_0_), channel_id=1, source_target_pairs={{0,4},{1,5},{4,8},{5,9},{6,2},{7,3},{8,12},{9,13},{10,6},{11,7},{1... | collective-permute-start | bytes 786440 | tf_op jit(solution)/shard_map/ppermute | solution.py:484
  47.3 9.2 %collective-permute-start.7 = (bf16[512,256]{1,0:T(8,128)(2,1)S(1)}, bf16[512,256]{1,0:T(8,128)(2,1)S(1)}, u32[]{:S(2)}, u32[]{:S(2)}) collective-permute-start(bf16[512,256]{1,0:T(8,128)(2,1)S(1)} %get-tuple-element.48.refs_1_), channel_id=1, source_target_pairs={{2,4},{3,5},{4,2},{5,3},{6,8},{7,9},{8,6},{9,7},{10,12},{11,13},{1... | collective-permute-start | bytes 786440 | tf_op jit(solution)/shard_map/ppermute | solution.py:484
